TPU v7x, 768 devices: a whole 4x8x12 slice. The times are simulated.
768 devices in a mesh: comp: 16 (over y_hi, x, core), dom: 48 (over y_lo, z).
Axes of the slice: x: 4, y: 8 (y_hi: 2, y_lo: 4; y = y_hi * 4 + y_lo), z: 12, core: 2. Of those that a mesh axis runs over, the one named last changes fastest.
Arguments:
- action: float32 [1152, 98304], P('comp', 'dom'), may hold values from 0.1 to 1
- coef_one: float32 [1152], P('comp'), may hold values from 0.1 to 0.6
- coef_two: float32 [1152], P('comp'), may hold values from 0.1 to 0.6
- transport_one: bfloat16 [768, 3, 128, 128], P('dom'), may hold values from -0.3125 to 0.3125
- transport_two: bfloat16 [768, 3, 128, 128], P('dom'), may hold values from -0.3125 to 0.3125
- block_cols: int32 [768, 3], P('dom'), may hold values from 0 to 17, as said below
- quad_one: bfloat16 [1152, 1152], replicated, may hold values from -0.1875 to 0.1875
- quad_two: bfloat16 [1152, 1152], replicated, may hold values from -0.1875 to 0.1875
Outputs:
- updated: float32 [48, 2048, 1152], P('dom', 'comp')
Inputs may be any that keep to these rules, and one draw needn't show every extreme that they name: `block_cols`: entry 1 of every block row is the block just before it and entry 2 the block just after it, in the extended counting; entry 0 is any block of the extended range.
All inputs are finite; a program needn't handle non-finite values.
Results may differ from a plain program's by a relative error of at most 0.0067.
Values may be sent and summed in bfloat16 or wider, within the bound.
No kernel may reach another device: no remote copies, remote signals or barrier semaphores. Data moves between devices by JAX's collectives and lax.ppermute only.
A program may use at most 32 MiB of HBM per device.

v0:
```python
import jax
import jax.numpy as jnp
from jax import lax
from jax.sharding import PartitionSpec as P

SUBSTEPS = 4


keep_share = 0.25


def extended_2(value, sides, width):
    for axis, dim in sides:
        size, length = (lax.axis_size(axis), value.shape[dim])
        up = [(i, (i + 1) % size) for i in range(size - 1)]
        down = [(j, i) for i, j in up]
        last = lax.slice_in_dim(value, length - width, length, axis=dim)
        initial = lax.slice_in_dim(value, 0, width, axis=dim)
        before = lax.ppermute(last, axis, up)
        after = lax.ppermute(initial, axis, down)
        value = jnp.concatenate([before, value, after], axis=dim)
    return value


def source_terms(cells, quad_one, quad_two):
    cell_wide = cells.astype(jnp.float32)
    first = jnp.dot(cells, quad_one, preferred_element_type=jnp.float32)
    second = jnp.dot(cells, quad_two, preferred_element_type=jnp.float32)
    return cell_wide + 0.5 * (first * cell_wide - second * cell_wide * cell_wide)


def per_device(
    action, coef_one, coef_two, transport_one, transport_two, block_cols, quad_one, quad_two
):
    comp_rows, cells_dev = action.shape
    width = transport_one.shape[2]
    nblocks = block_cols.shape[0]
    field = action
    for substep in range(SUBSTEPS):
        rounded = field.astype(jnp.bfloat16)
        padded = extended_2(rounded, (("dom", 1),), width)
        extended = padded.reshape(comp_rows, nblocks + 2, width)
        gathered = jnp.take(extended, block_cols, axis=1)
        flow_one = jnp.einsum(
            "kbjc,bjcd->kbd", gathered, transport_one, preferred_element_type=jnp.float32
        ).reshape(comp_rows, cells_dev)
        flow_two = jnp.einsum(
            "kbjc,bjcd->kbd", gathered, transport_two, preferred_element_type=jnp.float32
        ).reshape(comp_rows, cells_dev)
        moved = field + coef_one[:, None] * flow_one + coef_two[:, None] * flow_two
        field = jnp.maximum(moved, keep_share * field)
    final = field.astype(jnp.bfloat16)
    exchanged = lax.all_to_all(final, "comp", split_axis=1, concat_axis=0, tiled=True)
    result = source_terms(exchanged.T, quad_one, quad_two)
    return result[None]


def solution(mesh):
    in_specs = (
        P("comp", "dom"),
        P("comp"),
        P("comp"),
        P("dom", None, None, None),
        P("dom", None, None, None),
        P("dom", None),
        P(),
        P(),
    )
    out_specs = P("dom", "comp", None)
    return jax.shard_map(
        per_device, mesh=mesh, in_specs=in_specs, out_specs=out_specs, check_vma=False
    )
```

profile of v0, /device:TPU:8, one launch (start us, length us, event | category | flops | bytes accessed | tf_op | source)
XLA Modules:
  0.0 102.4 jit_solution(7178560074427246665)
XLA Ops:
  0.0 1.2 %convert_element_type.21 = bf16[72,2048]{1,0:T(8,128)(2,1)S(1)} convert(f32[72,2048]{1,0:T(8,128)} %param.10) | non-fusion elementwise | flops 147456 | bytes 884736 | tf_op jit(solution)/shard_map/convert_element_type | solution.py:40
  1.3 4.3 %collective-permute-start = (bf16[72,128]{1,0:T(8,128)(2,1)S(1)}, bf16[72,128]{1,0:T(8,128)(2,1)S(1)}, u32[]{:S(2)}, u32[]{:S(2)}) collective-permute-start(bf16[72,128]{1,0:T(8,128)(2,1)S(1)} %get-tuple-element.18), channel_id=1, source_target_pairs={{0,1},{1,2},{2,3},{3,4},{4,5},{5,6},{6,7},{7,8},{8,9},{9,10},{10,1... | collective-permute-start | bytes 55304 | tf_op jit(solution)/shard_map/ppermute | solution.py:19
  5.6 12.1 %collective-permute-start.1 = (bf16[72,128]{1,0:T(8,128)(2,1)S(1)}, bf16[72,128]{1,0:T(8,128)(2,1)S(1)}, u32[]{:S(2)}, u32[]{:S(2)}) collective-permute-start(bf16[72,128]{1,0:T(8,128)(2,1)S(1)} %get-tuple-element.19), channel_id=1, source_target_pairs={{1,0},{2,1},{3,2},{4,3},{5,4},{6,5},{7,6},{8,7},{9,8},{10,9},{11,1... | collective-permute-start | bytes 55304 | tf_op jit(solution)/shard_map/ppermute | solution.py:20
  20.1 1.7 %gather_fusion = bf16[48,72,128]{2,1,0:T(8,128)(2,1)S(1)} fusion(bf16[72,18,128]{2,0,1:T(8,128)(2,1)} %copy_bitcast_fusion.3, s32[1024]{0:T(1024)S(1)} %pad_clamp_fusion), kind=kCustom, calls=%fused_computation.clone | custom fusion | bytes 1769664 | tf_op jit(solution)/shard_map/jit(_take)/gather | solution.py:43
  21.9 2.0 %convolution_bitcast_fusion.6 = f32[16,9,8,128]{3,2,1,0:T(8,128)S(1)} fusion(bf16[16,3,128,128]{3,2,1,0:T(8,128)(2,1)} %param.14, bf16[16,3,72,128]{3,2,1,0:T(8,128)(2,1)S(1)} %bitcast.181, pred[16,3]{1,0:T(8,128)(4,1)S(1)} %copy.22), kind=kOutput, calls=%fused_computation.17 | convolution fusion | flops 113688576 | bytes 3047472 | tf_op jit(solution)/shard_map/kbjc,bjcd->kbd/dot_general | solution.py:47
  25.0 1.0 fusion.47
  26.0 1.9 %collective-permute-start.2 = (bf16[72,128]{1,0:T(8,128)(2,1)S(1)}, bf16[72,128]{1,0:T(8,128)(2,1)S(1)}, u32[]{:S(2)}, u32[]{:S(2)}) collective-permute-start(bf16[72,128]{1,0:T(8,128)(2,1)S(1)} %get-tuple-element.16), channel_id=1, source_target_pairs={{0,1},{1,2},{2,3},{3,4},{4,5},{5,6},{6,7},{7,8},{8,9},{9,10},{10,1... | collective-permute-start | bytes 55304 | tf_op jit(solution)/shard_map/ppermute | solution.py:19
  27.9 6.1 %collective-permute-start.3 = (bf16[72,128]{1,0:T(8,128)(2,1)S(1)}, bf16[72,128]{1,0:T(8,128)(2,1)S(1)}, u32[]{:S(2)}, u32[]{:S(2)}) collective-permute-start(bf16[72,128]{1,0:T(8,128)(2,1)S(1)} %get-tuple-element.17), channel_id=1, source_target_pairs={{1,0},{2,1},{3,2},{4,3},{5,4},{6,5},{7,6},{8,7},{9,8},{10,9},{11,1... | collective-permute-start | bytes 55304 | tf_op jit(solution)/shard_map/ppermute | solution.py:20
  34.0 1.4 %collective-permute-done.3 = bf16[72,128]{1,0:T(8,128)(2,1)S(1)} collective-permute-done((bf16[72,128]{1,0:T(8,128)(2,1)S(1)}, bf16[72,128]{1,0:T(8,128)(2,1)S(1)}, u32[]{:S(2)}, u32[]{:S(2)}) %collective-permute-start.3) | collective-permute-done | bytes 18464 | tf_op jit(solution)/shard_map/ppermute | solution.py:20
  36.3 1.7 %gather_fusion.1 = bf16[48,72,128]{2,1,0:T(8,128)(2,1)S(1)} fusion(bf16[72,18,128]{2,0,1:T(8,128)(2,1)} %copy_bitcast_fusion.2, s32[1024]{0:T(1024)S(1)} %pad_clamp_fusion), kind=kCustom, calls=%fused_computation.1.clone | custom fusion | bytes 1769664 | tf_op jit(solution)/shard_map/jit(_take)/gather | solution.py:43
  38.0 2.1 %convolution_bitcast_fusion.4 = f32[16,9,8,128]{3,2,1,0:T(8,128)S(1)} fusion(bf16[16,3,128,128]{3,2,1,0:T(8,128)(2,1)} %param.14, bf16[16,3,72,128]{3,2,1,0:T(8,128)(2,1)S(1)} %bitcast.183, pred[16,3]{1,0:T(8,128)(4,1)S(1)} %copy.22), kind=kOutput, calls=%fused_computation.15 | convolution fusion | flops 113688576 | bytes 3047472 | tf_op jit(solution)/shard_map/kbjc,bjcd->kbd/dot_general | solution.py:47
  42.2 1.9 %collective-permute-start.4 = (bf16[72,128]{1,0:T(8,128)(2,1)S(1)}, bf16[72,128]{1,0:T(8,128)(2,1)S(1)}, u32[]{:S(2)}, u32[]{:S(2)}) collective-permute-start(bf16[72,128]{1,0:T(8,128)(2,1)S(1)} %get-tuple-element.14), channel_id=1, source_target_pairs={{0,1},{1,2},{2,3},{3,4},{4,5},{5,6},{6,7},{7,8},{8,9},{9,10},{10,1... | collective-permute-start | bytes 55304 | tf_op jit(solution)/shard_map/ppermute | solution.py:19
  44.1 6.3 %collective-permute-start.5 = (bf16[72,128]{1,0:T(8,128)(2,1)S(1)}, bf16[72,128]{1,0:T(8,128)(2,1)S(1)}, u32[]{:S(2)}, u32[]{:S(2)}) collective-permute-start(bf16[72,128]{1,0:T(8,128)(2,1)S(1)} %get-tuple-element.15), channel_id=1, source_target_pairs={{1,0},{2,1},{3,2},{4,3},{5,4},{6,5},{7,6},{8,7},{9,8},{10,9},{11,1... | collective-permute-start | bytes 55304 | tf_op jit(solution)/shard_map/ppermute | solution.py:20
  50.4 1.4 %collective-permute-done.5 = bf16[72,128]{1,0:T(8,128)(2,1)S(1)} collective-permute-done((bf16[72,128]{1,0:T(8,128)(2,1)S(1)}, bf16[72,128]{1,0:T(8,128)(2,1)S(1)}, u32[]{:S(2)}, u32[]{:S(2)}) %collective-permute-start.5) | collective-permute-done | bytes 18464 | tf_op jit(solution)/shard_map/ppermute | solution.py:20
  52.6 1.7 %gather_fusion.2 = bf16[48,72,128]{2,1,0:T(8,128)(2,1)S(1)} fusion(bf16[72,18,128]{2,0,1:T(8,128)(2,1)} %copy_bitcast_fusion.1, s32[1024]{0:T(1024)S(1)} %pad_clamp_fusion), kind=kCustom, calls=%fused_computation.2.clone | custom fusion | bytes 1769664 | tf_op jit(solution)/shard_map/jit(_take)/gather | solution.py:43
  54.4 2.1 %convolution_bitcast_fusion.2 = f32[16,9,8,128]{3,2,1,0:T(8,128)S(1)} fusion(bf16[16,3,128,128]{3,2,1,0:T(8,128)(2,1)} %param.14, bf16[16,3,72,128]{3,2,1,0:T(8,128)(2,1)S(1)} %bitcast.185, pred[16,3]{1,0:T(8,128)(4,1)S(1)} %copy.22), kind=kOutput, calls=%fused_computation.13 | convolution fusion | flops 113688576 | bytes 3047472 | tf_op jit(solution)/shard_map/kbjc,bjcd->kbd/dot_general | solution.py:47
  58.5 1.9 %collective-permute-start.6 = (bf16[72,128]{1,0:T(8,128)(2,1)S(1)}, bf16[72,128]{1,0:T(8,128)(2,1)S(1)}, u32[]{:S(2)}, u32[]{:S(2)}) collective-permute-start(bf16[72,128]{1,0:T(8,128)(2,1)S(1)} %get-tuple-element.12), channel_id=1, source_target_pairs={{0,1},{1,2},{2,3},{3,4},{4,5},{5,6},{6,7},{7,8},{8,9},{9,10},{10,1... | collective-permute-start | bytes 55304 | tf_op jit(solution)/shard_map/ppermute | solution.py:19
  60.4 6.3 %collective-permute-start.7 = (bf16[72,128]{1,0:T(8,128)(2,1)S(1)}, bf16[72,128]{1,0:T(8,128)(2,1)S(1)}, u32[]{:S(2)}, u32[]{:S(2)}) collective-permute-start(bf16[72,128]{1,0:T(8,128)(2,1)S(1)} %get-tuple-element.13), channel_id=1, source_target_pairs={{1,0},{2,1},{3,2},{4,3},{5,4},{6,5},{7,6},{8,7},{9,8},{10,9},{11,1... | collective-permute-start | bytes 55304 | tf_op jit(solution)/shard_map/ppermute | solution.py:20
  66.8 1.4 %collective-permute-done.7 = bf16[72,128]{1,0:T(8,128)(2,1)S(1)} collective-permute-done((bf16[72,128]{1,0:T(8,128)(2,1)S(1)}, bf16[72,128]{1,0:T(8,128)(2,1)S(1)}, u32[]{:S(2)}, u32[]{:S(2)}) %collective-permute-start.7) | collective-permute-done | bytes 18464 | tf_op jit(solution)/shard_map/ppermute | solution.py:20
  69.0 1.7 %gather_fusion.3 = bf16[48,72,128]{2,1,0:T(8,128)(2,1)S(1)} fusion(bf16[72,18,128]{2,0,1:T(8,128)(2,1)} %copy_bitcast_fusion, s32[1024]{0:T(1024)S(1)} %pad_clamp_fusion), kind=kCustom, calls=%fused_computation.3.clone | custom fusion | bytes 1769664 | tf_op jit(solution)/shard_map/jit(_take)/gather | solution.py:43
  70.7 2.0 %convolution_bitcast_fusion = f32[16,9,8,128]{3,2,1,0:T(8,128)S(1)} fusion(bf16[16,3,128,128]{3,2,1,0:T(8,128)(2,1)} %param.14, bf16[16,3,72,128]{3,2,1,0:T(8,128)(2,1)S(1)} %bitcast.179, pred[16,3]{1,0:T(8,128)(4,1)S(1)} %copy.22), kind=kOutput, calls=%fused_computation.11 | convolution fusion | flops 113688576 | bytes 3047472 | tf_op jit(solution)/shard_map/kbjc,bjcd->kbd/dot_general | solution.py:47
  74.1 24.9 %all_to_all.19 = bf16[72,16,128]{2,0,1:T(8,128)(2,1)S(1)} all-to-all(bf16[72,16,128]{2,0,1:T(8,128)(2,1)S(1)} %copy_bitcast_fusion.4), channel_id=1, replica_groups=mesh['comp'=16,'dom'=48] {'comp'}, dimensions={1} | all-to-all | bytes 589824 | tf_op jit(solution)/shard_map/all_to_all | solution.py:53
  99.8 1.1 %copy-done.5 = bf16[1152,1152]{1,0:T(8,128)(2,1)S(1)} copy-done((bf16[1152,1152]{1,0:T(8,128)(2,1)S(1)}, bf16[1152,1152]{1,0:T(8,128)(2,1)}, u32[]{:S(2)}) %copy-start.5) | copy-done | bytes 2654232
  100.9 1.5 %fusion.4 = f32[1,128,1152]{2,1,0:T(8,128)} fusion(f32[128,1152]{1,0:T(8,128)S(1)} %convolution_multiply_fusion.1, bf16[1152,128]{1,0:T(8,128)(2,1)S(1)} %bitcast.189, bf16[1152,1152]{1,0:T(8,128)(2,1)S(1)} %copy-done.5, bf16[1152,128]{0,1:T(8,128)(2,1)S(1)} %copy.43), kind=kOutput, calls=%fused_computation.10 | convolution fusion | flops 340623360 | bytes 4423680 | tf_op jit(solution)/shard_map/dot_general | solution.py:28
  (51 shorter events, 12.2 us)
Async XLA Ops:
  0.0 99.2 %copy-start = (bf16[1152,1152]{1,0:T(8,128)(2,1)S(1)}, bf16[1152,1152]{1,0:T(8,128)(2,1)}, u32[]{:S(2)}) copy-start(bf16[1152,1152]{1,0:T(8,128)(2,1)} %param.16) | copy-start | bytes 7962628
  1.3 18.1 %collective-permute-start = (bf16[72,128]{1,0:T(8,128)(2,1)S(1)}, bf16[72,128]{1,0:T(8,128)(2,1)S(1)}, u32[]{:S(2)}, u32[]{:S(2)}) collective-permute-start(bf16[72,128]{1,0:T(8,128)(2,1)S(1)} %get-tuple-element.18), channel_id=1, source_target_pairs={{0,1},{1,2},{2,3},{3,4},{4,5},{5,6},{6,7},{7,8},{8,9},{9,10},{10,1... | collective-permute-start | bytes 55304 | tf_op jit(solution)/shard_map/ppermute | solution.py:19
  5.6 13.8 %collective-permute-start.1 = (bf16[72,128]{1,0:T(8,128)(2,1)S(1)}, bf16[72,128]{1,0:T(8,128)(2,1)S(1)}, u32[]{:S(2)}, u32[]{:S(2)}) collective-permute-start(bf16[72,128]{1,0:T(8,128)(2,1)S(1)} %get-tuple-element.19), channel_id=1, source_target_pairs={{1,0},{2,1},{3,2},{4,3},{5,4},{6,5},{7,6},{8,7},{9,8},{10,9},{11,1... | collective-permute-start | bytes 55304 | tf_op jit(solution)/shard_map/ppermute | solution.py:20
  21.8 2.1 %copy-start.1 = (bf16[16,3,128,128]{3,2,1,0:T(8,128)(2,1)S(1)}, bf16[16,3,128,128]{3,2,1,0:T(8,128)(2,1)}, u32[]{:S(2)}) copy-start(bf16[16,3,128,128]{3,2,1,0:T(8,128)(2,1)} %param.13) | copy-start | bytes 4718596
  23.9 1.1 %copy-start.7 = (f32[72,2048]{1,0:T(8,128)S(1)}, f32[72,2048]{1,0:T(8,128)}, u32[]{:S(2)}) copy-start(f32[72,2048]{1,0:T(8,128)} %param.10) | copy-start | bytes 1769476
  23.9 1.1 %copy-start.10 = (f32[72]{0:T(128)S(1)}, f32[72]{0:T(128)}, u32[]{:S(2)}) copy-start(f32[72]{0:T(128)} %param.12) | copy-start | bytes 868
  23.9 1.0 %copy-start.11 = (f32[72]{0:T(128)S(1)}, f32[72]{0:T(128)}, u32[]{:S(2)}) copy-start(f32[72]{0:T(128)} %param.11) | copy-start | bytes 868
  26.0 8.0 %collective-permute-start.2 = (bf16[72,128]{1,0:T(8,128)(2,1)S(1)}, bf16[72,128]{1,0:T(8,128)(2,1)S(1)}, u32[]{:S(2)}, u32[]{:S(2)}) collective-permute-start(bf16[72,128]{1,0:T(8,128)(2,1)S(1)} %get-tuple-element.16), channel_id=1, source_target_pairs={{0,1},{1,2},{2,3},{3,4},{4,5},{5,6},{6,7},{7,8},{8,9},{9,10},{10,1... | collective-permute-start | bytes 55304 | tf_op jit(solution)/shard_map/ppermute | solution.py:19
  27.9 7.5 %collective-permute-start.3 = (bf16[72,128]{1,0:T(8,128)(2,1)S(1)}, bf16[72,128]{1,0:T(8,128)(2,1)S(1)}, u32[]{:S(2)}, u32[]{:S(2)}) collective-permute-start(bf16[72,128]{1,0:T(8,128)(2,1)S(1)} %get-tuple-element.17), channel_id=1, source_target_pairs={{1,0},{2,1},{3,2},{4,3},{5,4},{6,5},{7,6},{8,7},{9,8},{10,9},{11,1... | collective-permute-start | bytes 55304 | tf_op jit(solution)/shard_map/ppermute | solution.py:20
  38.0 2.1 %copy-start.2 = (bf16[16,3,128,128]{3,2,1,0:T(8,128)(2,1)S(1)}, bf16[16,3,128,128]{3,2,1,0:T(8,128)(2,1)}, u32[]{:S(2)}) copy-start(bf16[16,3,128,128]{3,2,1,0:T(8,128)(2,1)} %param.13) | copy-start | bytes 4718596
  40.1 1.1 %copy-start.9 = (f32[72,2048]{1,0:T(8,128)S(1)}, f32[72,2048]{1,0:T(8,128)}, u32[]{:S(2)}) copy-start(f32[72,2048]{1,0:T(8,128)} %get-tuple-element.11) | copy-start | bytes 1769476
  42.2 8.2 %collective-permute-start.4 = (bf16[72,128]{1,0:T(8,128)(2,1)S(1)}, bf16[72,128]{1,0:T(8,128)(2,1)S(1)}, u32[]{:S(2)}, u32[]{:S(2)}) collective-permute-start(bf16[72,128]{1,0:T(8,128)(2,1)S(1)} %get-tuple-element.14), channel_id=1, source_target_pairs={{0,1},{1,2},{2,3},{3,4},{4,5},{5,6},{6,7},{7,8},{8,9},{9,10},{10,1... | collective-permute-start | bytes 55304 | tf_op jit(solution)/shard_map/ppermute | solution.py:19
  44.1 7.8 %collective-permute-start.5 = (bf16[72,128]{1,0:T(8,128)(2,1)S(1)}, bf16[72,128]{1,0:T(8,128)(2,1)S(1)}, u32[]{:S(2)}, u32[]{:S(2)}) collective-permute-start(bf16[72,128]{1,0:T(8,128)(2,1)S(1)} %get-tuple-element.15), channel_id=1, source_target_pairs={{1,0},{2,1},{3,2},{4,3},{5,4},{6,5},{7,6},{8,7},{9,8},{10,9},{11,1... | collective-permute-start | bytes 55304 | tf_op jit(solution)/shard_map/ppermute | solution.py:20
  54.3 2.1 %copy-start.3 = (bf16[16,3,128,128]{3,2,1,0:T(8,128)(2,1)S(1)}, bf16[16,3,128,128]{3,2,1,0:T(8,128)(2,1)}, u32[]{:S(2)}) copy-start(bf16[16,3,128,128]{3,2,1,0:T(8,128)(2,1)} %param.13) | copy-start | bytes 4718596
  56.4 1.1 %copy-start.8 = (f32[72,2048]{1,0:T(8,128)S(1)}, f32[72,2048]{1,0:T(8,128)}, u32[]{:S(2)}) copy-start(f32[72,2048]{1,0:T(8,128)} %get-tuple-element.9) | copy-start | bytes 1769476
  58.5 8.2 %collective-permute-start.6 = (bf16[72,128]{1,0:T(8,128)(2,1)S(1)}, bf16[72,128]{1,0:T(8,128)(2,1)S(1)}, u32[]{:S(2)}, u32[]{:S(2)}) collective-permute-start(bf16[72,128]{1,0:T(8,128)(2,1)S(1)} %get-tuple-element.12), channel_id=1, source_target_pairs={{0,1},{1,2},{2,3},{3,4},{4,5},{5,6},{6,7},{7,8},{8,9},{9,10},{10,1... | collective-permute-start | bytes 55304 | tf_op jit(solution)/shard_map/ppermute | solution.py:19
  60.4 7.8 %collective-permute-start.7 = (bf16[72,128]{1,0:T(8,128)(2,1)S(1)}, bf16[72,128]{1,0:T(8,128)(2,1)S(1)}, u32[]{:S(2)}, u32[]{:S(2)}) collective-permute-start(bf16[72,128]{1,0:T(8,128)(2,1)S(1)} %get-tuple-element.13), channel_id=1, source_target_pairs={{1,0},{2,1},{3,2},{4,3},{5,4},{6,5},{7,6},{8,7},{9,8},{10,9},{11,1... | collective-permute-start | bytes 55304 | tf_op jit(solution)/shard_map/ppermute | solution.py:20
  70.7 2.1 %copy-start.4 = (bf16[16,3,128,128]{3,2,1,0:T(8,128)(2,1)S(1)}, bf16[16,3,128,128]{3,2,1,0:T(8,128)(2,1)}, u32[]{:S(2)}) copy-start(bf16[16,3,128,128]{3,2,1,0:T(8,128)(2,1)} %param.13) | copy-start | bytes 4718596
  72.8 1.1 %copy-start.6 = (f32[72,2048]{1,0:T(8,128)S(1)}, f32[72,2048]{1,0:T(8,128)}, u32[]{:S(2)}) copy-start(f32[72,2048]{1,0:T(8,128)} %get-tuple-element.7) | copy-start | bytes 1769476
  99.2 1.8 %copy-start.5 = (bf16[1152,1152]{1,0:T(8,128)(2,1)S(1)}, bf16[1152,1152]{1,0:T(8,128)(2,1)}, u32[]{:S(2)}) copy-start(bf16[1152,1152]{1,0:T(8,128)(2,1)} %param.17) | copy-start | bytes 7962628
where the time goes:
time: 103 us; the launch traced here: 102 us
  starting transfers between devices  40.8 us (40%)
  blocking collectives  24.9 us (24%)
  matrix products  12.4 us (12%)
  local copies, waits for them, and re-layouts  10.6 us (10%)
  other arithmetic  9.05 us (9%)
  waiting for transfers between devices  4.3 us (4%)
    ppermute x4, starting transfers between devices, extended_2(): after = lax.ppermute(initial, axis, down)  30.8 us
    all_to_all x1, blocking collectives, per_device(): lax.all_to_all(final, 'comp', split_axis=1, concat_axis=0, tiled=True)  24.9 us
    ppermute x4, starting transfers between devices, extended_2(): before = lax.ppermute(last, axis, up)  10 us
    dot_general x4, matrix products, per_device(): jnp.einsum('kbjc,bjcd->kbd', gathered, transport_two, preferred_element_t...  8.2 us
    gather x4, local copies, waits for them, and re-layouts, per_device(): gathered = jnp.take(extended, block_cols, axis=1)  6.84 us
    convert_element_type x4, other arithmetic, per_device(): rounded = field.astype(jnp.bfloat16)  4.31 us
    ppermute x4, waiting for transfers between devices, extended_2(): after = lax.ppermute(initial, axis, down)  4.29 us
    unnamed x24, local copies, waits for them, and re-layouts  3.23 us
  transfers between devices with their start and end apart: 8, of which 3 were waited for; matrix products, arithmetic and copies ran while one was open for 2% of the time, Pallas kernels for 0%

commit v1 on v0

v1 whole, which is shorter than its diff:
```python
import functools

import jax
import jax.numpy as jnp
from jax import lax
from jax.experimental import pallas as pl
from jax.experimental.pallas import tpu as pltpu
from jax.sharding import PartitionSpec as P

SUBSTEPS = 4
KEEP = 0.25


def in_vmem(x):
    return pltpu.with_memory_space_constraint(x, pltpu.VMEM)


def whole():
    return pl.BlockSpec(memory_space=pltpu.VMEM)


def call(body, outs, n_vmem, limit, name):
    return pl.pallas_call(
        body,
        out_shape=[pltpu.VMEM(s, d) for s, d in outs],
        grid_spec=pltpu.PrefetchScalarGridSpec(
            num_scalar_prefetch=1,
            grid=(),
            in_specs=[whole()] * n_vmem,
            out_specs=[whole()] * len(outs),
        ),
        compiler_params=pltpu.CompilerParams(vmem_limit_bytes=limit),
        name=name,
    )


def row_update(b, chosen, before, after, value, one, two, coef_one, coef_two):
    width = value.shape[1]
    gathered = jnp.concatenate([chosen, before, after], axis=1)
    both = jnp.concatenate([one, two], axis=1)
    flow = jnp.dot(gathered, both, preferred_element_type=jnp.float32)
    moved = value + coef_one * flow[:, :width] + coef_two * flow[:, width:]
    return jnp.maximum(moved, KEEP * value)


def chosen_block(e, left, right, blocks_ref):
    n = blocks_ref.shape[0]
    inner = blocks_ref[jnp.clip(e - 1, 0, n - 1)]
    return jnp.where(e == 0, left, jnp.where(e == n + 1, right, inner))


def edge_kernel(cols, left_ref, right_ref, blocks_ref, first_ref, last_ref, one_ref, two_ref, c1_ref, c2_ref, *outs):
    first16, last16, first32, last32 = outs
    n, rows, width = blocks_ref.shape
    left, right = left_ref[...], right_ref[...]
    c1, c2 = c1_ref[...], c2_ref[...]
    for b, value_ref, out16, out32 in ((0, first_ref, first16, first32), (n - 1, last_ref, last16, last32)):
        new = row_update(
            b,
            chosen_block(cols[3 * b], left, right, blocks_ref),
            left if b == 0 else blocks_ref[b - 1],
            right if b == n - 1 else blocks_ref[b + 1],
            value_ref[...],
            one_ref[b].reshape(-1, width),
            two_ref[b].reshape(-1, width),
            c1,
            c2,
        )
        out32[...] = new
        out16[...] = new.astype(jnp.bfloat16)


def inner_kernel(cols, left_ref, right_ref, blocks_ref, field_ref, first16, last16, one_ref, two_ref, c1_ref, c2_ref, *outs):
    out16, out32 = outs
    n, rows, width = blocks_ref.shape
    left, right = left_ref[...], right_ref[...]
    c1, c2 = c1_ref[...], c2_ref[...]
    out16[0] = first16[...]
    out16[n - 1] = last16[...]
    for b in range(1, n - 1):
        new = row_update(
            b,
            chosen_block(cols[3 * b], left, right, blocks_ref),
            blocks_ref[b - 1],
            blocks_ref[b + 1],
            field_ref[b],
            one_ref[b].reshape(-1, width),
            two_ref[b].reshape(-1, width),
            c1,
            c2,
        )
        out32[b] = new
        out16[b] = new.astype(jnp.bfloat16)


def last_kernel(cols, left_ref, right_ref, blocks_ref, field_ref, first_ref, last_ref, one_ref, two_ref, c1_ref, c2_ref, *outs):
    (out16,) = outs
    n, rows, width = blocks_ref.shape
    left, right = left_ref[...], right_ref[...]
    c1, c2 = c1_ref[...], c2_ref[...]
    for b in range(n):
        value = first_ref[...] if b == 0 else last_ref[...] if b == n - 1 else field_ref[b]
        new = row_update(
            b,
            chosen_block(cols[3 * b], left, right, blocks_ref),
            left if b == 0 else blocks_ref[b - 1],
            right if b == n - 1 else blocks_ref[b + 1],
            value,
            one_ref[b].reshape(-1, width),
            two_ref[b].reshape(-1, width),
            c1,
            c2,
        )
        out16[b] = new.astype(jnp.bfloat16)


def load_kernel(cols, action_ref, out16, out32, first32, last32):
    n, rows, width = out16.shape
    for b in range(n):
        value = action_ref[:, b * width : (b + 1) * width]
        out32[b] = value
        out16[b] = value.astype(jnp.bfloat16)
    first32[...] = action_ref[:, :width]
    last32[...] = action_ref[:, (n - 1) * width :]


def source_kernel(cells_ref, one_ref, two_ref, out_ref):
    step = pl.program_id(0)
    tile = out_ref.shape[2]
    cells = cells_ref[...].T
    own = cells_ref[pl.ds(pl.multiple_of(step * tile, tile), tile), :].astype(jnp.float32).T
    first = jnp.dot(cells, one_ref[...], preferred_element_type=jnp.float32)
    second = jnp.dot(cells, two_ref[...], preferred_element_type=jnp.float32)
    out_ref[0] = own + 0.5 * (first * own - second * own * own)


def source_terms(exchanged, quad_one, quad_two):
    comps, cells = exchanged.shape
    tile = 384
    return pl.pallas_call(
        source_kernel,
        out_shape=jax.ShapeDtypeStruct((1, cells, comps), jnp.float32),
        grid=(comps // tile,),
        in_specs=[
            pl.BlockSpec((comps, cells), lambda i: (0, 0)),
            pl.BlockSpec((comps, tile), lambda i: (0, i)),
            pl.BlockSpec((comps, tile), lambda i: (0, i)),
        ],
        out_specs=pl.BlockSpec((1, cells, tile), lambda i: (0, 0, i)),
        compiler_params=pltpu.CompilerParams(vmem_limit_bytes=16 << 20),
        name="source_terms",
    )(exchanged, quad_one, quad_two)


def per_device(
    action, coef_one, coef_two, transport_one, transport_two, block_cols, quad_one, quad_two
):
    rows, cells_dev = action.shape
    n, _, width, _ = transport_one.shape
    dom = lax.axis_size("dom")
    up = [(i, i + 1) for i in range(dom - 1)]
    down = [(i + 1, i) for i in range(dom - 1)]
    bf16, f32 = jnp.bfloat16, jnp.float32
    block, blocks = (rows, width), (n, rows, width)

    cols = block_cols.reshape(-1)
    one, two = in_vmem(transport_one), in_vmem(transport_two)
    c1 = in_vmem(jnp.broadcast_to(coef_one[:, None], block))
    c2 = in_vmem(jnp.broadcast_to(coef_two[:, None], block))

    first = action[:, :width].astype(bf16)
    last = action[:, cells_dev - width :].astype(bf16)
    left = lax.ppermute(last, "dom", up)
    right = lax.ppermute(first, "dom", down)
    value16, value32, first32, last32 = call(
        load_kernel, [(blocks, bf16), (blocks, f32), (block, f32), (block, f32)], 1, 4 << 20, "load"
    )(cols, in_vmem(action))
    for substep in range(SUBSTEPS - 1):
        first, last, first32, last32 = call(
            edge_kernel, [(block, bf16), (block, bf16), (block, f32), (block, f32)], 9, 4 << 20, "edges"
        )(cols, in_vmem(left), in_vmem(right), value16, first32, last32, one, two, c1, c2)
        new_left = lax.ppermute(last, "dom", up)
        new_right = lax.ppermute(first, "dom", down)
        value16, value32 = call(
            inner_kernel, [(blocks, bf16), (blocks, f32)], 10, 4 << 20, "inner"
        )(cols, in_vmem(left), in_vmem(right), value16, value32, first, last, one, two, c1, c2)
        left, right = new_left, new_right
    (final,) = call(last_kernel, [(blocks, bf16)], 10, 4 << 20, "last")(
        cols, in_vmem(left), in_vmem(right), value16, value32, first32, last32, one, two, c1, c2
    )
    exchanged = lax.all_to_all(final, "comp", split_axis=0, concat_axis=0, tiled=True)
    return source_terms(exchanged.reshape(n * rows, width), quad_one, quad_two)


def solution(mesh):
    in_specs = (
        P("comp", "dom"),
        P("comp"),
        P("comp"),
        P("dom", None, None, None),
        P("dom", None, None, None),
        P("dom", None),
        P(),
        P(),
    )
    out_specs = P("dom", "comp", None)
    return jax.shard_map(
        per_device, mesh=mesh, in_specs=in_specs, out_specs=out_specs, check_vma=False
    )
```

time: 103 us -> 87.1 us (0.85)
  matrix products: 12.4 us -> 0 us
  Pallas kernels: 0 us -> 10.8 us
  other arithmetic: 9.05 us -> 1.21 us
  local copies, waits for them, and re-layouts: 10.6 us -> 4.8 us
    dot_general x10 -> x0, matrix products: 12.4 us -> none  [the longest x4 8.2 us: per_device(): jnp.einsum('kbjc,bjcd->kbd', gathered, transport_two, preferred_element_t...]
    pallas_call x0 -> x9, Pallas kernels: none -> 10.8 us  [the longest x3 3.73 us: per_device(): call(inner_kernel, [(blocks, bf16), (blocks, f32)], 10, 4 << 20, 'inner')]
    gather x4 -> x0, local copies, waits for them, and re-layouts: 6.84 us -> none  [per_device(): gathered = jnp.take(extended, block_cols, axis=1)]
    convert_element_type x4 -> x0, other arithmetic: 4.31 us -> none  [per_device(): rounded = field.astype(jnp.bfloat16)]
    reshape x4 -> x0, other arithmetic: 3.14 us -> none  [per_device(): extended = padded.reshape(comp_rows, nblocks + 2, width)]
    broadcast_in_dim x1 -> x2, local copies, waits for them, and re-layouts: 0.09 us -> 1.46 us  [the longest x1 0.73 us: per_device(): c2 = in_vmem(jnp.broadcast_to(coef_two[:, None], block))]
    another operation x0 -> x1, other arithmetic: none -> 1.21 us
    unnamed x24 -> x13, local copies, waits for them, and re-layouts: 3.23 us -> 3.25 us
  transfers between devices with their start and end apart: 8 -> 8, of which waited for: 3 -> 4; matrix products, arithmetic and copies ran while one was open for 2% -> 1% of each run, Pallas kernels for 0% -> 5%
where the time goes in v1:
time: 87.1 us; the launch traced here: 86.6 us
  starting transfers between devices  40.8 us (47%)
  blocking collectives  24.9 us (29%)
  Pallas kernels  10.8 us (12%)
  local copies, waits for them, and re-layouts  4.8 us (6%)
  waiting for transfers between devices  3.82 us (4%)
  other arithmetic  1.21 us (1%)
    all_to_all x1, blocking collectives, per_device(): lax.all_to_all(final, 'comp', split_axis=0, concat_axis=0, tiled=True)  24.9 us
    ppermute x3, starting transfers between devices, per_device(): new_right = lax.ppermute(first, 'dom', down)  18.7 us
    ppermute x1, starting transfers between devices, per_device(): right = lax.ppermute(first, 'dom', down)  14.5 us
    ppermute x3, starting transfers between devices, per_device(): new_left = lax.ppermute(last, 'dom', up)  5.76 us
    pallas_call x3, Pallas kernels, per_device(): call(inner_kernel, [(blocks, bf16), (blocks, f32)], 10, 4 << 20, 'inner')  3.73 us
    ppermute x1, waiting for transfers between devices, per_device(): left = lax.ppermute(last, 'dom', up)  3.3 us
    unnamed x13, local copies, waits for them, and re-layouts  3.25 us
    pallas_call x1, Pallas kernels, source_terms(): pl.pallas_call(source_kernel, out_shape=jax.ShapeDtypeStruct((1, cells, c...  2.94 us
  transfers between devices with their start and end apart: 8, of which 4 were waited for; matrix products, arithmetic and copies ran while one was open for 1% of the time, Pallas kernels for 5%

profile of v1, /device:TPU:8, one launch (start us, length us, event | category | flops | bytes accessed | tf_op | source)
XLA Modules:
  0.0 86.6 jit_solution(7184898608101450549)
XLA Ops:
  0.0 1.2 %convert.4 = bf16[72,2048]{1,0:T(8,128)(2,1)S(1)} convert(f32[72,2048]{1,0:T(8,128)} %action_ref.1) | non-fusion elementwise | flops 147456 | bytes 884736 | tf_op jit(solution)/shard_map/convert.1
  1.2 14.5 %collective-permute-start.1 = (bf16[72,128]{1,0:T(8,128)(2,1)S(1)}, bf16[72,128]{1,0:T(8,128)(2,1)S(1)}, u32[]{:S(2)}, u32[]{:S(2)}) collective-permute-start(bf16[72,128]{1,0:T(8,128)(2,1)S(1)} %get-tuple-element.49), channel_id=1, source_target_pairs={{1,0},{2,1},{3,2},{4,3},{5,4},{6,5},{7,6},{8,7},{9,8},{10,9},{11,1... | collective-permute-start | bytes 55304 | tf_op jit(solution)/shard_map/ppermute | solution.py:174
  15.7 1.9 %collective-permute-start = (bf16[72,128]{1,0:T(8,128)(2,1)S(1)}, bf16[72,128]{1,0:T(8,128)(2,1)S(1)}, u32[]{:S(2)}, u32[]{:S(2)}) collective-permute-start(bf16[72,128]{1,0:T(8,128)(2,1)S(1)} %get-tuple-element.50), channel_id=1, source_target_pairs={{0,1},{1,2},{2,3},{3,4},{4,5},{5,6},{6,7},{7,8},{8,9},{9,10},{10,1... | collective-permute-start | bytes 55304 | tf_op jit(solution)/shard_map/ppermute | solution.py:173
  17.6 0.8 copy.10
  18.5 1.1 %copy-done.5 = f32[72,2048]{1,0:T(8,128)S(1)} copy-done((f32[72,2048]{1,0:T(8,128)S(1)}, f32[72,2048]{1,0:T(8,128)}, u32[]{:S(2)}) %copy-start.5) | copy-done | bytes 589848
  20.2 3.3 %collective-permute-done.left_ref = bf16[72,128]{1,0:T(8,128)(2,1)S(1)} collective-permute-done((bf16[72,128]{1,0:T(8,128)(2,1)S(1)}, bf16[72,128]{1,0:T(8,128)(2,1)S(1)}, u32[]{:S(2)}, u32[]{:S(2)}) %collective-permute-start) | collective-permute-done | bytes 18464 | tf_op jit(solution)/shard_map/ppermute | solution.py:173
  23.5 0.7 broadcast_in_dim.4.c1_ref
  24.2 0.7 broadcast_in_dim.5.c2_ref
  24.9 1.4 %copy-done.1 = bf16[16,3,128,128]{3,2,1,0:T(8,128)(2,1)S(1)} copy-done((bf16[16,3,128,128]{3,2,1,0:T(8,128)(2,1)S(1)}, bf16[16,3,128,128]{3,2,1,0:T(8,128)(2,1)}, u32[]{:S(2)}) %copy-start.1) | copy-done | bytes 1572888
  26.4 0.7 edges.3
  27.1 1.9 %collective-permute-start.2 = (bf16[72,128]{1,0:T(8,128)(2,1)S(1)}, bf16[72,128]{1,0:T(8,128)(2,1)S(1)}, u32[]{:S(2)}, u32[]{:S(2)}) collective-permute-start(bf16[72,128]{1,0:T(8,128)(2,1)S(1)} %get-tuple-element.30.last16), channel_id=1, source_target_pairs={{0,1},{1,2},{2,3},{3,4},{4,5},{5,6},{6,7},{7,8},{8,9},{9,10},{10,1... | collective-permute-start | bytes 55304 | tf_op jit(solution)/shard_map/ppermute | solution.py:182
  29.0 6.0 %collective-permute-start.3 = (bf16[72,128]{1,0:T(8,128)(2,1)S(1)}, bf16[72,128]{1,0:T(8,128)(2,1)S(1)}, u32[]{:S(2)}, u32[]{:S(2)}) collective-permute-start(bf16[72,128]{1,0:T(8,128)(2,1)S(1)} %get-tuple-element.31.first16), channel_id=1, source_target_pairs={{1,0},{2,1},{3,2},{4,3},{5,4},{6,5},{7,6},{8,7},{9,8},{10,9},{11,1... | collective-permute-start | bytes 55304 | tf_op jit(solution)/shard_map/ppermute | solution.py:183
  35.1 1.2 %inner.3 = (bf16[16,72,128]{2,1,0:T(8,128)(2,1)S(1)}, f32[16,72,128]{2,1,0:T(8,128)S(1)}) custom-call(s32[48]{0:T(128)S(1)} %reshape.8.cols, bf16[72,128]{1,0:T(8,128)(2,1)S(1)} %collective-permute-done.left_ref, bf16[72,128]{1,0:T(8,128)(2,1)S(1)} %collective-permute-done.1.right_ref, bf16[16,72,128]{2,1,0:T(8,128)(2,1)S(1)} %get-tuple-element.27.blocks_ref, ...), custom_call_target="tpu_custom_call" | custom-call | tf_op jit(solution)/shard_map/inner/pallas_call | solution.py:184
  36.5 0.7 edges.4
  37.3 1.9 %collective-permute-start.4 = (bf16[72,128]{1,0:T(8,128)(2,1)S(1)}, bf16[72,128]{1,0:T(8,128)(2,1)S(1)}, u32[]{:S(2)}, u32[]{:S(2)}) collective-permute-start(bf16[72,128]{1,0:T(8,128)(2,1)S(1)} %get-tuple-element.36.last16), channel_id=1, source_target_pairs={{0,1},{1,2},{2,3},{3,4},{4,5},{5,6},{6,7},{7,8},{8,9},{9,10},{10,1... | collective-permute-start | bytes 55304 | tf_op jit(solution)/shard_map/ppermute | solution.py:182
  39.2 6.3 %collective-permute-start.5 = (bf16[72,128]{1,0:T(8,128)(2,1)S(1)}, bf16[72,128]{1,0:T(8,128)(2,1)S(1)}, u32[]{:S(2)}, u32[]{:S(2)}) collective-permute-start(bf16[72,128]{1,0:T(8,128)(2,1)S(1)} %get-tuple-element.37.first16), channel_id=1, source_target_pairs={{1,0},{2,1},{3,2},{4,3},{5,4},{6,5},{7,6},{8,7},{9,8},{10,9},{11,1... | collective-permute-start | bytes 55304 | tf_op jit(solution)/shard_map/ppermute | solution.py:183
  45.5 1.2 %inner.4 = (bf16[16,72,128]{2,1,0:T(8,128)(2,1)S(1)}, f32[16,72,128]{2,1,0:T(8,128)S(1)}) custom-call(s32[48]{0:T(128)S(1)} %reshape.8.cols, bf16[72,128]{1,0:T(8,128)(2,1)S(1)} %collective-permute-done.2.left_ref, bf16[72,128]{1,0:T(8,128)(2,1)S(1)} %collective-permute-done.3.right_ref, bf16[16,72,128]{2,1,0:T(8,128)(2,1)S(1)} %get-tuple-element.33.blocks_ref, ...), custom_call_target="tpu_custom_call" | custom-call | tf_op jit(solution)/shard_map/inner/pallas_call | solution.py:184
  47.0 0.7 edges.5
  47.7 1.9 %collective-permute-start.6 = (bf16[72,128]{1,0:T(8,128)(2,1)S(1)}, bf16[72,128]{1,0:T(8,128)(2,1)S(1)}, u32[]{:S(2)}, u32[]{:S(2)}) collective-permute-start(bf16[72,128]{1,0:T(8,128)(2,1)S(1)} %get-tuple-element.42.last16), channel_id=1, source_target_pairs={{0,1},{1,2},{2,3},{3,4},{4,5},{5,6},{6,7},{7,8},{8,9},{9,10},{10,1... | collective-permute-start | bytes 55304 | tf_op jit(solution)/shard_map/ppermute | solution.py:182
  49.7 6.3 %collective-permute-start.7 = (bf16[72,128]{1,0:T(8,128)(2,1)S(1)}, bf16[72,128]{1,0:T(8,128)(2,1)S(1)}, u32[]{:S(2)}, u32[]{:S(2)}) collective-permute-start(bf16[72,128]{1,0:T(8,128)(2,1)S(1)} %get-tuple-element.43.first16), channel_id=1, source_target_pairs={{1,0},{2,1},{3,2},{4,3},{5,4},{6,5},{7,6},{8,7},{9,8},{10,9},{11,1... | collective-permute-start | bytes 55304 | tf_op jit(solution)/shard_map/ppermute | solution.py:183
  56.0 1.2 %inner.5 = (bf16[16,72,128]{2,1,0:T(8,128)(2,1)S(1)}, f32[16,72,128]{2,1,0:T(8,128)S(1)}) custom-call(s32[48]{0:T(128)S(1)} %reshape.8.cols, bf16[72,128]{1,0:T(8,128)(2,1)S(1)} %collective-permute-done.4.left_ref, bf16[72,128]{1,0:T(8,128)(2,1)S(1)} %collective-permute-done.5.right_ref, bf16[16,72,128]{2,1,0:T(8,128)(2,1)S(1)} %get-tuple-element.39.blocks_ref, ...), custom_call_target="tpu_custom_call" | custom-call | tf_op jit(solution)/shard_map/inner/pallas_call | solution.py:184
  57.4 1.3 %last.1 = bf16[16,72,128]{2,1,0:T(8,128)(2,1)S(1)} custom-call(s32[48]{0:T(128)S(1)} %reshape.8.cols, bf16[72,128]{1,0:T(8,128)(2,1)S(1)} %collective-permute-done.6.left_ref, bf16[72,128]{1,0:T(8,128)(2,1)S(1)} %collective-permute-done.7.right_ref, bf16[16,72,128]{2,1,0:T(8,128)(2,1)S(1)} %get-tuple-element.45.blocks_ref, ...), custom_call_target="tpu_custom_call" | custom-call | tf_op jit(solution)/shard_map/last/pallas_call | solution.py:188
  58.7 24.9 %all_to_all.5 = bf16[16,72,128]{2,1,0:T(8,128)(2,1)S(1)} all-to-all(bf16[16,72,128]{2,1,0:T(8,128)(2,1)S(1)} %last.1), channel_id=1, replica_groups=mesh['comp'=16,'dom'=48] {'comp'}, dimensions={0} | all-to-all | bytes 589824 | tf_op jit(solution)/shard_map/all_to_all | solution.py:191
  83.7 2.9 %source_terms.1 = f32[1,128,1152]{2,1,0:T(8,128)} custom-call(bf16[1152,128]{1,0:T(8,128)(2,1)S(1)} %bitcast.1, bf16[1152,1152]{1,0:T(8,128)(2,1)S(1)} %copy-done.3, bf16[1152,1152]{1,0:T(8,128)(2,1)S(1)} %copy-done.4), custom_call_target="tpu_custom_call" | custom-call | tf_op jit(solution)/shard_map/source_terms/pallas_call | solution.py:140
  (20 shorter events, 1.2 us)
Async XLA Ops:
  0.0 24.9 %copy-start = (bf16[16,3,128,128]{3,2,1,0:T(8,128)(2,1)S(1)}, bf16[16,3,128,128]{3,2,1,0:T(8,128)(2,1)}, u32[]{:S(2)}) copy-start(bf16[16,3,128,128]{3,2,1,0:T(8,128)(2,1)} %one_ref.14) | copy-start | bytes 4718596
  1.2 18.9 %collective-permute-start.1 = (bf16[72,128]{1,0:T(8,128)(2,1)S(1)}, bf16[72,128]{1,0:T(8,128)(2,1)S(1)}, u32[]{:S(2)}, u32[]{:S(2)}) collective-permute-start(bf16[72,128]{1,0:T(8,128)(2,1)S(1)} %get-tuple-element.49), channel_id=1, source_target_pairs={{1,0},{2,1},{3,2},{4,3},{5,4},{6,5},{7,6},{8,7},{9,8},{10,9},{11,1... | collective-permute-start | bytes 55304 | tf_op jit(solution)/shard_map/ppermute | solution.py:174
  15.7 7.8 %collective-permute-start = (bf16[72,128]{1,0:T(8,128)(2,1)S(1)}, bf16[72,128]{1,0:T(8,128)(2,1)S(1)}, u32[]{:S(2)}, u32[]{:S(2)}) collective-permute-start(bf16[72,128]{1,0:T(8,128)(2,1)S(1)} %get-tuple-element.50), channel_id=1, source_target_pairs={{0,1},{1,2},{2,3},{3,4},{4,5},{5,6},{6,7},{7,8},{8,9},{9,10},{10,1... | collective-permute-start | bytes 55304 | tf_op jit(solution)/shard_map/ppermute | solution.py:173
  18.5 1.1 %copy-start.5 = (f32[72,2048]{1,0:T(8,128)S(1)}, f32[72,2048]{1,0:T(8,128)}, u32[]{:S(2)}) copy-start(f32[72,2048]{1,0:T(8,128)} %action_ref.1) | copy-start | bytes 1769476
  24.9 1.4 %copy-start.1 = (bf16[16,3,128,128]{3,2,1,0:T(8,128)(2,1)S(1)}, bf16[16,3,128,128]{3,2,1,0:T(8,128)(2,1)}, u32[]{:S(2)}) copy-start(bf16[16,3,128,128]{3,2,1,0:T(8,128)(2,1)} %two_ref.14) | copy-start | bytes 4718596
  26.4 8.7 %copy-start.2 = (bf16[16,3,128,128]{3,2,1,0:T(8,128)(2,1)S(1)}, bf16[16,3,128,128]{3,2,1,0:T(8,128)(2,1)}, u32[]{:S(2)}) copy-start(bf16[16,3,128,128]{3,2,1,0:T(8,128)(2,1)} %two_ref.14) | copy-start | bytes 4718596
  27.1 9.2 %collective-permute-start.2 = (bf16[72,128]{1,0:T(8,128)(2,1)S(1)}, bf16[72,128]{1,0:T(8,128)(2,1)S(1)}, u32[]{:S(2)}, u32[]{:S(2)}) collective-permute-start(bf16[72,128]{1,0:T(8,128)(2,1)S(1)} %get-tuple-element.30.last16), channel_id=1, source_target_pairs={{0,1},{1,2},{2,3},{3,4},{4,5},{5,6},{6,7},{7,8},{8,9},{9,10},{10,1... | collective-permute-start | bytes 55304 | tf_op jit(solution)/shard_map/ppermute | solution.py:182
  29.0 7.5 %collective-permute-start.3 = (bf16[72,128]{1,0:T(8,128)(2,1)S(1)}, bf16[72,128]{1,0:T(8,128)(2,1)S(1)}, u32[]{:S(2)}, u32[]{:S(2)}) collective-permute-start(bf16[72,128]{1,0:T(8,128)(2,1)S(1)} %get-tuple-element.31.first16), channel_id=1, source_target_pairs={{1,0},{2,1},{3,2},{4,3},{5,4},{6,5},{7,6},{8,7},{9,8},{10,9},{11,1... | collective-permute-start | bytes 55304 | tf_op jit(solution)/shard_map/ppermute | solution.py:183
  37.3 9.5 %collective-permute-start.4 = (bf16[72,128]{1,0:T(8,128)(2,1)S(1)}, bf16[72,128]{1,0:T(8,128)(2,1)S(1)}, u32[]{:S(2)}, u32[]{:S(2)}) collective-permute-start(bf16[72,128]{1,0:T(8,128)(2,1)S(1)} %get-tuple-element.36.last16), channel_id=1, source_target_pairs={{0,1},{1,2},{2,3},{3,4},{4,5},{5,6},{6,7},{7,8},{8,9},{9,10},{10,1... | collective-permute-start | bytes 55304 | tf_op jit(solution)/shard_map/ppermute | solution.py:182
  39.2 7.8 %collective-permute-start.5 = (bf16[72,128]{1,0:T(8,128)(2,1)S(1)}, bf16[72,128]{1,0:T(8,128)(2,1)S(1)}, u32[]{:S(2)}, u32[]{:S(2)}) collective-permute-start(bf16[72,128]{1,0:T(8,128)(2,1)S(1)} %get-tuple-element.37.first16), channel_id=1, source_target_pairs={{1,0},{2,1},{3,2},{4,3},{5,4},{6,5},{7,6},{8,7},{9,8},{10,9},{11,1... | collective-permute-start | bytes 55304 | tf_op jit(solution)/shard_map/ppermute | solution.py:183
  47.7 9.5 %collective-permute-start.6 = (bf16[72,128]{1,0:T(8,128)(2,1)S(1)}, bf16[72,128]{1,0:T(8,128)(2,1)S(1)}, u32[]{:S(2)}, u32[]{:S(2)}) collective-permute-start(bf16[72,128]{1,0:T(8,128)(2,1)S(1)} %get-tuple-element.42.last16), channel_id=1, source_target_pairs={{0,1},{1,2},{2,3},{3,4},{4,5},{5,6},{6,7},{7,8},{8,9},{9,10},{10,1... | collective-permute-start | bytes 55304 | tf_op jit(solution)/shard_map/ppermute | solution.py:182
  49.7 7.8 %collective-permute-start.7 = (bf16[72,128]{1,0:T(8,128)(2,1)S(1)}, bf16[72,128]{1,0:T(8,128)(2,1)S(1)}, u32[]{:S(2)}, u32[]{:S(2)}) collective-permute-start(bf16[72,128]{1,0:T(8,128)(2,1)S(1)} %get-tuple-element.43.first16), channel_id=1, source_target_pairs={{1,0},{2,1},{3,2},{4,3},{5,4},{6,5},{7,6},{8,7},{9,8},{10,9},{11,1... | collective-permute-start | bytes 55304 | tf_op jit(solution)/shard_map/ppermute | solution.py:183
  56.0 27.7 %copy-start.4 = (bf16[1152,1152]{1,0:T(8,128)(2,1)S(1)}, bf16[1152,1152]{1,0:T(8,128)(2,1)}, u32[]{:S(2)}) copy-start(bf16[1152,1152]{1,0:T(8,128)(2,1)} %two_ref.15) | copy-start | bytes 7962628
  57.2 26.4 %copy-start.3 = (bf16[1152,1152]{1,0:T(8,128)(2,1)S(1)}, bf16[1152,1152]{1,0:T(8,128)(2,1)}, u32[]{:S(2)}) copy-start(bf16[1152,1152]{1,0:T(8,128)(2,1)} %one_ref.15) | copy-start | bytes 7962628

commit v2 on v1

v2 whole, which is shorter than its diff:
```python
import jax
import jax.numpy as jnp
from jax import lax
from jax.experimental import pallas as pl
from jax.experimental.pallas import tpu as pltpu
from jax.sharding import PartitionSpec as P

SUBSTEPS = 4
KEEP = 0.25


def in_vmem(x):
    return pltpu.with_memory_space_constraint(x, pltpu.VMEM)


def in_hbm(x):
    return pltpu.with_memory_space_constraint(x, pltpu.HBM)


def in_smem(x):
    return pltpu.with_memory_space_constraint(x, pltpu.SMEM)


def vmem():
    return pl.BlockSpec(memory_space=pltpu.VMEM)


def smem():
    return pl.BlockSpec(memory_space=pltpu.SMEM)


def hbm():
    return pl.BlockSpec(memory_space=pltpu.HBM)


def call(body, outs, in_specs, name, scratch=(), limit=4 << 20):
    return pl.pallas_call(
        body,
        out_shape=[pltpu.VMEM(s, d) for s, d in outs],
        in_specs=in_specs,
        out_specs=[vmem()] * len(outs),
        scratch_shapes=list(scratch),
        compiler_params=pltpu.CompilerParams(vmem_limit_bytes=limit),
        name=name,
    )


def row_update(b, chosen, before, after, value, one, two, coef_one, coef_two):
    width = value.shape[1]
    gathered = jnp.concatenate([chosen, before, after], axis=1)
    both = jnp.concatenate([one, two], axis=1)
    flow = jnp.dot(gathered, both, preferred_element_type=jnp.float32)
    moved = value + coef_one * flow[:, :width] + coef_two * flow[:, width:]
    return jnp.maximum(moved, KEEP * value)


def chosen_block(e, left, right, blocks_ref):
    n = blocks_ref.shape[0]
    inner = blocks_ref[jnp.clip(e - 1, 0, n - 1)]
    return jnp.where(e == 0, left, jnp.where(e == n + 1, right, inner))


def edge_kernel(cols, left_ref, right_ref, blocks_ref, first_ref, last_ref, one_ref, two_ref, c1_ref, c2_ref, *outs):
    last16, first16, last32, first32 = outs
    n, rows, width = blocks_ref.shape
    left, right = left_ref[...], right_ref[...]
    c1, c2 = c1_ref[...], c2_ref[...]
    for b, value_ref, out16, out32 in ((0, first_ref, first16, first32), (n - 1, last_ref, last16, last32)):
        new = row_update(
            b,
            chosen_block(cols[0, b], left, right, blocks_ref),
            left if b == 0 else blocks_ref[b - 1],
            right if b == n - 1 else blocks_ref[b + 1],
            value_ref[...],
            one_ref[b].reshape(-1, width),
            two_ref[b].reshape(-1, width),
            c1,
            c2,
        )
        out32[...] = new
        out16[...] = new.astype(jnp.bfloat16)


def inner_kernel(cols, left_ref, right_ref, blocks_ref, field_ref, first16, last16, one_ref, two_ref, c1_ref, c2_ref, *outs):
    out16, out32 = outs
    n, rows, width = blocks_ref.shape
    left, right = left_ref[...], right_ref[...]
    c1, c2 = c1_ref[...], c2_ref[...]
    out16[0] = first16[...]
    out16[n - 1] = last16[...]
    for b in range(1, n - 1):
        new = row_update(
            b,
            chosen_block(cols[0, b], left, right, blocks_ref),
            blocks_ref[b - 1],
            blocks_ref[b + 1],
            field_ref[b],
            one_ref[b].reshape(-1, width),
            two_ref[b].reshape(-1, width),
            c1,
            c2,
        )
        out32[b] = new
        out16[b] = new.astype(jnp.bfloat16)


def last_kernel(cols, left_ref, right_ref, blocks_ref, field_ref, first_ref, last_ref, one_ref, two_ref, c1_ref, c2_ref, *outs):
    (out16,) = outs
    n, rows, width = blocks_ref.shape
    left, right = left_ref[...], right_ref[...]
    c1, c2 = c1_ref[...], c2_ref[...]
    for b in range(n):
        value = first_ref[...] if b == 0 else last_ref[...] if b == n - 1 else field_ref[b]
        new = row_update(
            b,
            chosen_block(cols[0, b], left, right, blocks_ref),
            left if b == 0 else blocks_ref[b - 1],
            right if b == n - 1 else blocks_ref[b + 1],
            value,
            one_ref[b].reshape(-1, width),
            two_ref[b].reshape(-1, width),
            c1,
            c2,
        )
        out16[b] = new.astype(jnp.bfloat16)


def begin_kernel(action_ref, last16, first16, buffers, sems):
    width = first16.shape[1]
    cells = action_ref.shape[1]
    copies = [
        pltpu.make_async_copy(action_ref.at[:, pl.ds(cells - width, width)], buffers.at[0], sems.at[0]),
        pltpu.make_async_copy(action_ref.at[:, pl.ds(0, width)], buffers.at[1], sems.at[1]),
    ]
    for copy in copies:
        copy.start()
    for copy, out, i in zip(copies, (last16, first16), (0, 1)):
        copy.wait()
        out[...] = buffers[i].astype(jnp.bfloat16)


def load_kernel(action_ref, coef_one_ref, coef_two_ref, one_hbm, two_hbm, *refs):
    out16, out32, first32, last32, one, two, c1, c2, sems = refs
    n, rows, width = out16.shape
    copies = [
        pltpu.make_async_copy(action_ref.at[:, pl.ds(b * width, width)], out32.at[b], sems.at[b])
        for b in range(n)
    ]
    weights = [
        pltpu.make_async_copy(one_hbm, one, sems.at[n]),
        pltpu.make_async_copy(two_hbm, two, sems.at[n + 1]),
    ]
    for copy in copies + weights:
        copy.start()
    c1[...] = jnp.broadcast_to(coef_one_ref[...], (width, rows)).T
    c2[...] = jnp.broadcast_to(coef_two_ref[...], (width, rows)).T
    for b in range(n):
        copies[b].wait()
        out16[b] = out32[b].astype(jnp.bfloat16)
    first32[...] = out32[0]
    last32[...] = out32[n - 1]
    for copy in weights:
        copy.wait()


def source_kernel(cells_ref, one_ref, two_ref, out_hbm, buffers, sems):
    steps, _, tile = buffers.shape
    cells = cells_ref[...].T
    copies = []
    for i in range(steps):
        at = slice(i * tile, (i + 1) * tile)
        own = cells[:, at].astype(jnp.float32)
        first = jnp.dot(cells, one_ref[:, at], preferred_element_type=jnp.float32)
        second = jnp.dot(cells, two_ref[:, at], preferred_element_type=jnp.float32)
        buffers[i] = own + 0.5 * (first * own - second * own * own)
        copies.append(pltpu.make_async_copy(buffers.at[i], out_hbm.at[0, :, pl.ds(i * tile, tile)], sems.at[i]))
        copies[-1].start()
    for copy in copies:
        copy.wait()


def source_terms(exchanged, quad_one, quad_two):
    comps, cells = exchanged.shape
    tile = 384
    steps = comps // tile
    return pl.pallas_call(
        source_kernel,
        out_shape=jax.ShapeDtypeStruct((1, cells, comps), jnp.float32),
        in_specs=[vmem()] * 3,
        out_specs=hbm(),
        scratch_shapes=[
            pltpu.VMEM((steps, cells, tile), jnp.float32),
            pltpu.SemaphoreType.DMA((steps,)),
        ],
        compiler_params=pltpu.CompilerParams(vmem_limit_bytes=8 << 20),
        name="source_terms",
    )(in_vmem(exchanged), in_vmem(quad_one), in_vmem(quad_two))


def per_device(
    action, coef_one, coef_two, transport_one, transport_two, block_cols, quad_one, quad_two
):
    rows, cells_dev = action.shape
    n, nnz, width, _ = transport_one.shape
    dom = lax.axis_size("dom")
    up = [(i, i + 1) for i in range(dom - 1)]
    down = [(i + 1, i) for i in range(dom - 1)]
    bf16, f32 = jnp.bfloat16, jnp.float32
    block, blocks, weights = (rows, width), (n, rows, width), (n, nnz, width, width)

    cols = in_smem(block_cols.T)
    last, first = call(
        begin_kernel,
        [(block, bf16), (block, bf16)],
        [hbm()],
        "begin",
        [pltpu.VMEM((2, rows, width), f32), pltpu.SemaphoreType.DMA((2,))],
    )(in_hbm(action))
    left = lax.ppermute(last, "dom", up)
    right = lax.ppermute(first, "dom", down)
    value16, value32, first32, last32, one, two, c1, c2 = call(
        load_kernel,
        [(blocks, bf16), (blocks, f32), (block, f32), (block, f32), (weights, bf16), (weights, bf16), (block, f32), (block, f32)],
        [hbm(), vmem(), vmem(), hbm(), hbm()],
        "load",
        [pltpu.SemaphoreType.DMA((n + 2,))],
    )(
        in_hbm(action), coef_one.reshape(1, rows), coef_two.reshape(1, rows), in_hbm(transport_one), in_hbm(transport_two)
    )
    for substep in range(SUBSTEPS - 1):
        last, first, last32, first32 = call(
            edge_kernel, [(block, bf16), (block, bf16), (block, f32), (block, f32)], [smem()] + [vmem()] * 9, "edges"
        )(cols, in_vmem(left), in_vmem(right), value16, first32, last32, one, two, c1, c2)
        new_left = lax.ppermute(last, "dom", up)
        new_right = lax.ppermute(first, "dom", down)
        value16, value32 = call(
            inner_kernel, [(blocks, bf16), (blocks, f32)], [smem()] + [vmem()] * 10, "inner"
        )(cols, in_vmem(left), in_vmem(right), value16, value32, first, last, one, two, c1, c2)
        left, right = new_left, new_right
    (final,) = call(last_kernel, [(blocks, bf16)], [smem()] + [vmem()] * 10, "last")(
        cols, in_vmem(left), in_vmem(right), value16, value32, first32, last32, one, two, c1, c2
    )
    exchanged = lax.all_to_all(final, "comp", split_axis=0, concat_axis=0, tiled=True)
    return source_terms(exchanged.reshape(n * rows, width), quad_one, quad_two)


def solution(mesh):
    in_specs = (
        P("comp", "dom"),
        P("comp"),
        P("comp"),
        P("dom", None, None, None),
        P("dom", None, None, None),
        P("dom", None),
        P(),
        P(),
    )
    out_specs = P("dom", "comp", None)
    return jax.shard_map(
        per_device, mesh=mesh, in_specs=in_specs, out_specs=out_specs, check_vma=False
    )
```

time: 87.1 us -> 80.7 us (0.927)
  local copies, waits for them, and re-layouts: 4.8 us -> 1.32 us
  waiting for transfers between devices: 3.82 us -> 0.58 us
  Pallas kernels: 10.8 us -> 12.5 us
  other arithmetic: 1.21 us -> 0 us
    ppermute x1, waiting for transfers between devices: 3.3 us -> 0.01 us  [per_device(): left = lax.ppermute(last, 'dom', up)]
    ppermute x1, starting transfers between devices: 14.5 us -> 12.1 us  [per_device(): right = lax.ppermute(first, 'dom', down)]
    ppermute x1, starting transfers between devices: 1.92 us -> 4.28 us  [per_device(): left = lax.ppermute(last, 'dom', up)]
    unnamed x13 -> x10, local copies, waits for them, and re-layouts: 3.25 us -> 1.32 us
    pallas_call x1, Pallas kernels: 0.6 us -> 2.38 us  [per_device(): call(load_kernel, [(blocks, bf16), (blocks, f32), (block, f32), (block, f...]
    broadcast_in_dim x2 -> x0, local copies, waits for them, and re-layouts: 1.46 us -> none  [the longest x1 0.73 us: per_device(): c2 = in_vmem(jnp.broadcast_to(coef_two[:, None], block))]
    another operation x1 -> x0, other arithmetic: 1.21 us -> none
    pallas_call x1, Pallas kernels: 2.94 us -> 1.95 us  [source_terms(): pl.pallas_call(source_kernel, out_shape=jax.ShapeDtypeStruct((1, cells, c...]
  transfers between devices with their start and end apart: 8 -> 8, of which waited for: 4 -> 3; matrix products, arithmetic and copies ran while one was open for 1% -> 0% of each run, Pallas kernels for 5% -> 8%
where the time goes in v2:
time: 80.7 us; the launch traced here: 80.3 us
  starting transfers between devices  40.8 us (51%)
  blocking collectives  24.9 us (31%)
  Pallas kernels  12.5 us (15%)
  local copies, waits for them, and re-layouts  1.32 us (2%)
    all_to_all x1, blocking collectives, per_device(): lax.all_to_all(final, 'comp', split_axis=0, concat_axis=0, tiled=True)  24.9 us
    ppermute x3, starting transfers between devices, per_device(): new_right = lax.ppermute(first, 'dom', down)  18.7 us
    ppermute x1, starting transfers between devices, per_device(): right = lax.ppermute(first, 'dom', down)  12.1 us
    ppermute x3, starting transfers between devices, per_device(): new_left = lax.ppermute(last, 'dom', up)  5.76 us
    ppermute x1, starting transfers between devices, per_device(): left = lax.ppermute(last, 'dom', up)  4.28 us
    pallas_call x3, Pallas kernels, per_device(): call(inner_kernel, [(blocks, bf16), (blocks, f32)], [smem()] + [vmem()] *...  3.7 us
    pallas_call x1, Pallas kernels, per_device(): call(load_kernel, [(blocks, bf16), (blocks, f32), (block, f32), (block, f...  2.38 us
    pallas_call x3, Pallas kernels, per_device(): call(edge_kernel, [(block, bf16), (block, bf16), (block, f32), (block, f3...  2.33 us
  transfers between devices with their start and end apart: 8, of which 3 were waited for; matrix products, arithmetic and copies ran while one was open for 0% of the time, Pallas kernels for 8%

profile of v2, /device:TPU:8, one launch (start us, length us, event | category | flops | bytes accessed | tf_op | source)
XLA Modules:
  0.0 80.3 jit_solution(6127177162495047139)
XLA Ops:
  0.0 0.8 %begin.1 = (bf16[72,128]{1,0:T(8,128)(2,1)S(1)}, bf16[72,128]{1,0:T(8,128)(2,1)S(1)}) custom-call(f32[72,2048]{1,0:T(8,128)} %action_ref.3), custom_call_target="tpu_custom_call" | custom-call | tf_op jit(solution)/shard_map/begin/pallas_call | solution.py:212
  0.8 4.3 %collective-permute-start = (bf16[72,128]{1,0:T(8,128)(2,1)S(1)}, bf16[72,128]{1,0:T(8,128)(2,1)S(1)}, u32[]{:S(2)}, u32[]{:S(2)}) collective-permute-start(bf16[72,128]{1,0:T(8,128)(2,1)S(1)} %get-tuple-element.33), channel_id=1, source_target_pairs={{0,1},{1,2},{2,3},{3,4},{4,5},{5,6},{6,7},{7,8},{8,9},{9,10},{10,1... | collective-permute-start | bytes 55304 | tf_op jit(solution)/shard_map/ppermute | solution.py:219
  5.1 12.1 %collective-permute-start.1 = (bf16[72,128]{1,0:T(8,128)(2,1)S(1)}, bf16[72,128]{1,0:T(8,128)(2,1)S(1)}, u32[]{:S(2)}, u32[]{:S(2)}) collective-permute-start(bf16[72,128]{1,0:T(8,128)(2,1)S(1)} %get-tuple-element.34), channel_id=1, source_target_pairs={{1,0},{2,1},{3,2},{4,3},{5,4},{6,5},{7,6},{8,7},{9,8},{10,9},{11,1... | collective-permute-start | bytes 55304 | tf_op jit(solution)/shard_map/ppermute | solution.py:220
  17.2 0.6 copy-done.3
  17.9 0.7 copy-done.4
  18.5 2.4 %load.1 = (bf16[16,72,128]{2,1,0:T(8,128)(2,1)S(1)}, f32[16,72,128]{2,1,0:T(8,128)S(1)}, f32[72,128]{1,0:T(8,128)S(1)}, f32[72,128]{1,0:T(8,128)S(1)}, bf16[16,3...) custom-call(f32[72,2048]{1,0:T(8,128)} %action_ref.3, ...), custom_call_target="tpu_custom_call" | custom-call | tf_op jit(solution)/shard_map/load/pallas_call | solution.py:221
  21.0 0.8 edges.3
  21.7 1.9 %collective-permute-start.2 = (bf16[72,128]{1,0:T(8,128)(2,1)S(1)}, bf16[72,128]{1,0:T(8,128)(2,1)S(1)}, u32[]{:S(2)}, u32[]{:S(2)}) collective-permute-start(bf16[72,128]{1,0:T(8,128)(2,1)S(1)} %get-tuple-element.42.last16), channel_id=1, source_target_pairs={{0,1},{1,2},{2,3},{3,4},{4,5},{5,6},{6,7},{7,8},{8,9},{9,10},{10,1... | collective-permute-start | bytes 55304 | tf_op jit(solution)/shard_map/ppermute | solution.py:234
  23.7 6.0 %collective-permute-start.3 = (bf16[72,128]{1,0:T(8,128)(2,1)S(1)}, bf16[72,128]{1,0:T(8,128)(2,1)S(1)}, u32[]{:S(2)}, u32[]{:S(2)}) collective-permute-start(bf16[72,128]{1,0:T(8,128)(2,1)S(1)} %get-tuple-element.43.first16), channel_id=1, source_target_pairs={{1,0},{2,1},{3,2},{4,3},{5,4},{6,5},{7,6},{8,7},{9,8},{10,9},{11,1... | collective-permute-start | bytes 55304 | tf_op jit(solution)/shard_map/ppermute | solution.py:235
  29.7 1.2 %inner.3 = (bf16[16,72,128]{2,1,0:T(8,128)(2,1)S(1)}, f32[16,72,128]{2,1,0:T(8,128)S(1)}) custom-call(s32[3,16]{1,0:T(4,128)S(1)} %bitcast.6, bf16[72,128]{1,0:T(8,128)(2,1)S(1)} %collective-permute-done.left_ref, bf16[72,128]{1,0:T(8,128)(2,1)S(1)} %collective-permute-done.1.right_ref, bf16[16,72,128]{2,1,0:T(8,128)(2,1)S(1)} %get-tuple-element.35.blocks_ref, ...), custom_call_target="tpu_custom_call" | custom-call | tf_op jit(solution)/shard_map/inner/pallas_call | solution.py:236
  31.0 0.2 collective-permute-done.3.right_ref
  31.2 0.8 edges.4
  31.9 1.9 %collective-permute-start.4 = (bf16[72,128]{1,0:T(8,128)(2,1)S(1)}, bf16[72,128]{1,0:T(8,128)(2,1)S(1)}, u32[]{:S(2)}, u32[]{:S(2)}) collective-permute-start(bf16[72,128]{1,0:T(8,128)(2,1)S(1)} %get-tuple-element.48.last16), channel_id=1, source_target_pairs={{0,1},{1,2},{2,3},{3,4},{4,5},{5,6},{6,7},{7,8},{8,9},{9,10},{10,1... | collective-permute-start | bytes 55304 | tf_op jit(solution)/shard_map/ppermute | solution.py:234
  33.9 6.3 %collective-permute-start.5 = (bf16[72,128]{1,0:T(8,128)(2,1)S(1)}, bf16[72,128]{1,0:T(8,128)(2,1)S(1)}, u32[]{:S(2)}, u32[]{:S(2)}) collective-permute-start(bf16[72,128]{1,0:T(8,128)(2,1)S(1)} %get-tuple-element.49.first16), channel_id=1, source_target_pairs={{1,0},{2,1},{3,2},{4,3},{5,4},{6,5},{7,6},{8,7},{9,8},{10,9},{11,1... | collective-permute-start | bytes 55304 | tf_op jit(solution)/shard_map/ppermute | solution.py:235
  40.2 1.2 %inner.4 = (bf16[16,72,128]{2,1,0:T(8,128)(2,1)S(1)}, f32[16,72,128]{2,1,0:T(8,128)S(1)}) custom-call(s32[3,16]{1,0:T(4,128)S(1)} %bitcast.8, bf16[72,128]{1,0:T(8,128)(2,1)S(1)} %collective-permute-done.2.left_ref, bf16[72,128]{1,0:T(8,128)(2,1)S(1)} %collective-permute-done.3.right_ref, bf16[16,72,128]{2,1,0:T(8,128)(2,1)S(1)} %get-tuple-element.45.blocks_ref, ...), custom_call_target="tpu_custom_call" | custom-call | tf_op jit(solution)/shard_map/inner/pallas_call | solution.py:236
  41.4 0.2 collective-permute-done.5.right_ref
  41.6 0.8 edges.5
  42.4 1.9 %collective-permute-start.6 = (bf16[72,128]{1,0:T(8,128)(2,1)S(1)}, bf16[72,128]{1,0:T(8,128)(2,1)S(1)}, u32[]{:S(2)}, u32[]{:S(2)}) collective-permute-start(bf16[72,128]{1,0:T(8,128)(2,1)S(1)} %get-tuple-element.54.last16), channel_id=1, source_target_pairs={{0,1},{1,2},{2,3},{3,4},{4,5},{5,6},{6,7},{7,8},{8,9},{9,10},{10,1... | collective-permute-start | bytes 55304 | tf_op jit(solution)/shard_map/ppermute | solution.py:234
  44.3 6.3 %collective-permute-start.7 = (bf16[72,128]{1,0:T(8,128)(2,1)S(1)}, bf16[72,128]{1,0:T(8,128)(2,1)S(1)}, u32[]{:S(2)}, u32[]{:S(2)}) collective-permute-start(bf16[72,128]{1,0:T(8,128)(2,1)S(1)} %get-tuple-element.55.first16), channel_id=1, source_target_pairs={{1,0},{2,1},{3,2},{4,3},{5,4},{6,5},{7,6},{8,7},{9,8},{10,9},{11,1... | collective-permute-start | bytes 55304 | tf_op jit(solution)/shard_map/ppermute | solution.py:235
  50.7 1.2 %inner.5 = (bf16[16,72,128]{2,1,0:T(8,128)(2,1)S(1)}, f32[16,72,128]{2,1,0:T(8,128)S(1)}) custom-call(s32[3,16]{1,0:T(4,128)S(1)} %bitcast.10, bf16[72,128]{1,0:T(8,128)(2,1)S(1)} %collective-permute-done.4.left_ref, bf16[72,128]{1,0:T(8,128)(2,1)S(1)} %collective-permute-done.5.right_ref, bf16[16,72,128]{2,1,0:T(8,128)(2,1)S(1)} %get-tuple-element.51.blocks_ref, ...), custom_call_target="tpu_custom_call" | custom-call | tf_op jit(solution)/shard_map/inner/pallas_call | solution.py:236
  51.9 0.2 collective-permute-done.7.right_ref
  52.1 1.3 %last.1 = bf16[16,72,128]{2,1,0:T(8,128)(2,1)S(1)} custom-call(s32[3,16]{1,0:T(4,128)S(1)} %bitcast.11, bf16[72,128]{1,0:T(8,128)(2,1)S(1)} %collective-permute-done.6.left_ref, bf16[72,128]{1,0:T(8,128)(2,1)S(1)} %collective-permute-done.7.right_ref, bf16[16,72,128]{2,1,0:T(8,128)(2,1)S(1)} %get-tuple-element.57.blocks_ref, ...), custom_call_target="tpu_custom_call" | custom-call | tf_op jit(solution)/shard_map/last/pallas_call | solution.py:240
  53.4 24.9 %all_to_all.5 = bf16[16,72,128]{2,1,0:T(8,128)(2,1)S(1)} all-to-all(bf16[16,72,128]{2,1,0:T(8,128)(2,1)S(1)} %last.1), channel_id=1, replica_groups=mesh['comp'=16,'dom'=48] {'comp'}, dimensions={0} | all-to-all | bytes 589824 | tf_op jit(solution)/shard_map/all_to_all | solution.py:243
  78.3 2.0 %source_terms.1 = f32[1,128,1152]{2,1,0:T(8,128)} custom-call(bf16[1152,128]{1,0:T(8,128)(2,1)S(1)} %bitcast.4, bf16[1152,1152]{1,0:T(8,128)(2,1)S(1)} %copy-done, bf16[1152,1152]{1,0:T(8,128)(2,1)S(1)} %copy-done.1), custom_call_target="tpu_custom_call" | custom-call | tf_op jit(solution)/shard_map/source_terms/pallas_call | solution.py:186
  (13 shorter events, 0.0 us)
Async XLA Ops:
  0.8 20.1 %collective-permute-start = (bf16[72,128]{1,0:T(8,128)(2,1)S(1)}, bf16[72,128]{1,0:T(8,128)(2,1)S(1)}, u32[]{:S(2)}, u32[]{:S(2)}) collective-permute-start(bf16[72,128]{1,0:T(8,128)(2,1)S(1)} %get-tuple-element.33), channel_id=1, source_target_pairs={{0,1},{1,2},{2,3},{3,4},{4,5},{5,6},{6,7},{7,8},{8,9},{9,10},{10,1... | collective-permute-start | bytes 55304 | tf_op jit(solution)/shard_map/ppermute | solution.py:219
  5.1 15.8 %collective-permute-start.1 = (bf16[72,128]{1,0:T(8,128)(2,1)S(1)}, bf16[72,128]{1,0:T(8,128)(2,1)S(1)}, u32[]{:S(2)}, u32[]{:S(2)}) collective-permute-start(bf16[72,128]{1,0:T(8,128)(2,1)S(1)} %get-tuple-element.34), channel_id=1, source_target_pairs={{1,0},{2,1},{3,2},{4,3},{5,4},{6,5},{7,6},{8,7},{9,8},{10,9},{11,1... | collective-permute-start | bytes 55304 | tf_op jit(solution)/shard_map/ppermute | solution.py:220
  17.2 0.7 copy-start.3
  17.9 0.7 copy-start.4
  18.5 2.4 %copy-start.2 = (s32[16,3]{0,1:T(4,128)S(1)}, s32[16,3]{0,1:T(4,128)}, u32[]{:S(2)}) copy-start(s32[16,3]{0,1:T(4,128)} %param.13) | copy-start | bytes 580
  21.7 9.2 %collective-permute-start.2 = (bf16[72,128]{1,0:T(8,128)(2,1)S(1)}, bf16[72,128]{1,0:T(8,128)(2,1)S(1)}, u32[]{:S(2)}, u32[]{:S(2)}) collective-permute-start(bf16[72,128]{1,0:T(8,128)(2,1)S(1)} %get-tuple-element.42.last16), channel_id=1, source_target_pairs={{0,1},{1,2},{2,3},{3,4},{4,5},{5,6},{6,7},{7,8},{8,9},{9,10},{10,1... | collective-permute-start | bytes 55304 | tf_op jit(solution)/shard_map/ppermute | solution.py:234
  23.7 7.5 %collective-permute-start.3 = (bf16[72,128]{1,0:T(8,128)(2,1)S(1)}, bf16[72,128]{1,0:T(8,128)(2,1)S(1)}, u32[]{:S(2)}, u32[]{:S(2)}) collective-permute-start(bf16[72,128]{1,0:T(8,128)(2,1)S(1)} %get-tuple-element.43.first16), channel_id=1, source_target_pairs={{1,0},{2,1},{3,2},{4,3},{5,4},{6,5},{7,6},{8,7},{9,8},{10,9},{11,1... | collective-permute-start | bytes 55304 | tf_op jit(solution)/shard_map/ppermute | solution.py:235
  31.9 9.5 %collective-permute-start.4 = (bf16[72,128]{1,0:T(8,128)(2,1)S(1)}, bf16[72,128]{1,0:T(8,128)(2,1)S(1)}, u32[]{:S(2)}, u32[]{:S(2)}) collective-permute-start(bf16[72,128]{1,0:T(8,128)(2,1)S(1)} %get-tuple-element.48.last16), channel_id=1, source_target_pairs={{0,1},{1,2},{2,3},{3,4},{4,5},{5,6},{6,7},{7,8},{8,9},{9,10},{10,1... | collective-permute-start | bytes 55304 | tf_op jit(solution)/shard_map/ppermute | solution.py:234
  33.9 7.8 %collective-permute-start.5 = (bf16[72,128]{1,0:T(8,128)(2,1)S(1)}, bf16[72,128]{1,0:T(8,128)(2,1)S(1)}, u32[]{:S(2)}, u32[]{:S(2)}) collective-permute-start(bf16[72,128]{1,0:T(8,128)(2,1)S(1)} %get-tuple-element.49.first16), channel_id=1, source_target_pairs={{1,0},{2,1},{3,2},{4,3},{5,4},{6,5},{7,6},{8,7},{9,8},{10,9},{11,1... | collective-permute-start | bytes 55304 | tf_op jit(solution)/shard_map/ppermute | solution.py:235
  42.4 9.5 %collective-permute-start.6 = (bf16[72,128]{1,0:T(8,128)(2,1)S(1)}, bf16[72,128]{1,0:T(8,128)(2,1)S(1)}, u32[]{:S(2)}, u32[]{:S(2)}) collective-permute-start(bf16[72,128]{1,0:T(8,128)(2,1)S(1)} %get-tuple-element.54.last16), channel_id=1, source_target_pairs={{0,1},{1,2},{2,3},{3,4},{4,5},{5,6},{6,7},{7,8},{8,9},{9,10},{10,1... | collective-permute-start | bytes 55304 | tf_op jit(solution)/shard_map/ppermute | solution.py:234
  44.3 7.8 %collective-permute-start.7 = (bf16[72,128]{1,0:T(8,128)(2,1)S(1)}, bf16[72,128]{1,0:T(8,128)(2,1)S(1)}, u32[]{:S(2)}, u32[]{:S(2)}) collective-permute-start(bf16[72,128]{1,0:T(8,128)(2,1)S(1)} %get-tuple-element.55.first16), channel_id=1, source_target_pairs={{1,0},{2,1},{3,2},{4,3},{5,4},{6,5},{7,6},{8,7},{9,8},{10,9},{11,1... | collective-permute-start | bytes 55304 | tf_op jit(solution)/shard_map/ppermute | solution.py:235
  50.7 27.7 %copy-start.1 = (bf16[1152,1152]{1,0:T(8,128)(2,1)S(1)}, bf16[1152,1152]{1,0:T(8,128)(2,1)}, u32[]{:S(2)}) copy-start(bf16[1152,1152]{1,0:T(8,128)(2,1)} %two_ref.1) | copy-start | bytes 7962628
  52.1 26.2 %copy-start = (bf16[1152,1152]{1,0:T(8,128)(2,1)S(1)}, bf16[1152,1152]{1,0:T(8,128)(2,1)}, u32[]{:S(2)}) copy-start(bf16[1152,1152]{1,0:T(8,128)(2,1)} %one_ref.1) | copy-start | bytes 7962628

commit v3 on v2

--- a/solution.py
+++ b/solution.py
@@ -17,10 +17,6 @@
     return pltpu.with_memory_space_constraint(x, pltpu.HBM)
 
 
-def in_smem(x):
-    return pltpu.with_memory_space_constraint(x, pltpu.SMEM)
-
-
 def vmem():
     return pl.BlockSpec(memory_space=pltpu.VMEM)
 
@@ -36,9 +32,9 @@
 def call(body, outs, in_specs, name, scratch=(), limit=4 << 20):
     return pl.pallas_call(
         body,
-        out_shape=[pltpu.VMEM(s, d) for s, d in outs],
+        out_shape=[space(shape, dtype) for space, shape, dtype in outs],
         in_specs=in_specs,
-        out_specs=[vmem()] * len(outs),
+        out_specs=[smem() if space is pltpu.SMEM else vmem() for space, _, _ in outs],
         scratch_shapes=list(scratch),
         compiler_params=pltpu.CompilerParams(vmem_limit_bytes=limit),
         name=name,
@@ -139,28 +135,31 @@
         out[...] = buffers[i].astype(jnp.bfloat16)
 
 
-def load_kernel(action_ref, coef_one_ref, coef_two_ref, one_hbm, two_hbm, *refs):
-    out16, out32, first32, last32, one, two, c1, c2, sems = refs
+def load_kernel(action_ref, coef_one_hbm, coef_two_hbm, two_hbm, cols_hbm, *refs):
+    cols, out16, out32, first32, last32, two, c1, c2, coefs, sems = refs
     n, rows, width = out16.shape
-    copies = [
+    small = [
+        pltpu.make_async_copy(coef_one_hbm, coefs.at[0], sems.at[n]),
+        pltpu.make_async_copy(coef_two_hbm, coefs.at[1], sems.at[n + 1]),
+        pltpu.make_async_copy(cols_hbm, cols, sems.at[n + 2]),
+    ]
+    blocks = [
         pltpu.make_async_copy(action_ref.at[:, pl.ds(b * width, width)], out32.at[b], sems.at[b])
         for b in range(n)
     ]
-    weights = [
-        pltpu.make_async_copy(one_hbm, one, sems.at[n]),
-        pltpu.make_async_copy(two_hbm, two, sems.at[n + 1]),
-    ]
-    for copy in copies + weights:
+    weights = pltpu.make_async_copy(two_hbm, two, sems.at[n + 3])
+    for copy in small + blocks + [weights]:
         copy.start()
-    c1[...] = jnp.broadcast_to(coef_one_ref[...], (width, rows)).T
-    c2[...] = jnp.broadcast_to(coef_two_ref[...], (width, rows)).T
+    for copy in small:
+        copy.wait()
+    c1[...] = jnp.broadcast_to(coefs[0], (width, rows)).T
+    c2[...] = jnp.broadcast_to(coefs[1], (width, rows)).T
     for b in range(n):
-        copies[b].wait()
+        blocks[b].wait()
         out16[b] = out32[b].astype(jnp.bfloat16)
     first32[...] = out32[0]
     last32[...] = out32[n - 1]
-    for copy in weights:
-        copy.wait()
+    weights.wait()
 
 
 def source_kernel(cells_ref, one_ref, two_ref, out_hbm, buffers, sems):
@@ -208,36 +207,45 @@
     bf16, f32 = jnp.bfloat16, jnp.float32
     block, blocks, weights = (rows, width), (n, rows, width), (n, nnz, width, width)
 
-    cols = in_smem(block_cols.T)
+    vm = lambda shape, dtype: (pltpu.VMEM, shape, dtype)
     last, first = call(
         begin_kernel,
-        [(block, bf16), (block, bf16)],
+        [vm(block, bf16), vm(block, bf16)],
         [hbm()],
         "begin",
         [pltpu.VMEM((2, rows, width), f32), pltpu.SemaphoreType.DMA((2,))],
     )(in_hbm(action))
     left = lax.ppermute(last, "dom", up)
     right = lax.ppermute(first, "dom", down)
-    value16, value32, first32, last32, one, two, c1, c2 = call(
+    cols, value16, value32, first32, last32, two, c1, c2 = call(
         load_kernel,
-        [(blocks, bf16), (blocks, f32), (block, f32), (block, f32), (weights, bf16), (weights, bf16), (block, f32), (block, f32)],
-        [hbm(), vmem(), vmem(), hbm(), hbm()],
+        [(pltpu.SMEM, (nnz, n), jnp.int32), vm(blocks, bf16), vm(blocks, f32), vm(block, f32), vm(block, f32)]
+        + [vm(weights, bf16), vm(block, f32), vm(block, f32)],
+        [hbm()] * 5,
         "load",
-        [pltpu.SemaphoreType.DMA((n + 2,))],
+        [pltpu.VMEM((2, 1, rows), f32), pltpu.SemaphoreType.DMA((n + 4,))],
     )(
-        in_hbm(action), coef_one.reshape(1, rows), coef_two.reshape(1, rows), in_hbm(transport_one), in_hbm(transport_two)
-    )
+        in_hbm(action),
+        in_hbm(coef_one.reshape(1, rows)),
+        in_hbm(coef_two.reshape(1, rows)),
+        in_hbm(transport_two),
+        in_hbm(block_cols.T),
+    )
+    one = in_vmem(transport_one)
     for substep in range(SUBSTEPS - 1):
         last, first, last32, first32 = call(
-            edge_kernel, [(block, bf16), (block, bf16), (block, f32), (block, f32)], [smem()] + [vmem()] * 9, "edges"
+            edge_kernel,
+            [vm(block, bf16), vm(block, bf16), vm(block, f32), vm(block, f32)],
+            [smem()] + [vmem()] * 9,
+            "edges",
         )(cols, in_vmem(left), in_vmem(right), value16, first32, last32, one, two, c1, c2)
         new_left = lax.ppermute(last, "dom", up)
         new_right = lax.ppermute(first, "dom", down)
         value16, value32 = call(
-            inner_kernel, [(blocks, bf16), (blocks, f32)], [smem()] + [vmem()] * 10, "inner"
+            inner_kernel, [vm(blocks, bf16), vm(blocks, f32)], [smem()] + [vmem()] * 10, "inner"
         )(cols, in_vmem(left), in_vmem(right), value16, value32, first, last, one, two, c1, c2)
         left, right = new_left, new_right
-    (final,) = call(last_kernel, [(blocks, bf16)], [smem()] + [vmem()] * 10, "last")(
+    (final,) = call(last_kernel, [vm(blocks, bf16)], [smem()] + [vmem()] * 10, "last")(
         cols, in_vmem(left), in_vmem(right), value16, value32, first32, last32, one, two, c1, c2
     )
     exchanged = lax.all_to_all(final, "comp", split_axis=0, concat_axis=0, tiled=True)

time: 80.7 us -> 76.9 us (0.953)
  Pallas kernels: 12.5 us -> 8.29 us
  waiting for transfers between devices: 0.58 us -> 2.21 us
  local copies, waits for them, and re-layouts: 1.32 us -> 0.01 us
    pallas_call x9, Pallas kernels: 10.5 us -> 6.34 us  [the longest x3 2.07 us: per_device(): call(inner_kernel, [vm(blocks, bf16), vm(blocks, f32)], [smem()] + [vmem(...]
    ppermute x3, waiting for transfers between devices: 0.57 us -> 2.19 us  [per_device(): new_right = lax.ppermute(first, 'dom', down)]
    unnamed x10 -> x6, local copies, waits for them, and re-layouts: 1.32 us -> 0.01 us
  transfers between devices with their start and end apart: 8 -> 8, of which waited for: 3 -> 3; matrix products, arithmetic and copies ran while one was open for 0% -> 0% of each run, Pallas kernels for 8% -> 5%
where the time goes in v3:
time: 76.9 us; the launch traced here: 76.5 us
  starting transfers between devices  40.8 us (53%)
  blocking collectives  25 us (33%)
  Pallas kernels  8.29 us (11%)
  waiting for transfers between devices  2.21 us (3%)
    all_to_all x1, blocking collectives, per_device(): lax.all_to_all(final, 'comp', split_axis=0, concat_axis=0, tiled=True)  25 us
    ppermute x3, starting transfers between devices, per_device(): new_right = lax.ppermute(first, 'dom', down)  18.7 us
    ppermute x1, starting transfers between devices, per_device(): right = lax.ppermute(first, 'dom', down)  12.1 us
    ppermute x3, starting transfers between devices, per_device(): new_left = lax.ppermute(last, 'dom', up)  5.76 us
    ppermute x1, starting transfers between devices, per_device(): left = lax.ppermute(last, 'dom', up)  4.28 us
    ppermute x3, waiting for transfers between devices, per_device(): new_right = lax.ppermute(first, 'dom', down)  2.19 us
    pallas_call x3, Pallas kernels, per_device(): call(inner_kernel, [vm(blocks, bf16), vm(blocks, f32)], [smem()] + [vmem(...  2.07 us
    pallas_call x1, Pallas kernels, source_terms(): pl.pallas_call(source_kernel, out_shape=jax.ShapeDtypeStruct((1, cells, c...  1.95 us
  transfers between devices with their start and end apart: 8, of which 3 were waited for; matrix products, arithmetic and copies ran while one was open for 0% of the time, Pallas kernels for 5%

profile of v3, /device:TPU:8, one launch (start us, length us, event | category | flops | bytes accessed | tf_op | source)
XLA Modules:
  0.0 76.5 jit_solution(8240993866461224171)
XLA Ops:
  0.0 0.9 %begin.1 = (bf16[72,128]{1,0:T(8,128)(2,1)S(1)}, bf16[72,128]{1,0:T(8,128)(2,1)S(1)}) custom-call(f32[72,2048]{1,0:T(8,128)} %action_ref.3), custom_call_target="tpu_custom_call" | custom-call | tf_op jit(solution)/shard_map/begin/pallas_call | solution.py:211
  0.9 4.3 %collective-permute-start = (bf16[72,128]{1,0:T(8,128)(2,1)S(1)}, bf16[72,128]{1,0:T(8,128)(2,1)S(1)}, u32[]{:S(2)}, u32[]{:S(2)}) collective-permute-start(bf16[72,128]{1,0:T(8,128)(2,1)S(1)} %get-tuple-element.34), channel_id=1, source_target_pairs={{0,1},{1,2},{2,3},{3,4},{4,5},{5,6},{6,7},{7,8},{8,9},{9,10},{10,1... | collective-permute-start | bytes 55304 | tf_op jit(solution)/shard_map/ppermute | solution.py:218
  5.2 12.1 %collective-permute-start.1 = (bf16[72,128]{1,0:T(8,128)(2,1)S(1)}, bf16[72,128]{1,0:T(8,128)(2,1)S(1)}, u32[]{:S(2)}, u32[]{:S(2)}) collective-permute-start(bf16[72,128]{1,0:T(8,128)(2,1)S(1)} %get-tuple-element.35), channel_id=1, source_target_pairs={{1,0},{2,1},{3,2},{4,3},{5,4},{6,5},{7,6},{8,7},{9,8},{10,9},{11,1... | collective-permute-start | bytes 55304 | tf_op jit(solution)/shard_map/ppermute | solution.py:219
  17.3 1.9 %load.1 = (s32[3,16]{1,0:T(4,128)S(4)}, bf16[16,72,128]{2,1,0:T(8,128)(2,1)S(1)}, f32[16,72,128]{2,1,0:T(8,128)S(1)}, f32[72,128]{1,0:T(8,128)S(1)}, f32[72,128]...) custom-call(f32[72,2048]{1,0:T(8,128)} %action_ref.3, ...), custom_call_target="tpu_custom_call" | custom-call | tf_op jit(solution)/shard_map/load/pallas_call | solution.py:220
  19.3 0.0 collective-permute-done.left_ref
  19.3 0.2 edges.3
  19.6 1.9 %collective-permute-start.2 = (bf16[72,128]{1,0:T(8,128)(2,1)S(1)}, bf16[72,128]{1,0:T(8,128)(2,1)S(1)}, u32[]{:S(2)}, u32[]{:S(2)}) collective-permute-start(bf16[72,128]{1,0:T(8,128)(2,1)S(1)} %get-tuple-element.42.last16), channel_id=1, source_target_pairs={{0,1},{1,2},{2,3},{3,4},{4,5},{5,6},{6,7},{7,8},{8,9},{9,10},{10,1... | collective-permute-start | bytes 55304 | tf_op jit(solution)/shard_map/ppermute | solution.py:242
  21.5 6.0 %collective-permute-start.3 = (bf16[72,128]{1,0:T(8,128)(2,1)S(1)}, bf16[72,128]{1,0:T(8,128)(2,1)S(1)}, u32[]{:S(2)}, u32[]{:S(2)}) collective-permute-start(bf16[72,128]{1,0:T(8,128)(2,1)S(1)} %get-tuple-element.43.first16), channel_id=1, source_target_pairs={{1,0},{2,1},{3,2},{4,3},{5,4},{6,5},{7,6},{8,7},{9,8},{10,9},{11,1... | collective-permute-start | bytes 55304 | tf_op jit(solution)/shard_map/ppermute | solution.py:243
  27.5 0.7 inner.3
  28.2 0.7 collective-permute-done.3.right_ref
  29.0 0.2 edges.4
  29.2 1.9 %collective-permute-start.4 = (bf16[72,128]{1,0:T(8,128)(2,1)S(1)}, bf16[72,128]{1,0:T(8,128)(2,1)S(1)}, u32[]{:S(2)}, u32[]{:S(2)}) collective-permute-start(bf16[72,128]{1,0:T(8,128)(2,1)S(1)} %get-tuple-element.48.last16), channel_id=1, source_target_pairs={{0,1},{1,2},{2,3},{3,4},{4,5},{5,6},{6,7},{7,8},{8,9},{9,10},{10,1... | collective-permute-start | bytes 55304 | tf_op jit(solution)/shard_map/ppermute | solution.py:242
  31.1 6.3 %collective-permute-start.5 = (bf16[72,128]{1,0:T(8,128)(2,1)S(1)}, bf16[72,128]{1,0:T(8,128)(2,1)S(1)}, u32[]{:S(2)}, u32[]{:S(2)}) collective-permute-start(bf16[72,128]{1,0:T(8,128)(2,1)S(1)} %get-tuple-element.49.first16), channel_id=1, source_target_pairs={{1,0},{2,1},{3,2},{4,3},{5,4},{6,5},{7,6},{8,7},{9,8},{10,9},{11,1... | collective-permute-start | bytes 55304 | tf_op jit(solution)/shard_map/ppermute | solution.py:243
  37.4 0.7 inner.4
  38.1 0.7 collective-permute-done.5.right_ref
  38.9 0.2 edges.5
  39.1 1.9 %collective-permute-start.6 = (bf16[72,128]{1,0:T(8,128)(2,1)S(1)}, bf16[72,128]{1,0:T(8,128)(2,1)S(1)}, u32[]{:S(2)}, u32[]{:S(2)}) collective-permute-start(bf16[72,128]{1,0:T(8,128)(2,1)S(1)} %get-tuple-element.54.last16), channel_id=1, source_target_pairs={{0,1},{1,2},{2,3},{3,4},{4,5},{5,6},{6,7},{7,8},{8,9},{9,10},{10,1... | collective-permute-start | bytes 55304 | tf_op jit(solution)/shard_map/ppermute | solution.py:242
  41.0 6.3 %collective-permute-start.7 = (bf16[72,128]{1,0:T(8,128)(2,1)S(1)}, bf16[72,128]{1,0:T(8,128)(2,1)S(1)}, u32[]{:S(2)}, u32[]{:S(2)}) collective-permute-start(bf16[72,128]{1,0:T(8,128)(2,1)S(1)} %get-tuple-element.55.first16), channel_id=1, source_target_pairs={{1,0},{2,1},{3,2},{4,3},{5,4},{6,5},{7,6},{8,7},{9,8},{10,9},{11,1... | collective-permute-start | bytes 55304 | tf_op jit(solution)/shard_map/ppermute | solution.py:243
  47.3 0.0 copy-start.2
  47.4 0.7 inner.5
  48.1 0.7 collective-permute-done.7.right_ref
  48.8 0.8 last.1
  49.6 25.0 %all_to_all.5 = bf16[16,72,128]{2,1,0:T(8,128)(2,1)S(1)} all-to-all(bf16[16,72,128]{2,1,0:T(8,128)(2,1)S(1)} %last.1), channel_id=1, replica_groups=mesh['comp'=16,'dom'=48] {'comp'}, dimensions={0} | all-to-all | bytes 589824 | tf_op jit(solution)/shard_map/all_to_all | solution.py:251
  74.6 1.9 %source_terms.1 = f32[1,128,1152]{2,1,0:T(8,128)} custom-call(bf16[1152,128]{1,0:T(8,128)(2,1)S(1)} %bitcast.4, bf16[1152,1152]{1,0:T(8,128)(2,1)S(1)} %copy-done.1, bf16[1152,1152]{1,0:T(8,128)(2,1)S(1)} %copy-done.2), custom_call_target="tpu_custom_call" | custom-call | tf_op jit(solution)/shard_map/source_terms/pallas_call | solution.py:185
  (9 shorter events, 0.0 us)
Async XLA Ops:
  0.0 19.3 %copy-start = (bf16[16,3,128,128]{3,2,1,0:T(8,128)(2,1)S(1)}, bf16[16,3,128,128]{3,2,1,0:T(8,128)(2,1)}, u32[]{:S(2)}) copy-start(bf16[16,3,128,128]{3,2,1,0:T(8,128)(2,1)} %one_ref.14) | copy-start | bytes 4718596
  0.9 18.4 %collective-permute-start = (bf16[72,128]{1,0:T(8,128)(2,1)S(1)}, bf16[72,128]{1,0:T(8,128)(2,1)S(1)}, u32[]{:S(2)}, u32[]{:S(2)}) collective-permute-start(bf16[72,128]{1,0:T(8,128)(2,1)S(1)} %get-tuple-element.34), channel_id=1, source_target_pairs={{0,1},{1,2},{2,3},{3,4},{4,5},{5,6},{6,7},{7,8},{8,9},{9,10},{10,1... | collective-permute-start | bytes 55304 | tf_op jit(solution)/shard_map/ppermute | solution.py:218
  5.2 14.1 %collective-permute-start.1 = (bf16[72,128]{1,0:T(8,128)(2,1)S(1)}, bf16[72,128]{1,0:T(8,128)(2,1)S(1)}, u32[]{:S(2)}, u32[]{:S(2)}) collective-permute-start(bf16[72,128]{1,0:T(8,128)(2,1)S(1)} %get-tuple-element.35), channel_id=1, source_target_pairs={{1,0},{2,1},{3,2},{4,3},{5,4},{6,5},{7,6},{8,7},{9,8},{10,9},{11,1... | collective-permute-start | bytes 55304 | tf_op jit(solution)/shard_map/ppermute | solution.py:219
  19.6 8.7 %collective-permute-start.2 = (bf16[72,128]{1,0:T(8,128)(2,1)S(1)}, bf16[72,128]{1,0:T(8,128)(2,1)S(1)}, u32[]{:S(2)}, u32[]{:S(2)}) collective-permute-start(bf16[72,128]{1,0:T(8,128)(2,1)S(1)} %get-tuple-element.42.last16), channel_id=1, source_target_pairs={{0,1},{1,2},{2,3},{3,4},{4,5},{5,6},{6,7},{7,8},{8,9},{9,10},{10,1... | collective-permute-start | bytes 55304 | tf_op jit(solution)/shard_map/ppermute | solution.py:242
  21.5 7.5 %collective-permute-start.3 = (bf16[72,128]{1,0:T(8,128)(2,1)S(1)}, bf16[72,128]{1,0:T(8,128)(2,1)S(1)}, u32[]{:S(2)}, u32[]{:S(2)}) collective-permute-start(bf16[72,128]{1,0:T(8,128)(2,1)S(1)} %get-tuple-element.43.first16), channel_id=1, source_target_pairs={{1,0},{2,1},{3,2},{4,3},{5,4},{6,5},{7,6},{8,7},{9,8},{10,9},{11,1... | collective-permute-start | bytes 55304 | tf_op jit(solution)/shard_map/ppermute | solution.py:243
  29.2 8.9 %collective-permute-start.4 = (bf16[72,128]{1,0:T(8,128)(2,1)S(1)}, bf16[72,128]{1,0:T(8,128)(2,1)S(1)}, u32[]{:S(2)}, u32[]{:S(2)}) collective-permute-start(bf16[72,128]{1,0:T(8,128)(2,1)S(1)} %get-tuple-element.48.last16), channel_id=1, source_target_pairs={{0,1},{1,2},{2,3},{3,4},{4,5},{5,6},{6,7},{7,8},{8,9},{9,10},{10,1... | collective-permute-start | bytes 55304 | tf_op jit(solution)/shard_map/ppermute | solution.py:242
  31.1 7.8 %collective-permute-start.5 = (bf16[72,128]{1,0:T(8,128)(2,1)S(1)}, bf16[72,128]{1,0:T(8,128)(2,1)S(1)}, u32[]{:S(2)}, u32[]{:S(2)}) collective-permute-start(bf16[72,128]{1,0:T(8,128)(2,1)S(1)} %get-tuple-element.49.first16), channel_id=1, source_target_pairs={{1,0},{2,1},{3,2},{4,3},{5,4},{6,5},{7,6},{8,7},{9,8},{10,9},{11,1... | collective-permute-start | bytes 55304 | tf_op jit(solution)/shard_map/ppermute | solution.py:243
  39.1 9.0 %collective-permute-start.6 = (bf16[72,128]{1,0:T(8,128)(2,1)S(1)}, bf16[72,128]{1,0:T(8,128)(2,1)S(1)}, u32[]{:S(2)}, u32[]{:S(2)}) collective-permute-start(bf16[72,128]{1,0:T(8,128)(2,1)S(1)} %get-tuple-element.54.last16), channel_id=1, source_target_pairs={{0,1},{1,2},{2,3},{3,4},{4,5},{5,6},{6,7},{7,8},{8,9},{9,10},{10,1... | collective-permute-start | bytes 55304 | tf_op jit(solution)/shard_map/ppermute | solution.py:242
  41.0 7.8 %collective-permute-start.7 = (bf16[72,128]{1,0:T(8,128)(2,1)S(1)}, bf16[72,128]{1,0:T(8,128)(2,1)S(1)}, u32[]{:S(2)}, u32[]{:S(2)}) collective-permute-start(bf16[72,128]{1,0:T(8,128)(2,1)S(1)} %get-tuple-element.55.first16), channel_id=1, source_target_pairs={{1,0},{2,1},{3,2},{4,3},{5,4},{6,5},{7,6},{8,7},{9,8},{10,9},{11,1... | collective-permute-start | bytes 55304 | tf_op jit(solution)/shard_map/ppermute | solution.py:243
  47.3 27.2 %copy-start.2 = (bf16[1152,1152]{1,0:T(8,128)(2,1)S(1)}, bf16[1152,1152]{1,0:T(8,128)(2,1)}, u32[]{:S(2)}) copy-start(bf16[1152,1152]{1,0:T(8,128)(2,1)} %two_ref.1) | copy-start | bytes 7962628
  48.8 25.8 %copy-start.1 = (bf16[1152,1152]{1,0:T(8,128)(2,1)S(1)}, bf16[1152,1152]{1,0:T(8,128)(2,1)}, u32[]{:S(2)}) copy-start(bf16[1152,1152]{1,0:T(8,128)(2,1)} %one_ref.15) | copy-start | bytes 7962628

commit v4 on v3

--- a/solution.py
+++ b/solution.py
@@ -29,19 +29,20 @@
     return pl.BlockSpec(memory_space=pltpu.HBM)
 
 
-def call(body, outs, in_specs, name, scratch=(), limit=4 << 20):
+def call(body, outs, in_specs, name, scratch=(), limit=4 << 20, aliases={}):
     return pl.pallas_call(
         body,
         out_shape=[space(shape, dtype) for space, shape, dtype in outs],
         in_specs=in_specs,
         out_specs=[smem() if space is pltpu.SMEM else vmem() for space, _, _ in outs],
         scratch_shapes=list(scratch),
+        input_output_aliases=aliases,
         compiler_params=pltpu.CompilerParams(vmem_limit_bytes=limit),
         name=name,
     )
 
 
-def row_update(b, chosen, before, after, value, one, two, coef_one, coef_two):
+def row_update(chosen, before, after, value, one, two, coef_one, coef_two):
     width = value.shape[1]
     gathered = jnp.concatenate([chosen, before, after], axis=1)
     both = jnp.concatenate([one, two], axis=1)
@@ -63,7 +64,6 @@
     c1, c2 = c1_ref[...], c2_ref[...]
     for b, value_ref, out16, out32 in ((0, first_ref, first16, first32), (n - 1, last_ref, last16, last32)):
         new = row_update(
-            b,
             chosen_block(cols[0, b], left, right, blocks_ref),
             left if b == 0 else blocks_ref[b - 1],
             right if b == n - 1 else blocks_ref[b + 1],
@@ -86,7 +86,6 @@
     out16[n - 1] = last16[...]
     for b in range(1, n - 1):
         new = row_update(
-            b,
             chosen_block(cols[0, b], left, right, blocks_ref),
             blocks_ref[b - 1],
             blocks_ref[b + 1],
@@ -100,15 +99,30 @@
         out16[b] = new.astype(jnp.bfloat16)
 
 
-def last_kernel(cols, left_ref, right_ref, blocks_ref, field_ref, first_ref, last_ref, one_ref, two_ref, c1_ref, c2_ref, *outs):
-    (out16,) = outs
+def last_inner_kernel(cols, blocks_ref, field_ref, one_ref, two_ref, c1_ref, c2_ref, out16):
+    n, rows, width = blocks_ref.shape
+    c1, c2 = c1_ref[...], c2_ref[...]
+    for b in range(1, n - 1):
+        new = row_update(
+            blocks_ref[jnp.clip(cols[0, b] - 1, 0, n - 1)],
+            blocks_ref[b - 1],
+            blocks_ref[b + 1],
+            field_ref[b],
+            one_ref[b].reshape(-1, width),
+            two_ref[b].reshape(-1, width),
+            c1,
+            c2,
+        )
+        out16[b] = new.astype(jnp.bfloat16)
+
+
+def last_edge_kernel(cols, left_ref, right_ref, blocks_ref, field_ref, first_ref, last_ref, one_ref, two_ref, c1_ref, c2_ref, inner_ref, out16):
     n, rows, width = blocks_ref.shape
     left, right = left_ref[...], right_ref[...]
     c1, c2 = c1_ref[...], c2_ref[...]
-    for b in range(n):
-        value = first_ref[...] if b == 0 else last_ref[...] if b == n - 1 else field_ref[b]
-        new = row_update(
-            b,
+
+    def one_row(b, value):
+        new = row_update(
             chosen_block(cols[0, b], left, right, blocks_ref),
             left if b == 0 else blocks_ref[b - 1],
             right if b == n - 1 else blocks_ref[b + 1],
@@ -119,6 +133,13 @@
             c2,
         )
         out16[b] = new.astype(jnp.bfloat16)
+
+    one_row(0, first_ref[...])
+    one_row(n - 1, last_ref[...])
+    for b in range(1, n - 1):
+        @pl.when((cols[0, b] == 0) | (cols[0, b] == n + 1))
+        def _(b=b):
+            one_row(b, field_ref[b])
 
 
 def begin_kernel(action_ref, last16, first16, buffers, sems):
@@ -169,8 +190,9 @@
     for i in range(steps):
         at = slice(i * tile, (i + 1) * tile)
         own = cells[:, at].astype(jnp.float32)
-        first = jnp.dot(cells, one_ref[:, at], preferred_element_type=jnp.float32)
-        second = jnp.dot(cells, two_ref[:, at], preferred_element_type=jnp.float32)
+        quads = jnp.concatenate([one_ref[:, at], two_ref[:, at]], axis=1)
+        both = jnp.dot(cells, quads, preferred_element_type=jnp.float32)
+        first, second = both[:, :tile], both[:, tile:]
         buffers[i] = own + 0.5 * (first * own - second * own * own)
         copies.append(pltpu.make_async_copy(buffers.at[i], out_hbm.at[0, :, pl.ds(i * tile, tile)], sems.at[i]))
         copies[-1].start()
@@ -180,7 +202,7 @@
 
 def source_terms(exchanged, quad_one, quad_two):
     comps, cells = exchanged.shape
-    tile = 384
+    tile = 128
     steps = comps // tile
     return pl.pallas_call(
         source_kernel,
@@ -245,9 +267,12 @@
             inner_kernel, [vm(blocks, bf16), vm(blocks, f32)], [smem()] + [vmem()] * 10, "inner"
         )(cols, in_vmem(left), in_vmem(right), value16, value32, first, last, one, two, c1, c2)
         left, right = new_left, new_right
-    (final,) = call(last_kernel, [vm(blocks, bf16)], [smem()] + [vmem()] * 10, "last")(
-        cols, in_vmem(left), in_vmem(right), value16, value32, first32, last32, one, two, c1, c2
-    )
+    (final,) = call(last_inner_kernel, [vm(blocks, bf16)], [smem()] + [vmem()] * 6, "last_inner")(
+        cols, value16, value32, one, two, c1, c2
+    )
+    (final,) = call(
+        last_edge_kernel, [vm(blocks, bf16)], [smem()] + [vmem()] * 11, "last_edge", aliases={11: 0}
+    )(cols, in_vmem(left), in_vmem(right), value16, value32, first32, last32, one, two, c1, c2, final)
     exchanged = lax.all_to_all(final, "comp", split_axis=0, concat_axis=0, tiled=True)
     return source_terms(exchanged.reshape(n * rows, width), quad_one, quad_two)
 

time: 76.9 us -> 76.4 us (level)
  transfers between devices with their start and end apart: 8 -> 8, of which waited for: 3 -> 3; matrix products, arithmetic and copies ran while one was open for 0% -> 0% of each run, Pallas kernels for 5% -> 6%
where the time goes in v4:
time: 76.4 us; the launch traced here: 76.1 us
  starting transfers between devices  40.8 us (53%)
  blocking collectives  25.2 us (33%)
  Pallas kernels  8.39 us (11%)
  waiting for transfers between devices  1.57 us (2%)
    all_to_all x1, blocking collectives, per_device(): lax.all_to_all(final, 'comp', split_axis=0, concat_axis=0, tiled=True)  25.2 us
    ppermute x3, starting transfers between devices, per_device(): new_right = lax.ppermute(first, 'dom', down)  18.7 us
    ppermute x1, starting transfers between devices, per_device(): right = lax.ppermute(first, 'dom', down)  12.1 us
    ppermute x3, starting transfers between devices, per_device(): new_left = lax.ppermute(last, 'dom', up)  5.76 us
    ppermute x1, starting transfers between devices, per_device(): left = lax.ppermute(last, 'dom', up)  4.28 us
    pallas_call x3, Pallas kernels, per_device(): call(inner_kernel, [vm(blocks, bf16), vm(blocks, f32)], [smem()] + [vmem(...  2.05 us
    pallas_call x1, Pallas kernels, per_device(): call(load_kernel, [(pltpu.SMEM, (nnz, n), jnp.int32), vm(blocks, bf16), v...  1.95 us
    pallas_call x1, Pallas kernels, source_terms(): pl.pallas_call(source_kernel, out_shape=jax.ShapeDtypeStruct((1, cells, c...  1.68 us
  transfers between devices with their start and end apart: 8, of which 3 were waited for; matrix products, arithmetic and copies ran while one was open for 0% of the time, Pallas kernels for 6%

profile of v4, /device:TPU:8, one launch (start us, length us, event | category | flops | bytes accessed | tf_op | source)
XLA Modules:
  0.0 76.1 jit_solution(9886279126959672911)
XLA Ops:
  0.0 0.9 %begin.1 = (bf16[72,128]{1,0:T(8,128)(2,1)S(1)}, bf16[72,128]{1,0:T(8,128)(2,1)S(1)}) custom-call(f32[72,2048]{1,0:T(8,128)} %action_ref.3), custom_call_target="tpu_custom_call" | custom-call | tf_op jit(solution)/shard_map/begin/pallas_call | solution.py:233
  0.9 4.3 %collective-permute-start = (bf16[72,128]{1,0:T(8,128)(2,1)S(1)}, bf16[72,128]{1,0:T(8,128)(2,1)S(1)}, u32[]{:S(2)}, u32[]{:S(2)}) collective-permute-start(bf16[72,128]{1,0:T(8,128)(2,1)S(1)} %get-tuple-element.34), channel_id=1, source_target_pairs={{0,1},{1,2},{2,3},{3,4},{4,5},{5,6},{6,7},{7,8},{8,9},{9,10},{10,1... | collective-permute-start | bytes 55304 | tf_op jit(solution)/shard_map/ppermute | solution.py:240
  5.2 12.1 %collective-permute-start.1 = (bf16[72,128]{1,0:T(8,128)(2,1)S(1)}, bf16[72,128]{1,0:T(8,128)(2,1)S(1)}, u32[]{:S(2)}, u32[]{:S(2)}) collective-permute-start(bf16[72,128]{1,0:T(8,128)(2,1)S(1)} %get-tuple-element.35), channel_id=1, source_target_pairs={{1,0},{2,1},{3,2},{4,3},{5,4},{6,5},{7,6},{8,7},{9,8},{10,9},{11,1... | collective-permute-start | bytes 55304 | tf_op jit(solution)/shard_map/ppermute | solution.py:241
  17.3 1.9 %load.1 = (s32[3,16]{1,0:T(4,128)S(4)}, bf16[16,72,128]{2,1,0:T(8,128)(2,1)S(1)}, f32[16,72,128]{2,1,0:T(8,128)S(1)}, f32[72,128]{1,0:T(8,128)S(1)}, f32[72,128]...) custom-call(f32[72,2048]{1,0:T(8,128)} %action_ref.3, ...), custom_call_target="tpu_custom_call" | custom-call | tf_op jit(solution)/shard_map/load/pallas_call | solution.py:242
  19.3 0.0 collective-permute-done.1.right_ref
  19.3 0.2 edges.3
  19.6 1.9 %collective-permute-start.2 = (bf16[72,128]{1,0:T(8,128)(2,1)S(1)}, bf16[72,128]{1,0:T(8,128)(2,1)S(1)}, u32[]{:S(2)}, u32[]{:S(2)}) collective-permute-start(bf16[72,128]{1,0:T(8,128)(2,1)S(1)} %get-tuple-element.42.last16), channel_id=1, source_target_pairs={{0,1},{1,2},{2,3},{3,4},{4,5},{5,6},{6,7},{7,8},{8,9},{9,10},{10,1... | collective-permute-start | bytes 55304 | tf_op jit(solution)/shard_map/ppermute | solution.py:264
  21.5 6.0 %collective-permute-start.3 = (bf16[72,128]{1,0:T(8,128)(2,1)S(1)}, bf16[72,128]{1,0:T(8,128)(2,1)S(1)}, u32[]{:S(2)}, u32[]{:S(2)}) collective-permute-start(bf16[72,128]{1,0:T(8,128)(2,1)S(1)} %get-tuple-element.43.first16), channel_id=1, source_target_pairs={{1,0},{2,1},{3,2},{4,3},{5,4},{6,5},{7,6},{8,7},{9,8},{10,9},{11,1... | collective-permute-start | bytes 55304 | tf_op jit(solution)/shard_map/ppermute | solution.py:265
  27.5 0.7 inner.3
  28.2 0.7 collective-permute-done.3.right_ref
  29.0 0.2 edges.4
  29.2 1.9 %collective-permute-start.4 = (bf16[72,128]{1,0:T(8,128)(2,1)S(1)}, bf16[72,128]{1,0:T(8,128)(2,1)S(1)}, u32[]{:S(2)}, u32[]{:S(2)}) collective-permute-start(bf16[72,128]{1,0:T(8,128)(2,1)S(1)} %get-tuple-element.48.last16), channel_id=1, source_target_pairs={{0,1},{1,2},{2,3},{3,4},{4,5},{5,6},{6,7},{7,8},{8,9},{9,10},{10,1... | collective-permute-start | bytes 55304 | tf_op jit(solution)/shard_map/ppermute | solution.py:264
  31.1 6.3 %collective-permute-start.5 = (bf16[72,128]{1,0:T(8,128)(2,1)S(1)}, bf16[72,128]{1,0:T(8,128)(2,1)S(1)}, u32[]{:S(2)}, u32[]{:S(2)}) collective-permute-start(bf16[72,128]{1,0:T(8,128)(2,1)S(1)} %get-tuple-element.49.first16), channel_id=1, source_target_pairs={{1,0},{2,1},{3,2},{4,3},{5,4},{6,5},{7,6},{8,7},{9,8},{10,9},{11,1... | collective-permute-start | bytes 55304 | tf_op jit(solution)/shard_map/ppermute | solution.py:265
  37.4 0.7 inner.4
  38.1 0.7 collective-permute-done.5.right_ref
  38.9 0.2 edges.5
  39.1 1.9 %collective-permute-start.6 = (bf16[72,128]{1,0:T(8,128)(2,1)S(1)}, bf16[72,128]{1,0:T(8,128)(2,1)S(1)}, u32[]{:S(2)}, u32[]{:S(2)}) collective-permute-start(bf16[72,128]{1,0:T(8,128)(2,1)S(1)} %get-tuple-element.54.last16), channel_id=1, source_target_pairs={{0,1},{1,2},{2,3},{3,4},{4,5},{5,6},{6,7},{7,8},{8,9},{9,10},{10,1... | collective-permute-start | bytes 55304 | tf_op jit(solution)/shard_map/ppermute | solution.py:264
  41.0 6.3 %collective-permute-start.7 = (bf16[72,128]{1,0:T(8,128)(2,1)S(1)}, bf16[72,128]{1,0:T(8,128)(2,1)S(1)}, u32[]{:S(2)}, u32[]{:S(2)}) collective-permute-start(bf16[72,128]{1,0:T(8,128)(2,1)S(1)} %get-tuple-element.55.first16), channel_id=1, source_target_pairs={{1,0},{2,1},{3,2},{4,3},{5,4},{6,5},{7,6},{8,7},{9,8},{10,9},{11,1... | collective-permute-start | bytes 55304 | tf_op jit(solution)/shard_map/ppermute | solution.py:265
  47.3 0.7 inner.5
  48.0 0.7 last_inner.1.inner_ref
  48.7 0.1 collective-permute-done.7.right_ref
  48.8 0.5 last_edge.1
  49.3 25.2 %all_to_all.5 = bf16[16,72,128]{2,1,0:T(8,128)(2,1)S(1)} all-to-all(bf16[16,72,128]{2,1,0:T(8,128)(2,1)S(1)} %last_edge.1), channel_id=1, replica_groups=mesh['comp'=16,'dom'=48] {'comp'}, dimensions={0} | all-to-all | bytes 589824 | tf_op jit(solution)/shard_map/all_to_all | solution.py:276
  74.5 1.7 %source_terms.1 = f32[1,128,1152]{2,1,0:T(8,128)} custom-call(bf16[1152,128]{1,0:T(8,128)(2,1)S(1)} %bitcast.4, bf16[1152,1152]{1,0:T(8,128)(2,1)S(1)} %copy-done.1, bf16[1152,1152]{1,0:T(8,128)(2,1)S(1)} %copy-done.2), custom_call_target="tpu_custom_call" | custom-call | tf_op jit(solution)/shard_map/source_terms/pallas_call | solution.py:207
  (10 shorter events, 0.0 us)
Async XLA Ops:
  0.0 19.3 %copy-start = (bf16[16,3,128,128]{3,2,1,0:T(8,128)(2,1)S(1)}, bf16[16,3,128,128]{3,2,1,0:T(8,128)(2,1)}, u32[]{:S(2)}) copy-start(bf16[16,3,128,128]{3,2,1,0:T(8,128)(2,1)} %one_ref.16) | copy-start | bytes 4718596
  0.9 18.4 %collective-permute-start = (bf16[72,128]{1,0:T(8,128)(2,1)S(1)}, bf16[72,128]{1,0:T(8,128)(2,1)S(1)}, u32[]{:S(2)}, u32[]{:S(2)}) collective-permute-start(bf16[72,128]{1,0:T(8,128)(2,1)S(1)} %get-tuple-element.34), channel_id=1, source_target_pairs={{0,1},{1,2},{2,3},{3,4},{4,5},{5,6},{6,7},{7,8},{8,9},{9,10},{10,1... | collective-permute-start | bytes 55304 | tf_op jit(solution)/shard_map/ppermute | solution.py:240
  5.2 14.1 %collective-permute-start.1 = (bf16[72,128]{1,0:T(8,128)(2,1)S(1)}, bf16[72,128]{1,0:T(8,128)(2,1)S(1)}, u32[]{:S(2)}, u32[]{:S(2)}) collective-permute-start(bf16[72,128]{1,0:T(8,128)(2,1)S(1)} %get-tuple-element.35), channel_id=1, source_target_pairs={{1,0},{2,1},{3,2},{4,3},{5,4},{6,5},{7,6},{8,7},{9,8},{10,9},{11,1... | collective-permute-start | bytes 55304 | tf_op jit(solution)/shard_map/ppermute | solution.py:241
  19.6 8.7 %collective-permute-start.2 = (bf16[72,128]{1,0:T(8,128)(2,1)S(1)}, bf16[72,128]{1,0:T(8,128)(2,1)S(1)}, u32[]{:S(2)}, u32[]{:S(2)}) collective-permute-start(bf16[72,128]{1,0:T(8,128)(2,1)S(1)} %get-tuple-element.42.last16), channel_id=1, source_target_pairs={{0,1},{1,2},{2,3},{3,4},{4,5},{5,6},{6,7},{7,8},{8,9},{9,10},{10,1... | collective-permute-start | bytes 55304 | tf_op jit(solution)/shard_map/ppermute | solution.py:264
  21.5 7.5 %collective-permute-start.3 = (bf16[72,128]{1,0:T(8,128)(2,1)S(1)}, bf16[72,128]{1,0:T(8,128)(2,1)S(1)}, u32[]{:S(2)}, u32[]{:S(2)}) collective-permute-start(bf16[72,128]{1,0:T(8,128)(2,1)S(1)} %get-tuple-element.43.first16), channel_id=1, source_target_pairs={{1,0},{2,1},{3,2},{4,3},{5,4},{6,5},{7,6},{8,7},{9,8},{10,9},{11,1... | collective-permute-start | bytes 55304 | tf_op jit(solution)/shard_map/ppermute | solution.py:265
  29.2 9.0 %collective-permute-start.4 = (bf16[72,128]{1,0:T(8,128)(2,1)S(1)}, bf16[72,128]{1,0:T(8,128)(2,1)S(1)}, u32[]{:S(2)}, u32[]{:S(2)}) collective-permute-start(bf16[72,128]{1,0:T(8,128)(2,1)S(1)} %get-tuple-element.48.last16), channel_id=1, source_target_pairs={{0,1},{1,2},{2,3},{3,4},{4,5},{5,6},{6,7},{7,8},{8,9},{9,10},{10,1... | collective-permute-start | bytes 55304 | tf_op jit(solution)/shard_map/ppermute | solution.py:264
  31.1 7.8 %collective-permute-start.5 = (bf16[72,128]{1,0:T(8,128)(2,1)S(1)}, bf16[72,128]{1,0:T(8,128)(2,1)S(1)}, u32[]{:S(2)}, u32[]{:S(2)}) collective-permute-start(bf16[72,128]{1,0:T(8,128)(2,1)S(1)} %get-tuple-element.49.first16), channel_id=1, source_target_pairs={{1,0},{2,1},{3,2},{4,3},{5,4},{6,5},{7,6},{8,7},{9,8},{10,9},{11,1... | collective-permute-start | bytes 55304 | tf_op jit(solution)/shard_map/ppermute | solution.py:265
  39.1 9.6 %collective-permute-start.6 = (bf16[72,128]{1,0:T(8,128)(2,1)S(1)}, bf16[72,128]{1,0:T(8,128)(2,1)S(1)}, u32[]{:S(2)}, u32[]{:S(2)}) collective-permute-start(bf16[72,128]{1,0:T(8,128)(2,1)S(1)} %get-tuple-element.54.last16), channel_id=1, source_target_pairs={{0,1},{1,2},{2,3},{3,4},{4,5},{5,6},{6,7},{7,8},{8,9},{9,10},{10,1... | collective-permute-start | bytes 55304 | tf_op jit(solution)/shard_map/ppermute | solution.py:264
  41.0 7.8 %collective-permute-start.7 = (bf16[72,128]{1,0:T(8,128)(2,1)S(1)}, bf16[72,128]{1,0:T(8,128)(2,1)S(1)}, u32[]{:S(2)}, u32[]{:S(2)}) collective-permute-start(bf16[72,128]{1,0:T(8,128)(2,1)S(1)} %get-tuple-element.55.first16), channel_id=1, source_target_pairs={{1,0},{2,1},{3,2},{4,3},{5,4},{6,5},{7,6},{8,7},{9,8},{10,9},{11,1... | collective-permute-start | bytes 55304 | tf_op jit(solution)/shard_map/ppermute | solution.py:265
  48.8 25.7 %copy-start.1 = (bf16[1152,1152]{1,0:T(8,128)(2,1)S(1)}, bf16[1152,1152]{1,0:T(8,128)(2,1)}, u32[]{:S(2)}) copy-start(bf16[1152,1152]{1,0:T(8,128)(2,1)} %one_ref.17) | copy-start | bytes 7962628
  48.8 25.7 %copy-start.2 = (bf16[1152,1152]{1,0:T(8,128)(2,1)S(1)}, bf16[1152,1152]{1,0:T(8,128)(2,1)}, u32[]{:S(2)}) copy-start(bf16[1152,1152]{1,0:T(8,128)(2,1)} %two_ref.1) | copy-start | bytes 7962628

commit v5 on v4

--- a/solution.py
+++ b/solution.py
@@ -7,6 +7,8 @@
 
 SUBSTEPS = 4
 KEEP = 0.25
+CHAIN = 12
+ROUND = 3
 
 
 def in_vmem(x):
@@ -51,39 +53,83 @@
     return jnp.maximum(moved, KEEP * value)
 
 
+def exchange_of(edge):
+    place = edge % CHAIN
+    return jnp.where(place == CHAIN - 1, 1, jnp.where(place == CHAIN - 2, 2, place % 2))
+
+
+def pairs_of(exchange, dom):
+    def carries(edge):
+        place = edge % CHAIN
+        return (1 if place == CHAIN - 1 else 2 if place == CHAIN - 2 else place % 2) == exchange
+
+    edges = [d for d in range(dom - 1) if carries(d)]
+    return [p for d in edges for p in ((d, d + 1), (d + 1, d))]
+
+
+def sides():
+    own = lax.axis_index("dom")
+    return exchange_of(own + CHAIN - 1), exchange_of(own)
+
+
+def pick(which, parts):
+    return jnp.where(which == 0, parts[0], jnp.where(which == 1, parts[1], parts[2]))
+
+
+def halos(received):
+    parts = [r[...] for r in received]
+    to_left, to_right = sides()
+    return pick(to_left, parts), pick(to_right, parts)
+
+
+def send(outs, first, last):
+    to_left, _ = sides()
+    for exchange, out in enumerate(outs):
+        out[...] = jnp.where(to_left == exchange, first, last)
+
+
 def chosen_block(e, left, right, blocks_ref):
     n = blocks_ref.shape[0]
     inner = blocks_ref[jnp.clip(e - 1, 0, n - 1)]
     return jnp.where(e == 0, left, jnp.where(e == n + 1, right, inner))
 
 
-def edge_kernel(cols, left_ref, right_ref, blocks_ref, first_ref, last_ref, one_ref, two_ref, c1_ref, c2_ref, *outs):
-    last16, first16, last32, first32 = outs
+def edge_rows(cols, left, right, blocks_ref, first, last, one_ref, two_ref, c1, c2):
     n, rows, width = blocks_ref.shape
-    left, right = left_ref[...], right_ref[...]
-    c1, c2 = c1_ref[...], c2_ref[...]
-    for b, value_ref, out16, out32 in ((0, first_ref, first16, first32), (n - 1, last_ref, last16, last32)):
-        new = row_update(
+    return [
+        row_update(
             chosen_block(cols[0, b], left, right, blocks_ref),
             left if b == 0 else blocks_ref[b - 1],
             right if b == n - 1 else blocks_ref[b + 1],
-            value_ref[...],
+            value,
             one_ref[b].reshape(-1, width),
             two_ref[b].reshape(-1, width),
             c1,
             c2,
         )
-        out32[...] = new
-        out16[...] = new.astype(jnp.bfloat16)
-
-
-def inner_kernel(cols, left_ref, right_ref, blocks_ref, field_ref, first16, last16, one_ref, two_ref, c1_ref, c2_ref, *outs):
+        for b, value in ((0, first), (n - 1, last))
+    ]
+
+
+def edge_kernel(cols, in0, in1, in2, blocks_ref, ends_ref, one_ref, two_ref, c1_ref, c2_ref, *outs):
+    out0, out1, out2, ends16, ends32 = outs
+    left, right = halos((in0, in1, in2))
+    first, last = edge_rows(
+        cols, left, right, blocks_ref, ends_ref[0], ends_ref[1], one_ref, two_ref, c1_ref[...], c2_ref[...]
+    )
+    ends32[0], ends32[1] = first, last
+    first, last = first.astype(jnp.bfloat16), last.astype(jnp.bfloat16)
+    ends16[0], ends16[1] = first, last
+    send((out0, out1, out2), first, last)
+
+
+def inner_kernel(cols, in0, in1, in2, blocks_ref, field_ref, ends16, one_ref, two_ref, c1_ref, c2_ref, *outs):
     out16, out32 = outs
     n, rows, width = blocks_ref.shape
-    left, right = left_ref[...], right_ref[...]
+    left, right = halos((in0, in1, in2))
     c1, c2 = c1_ref[...], c2_ref[...]
-    out16[0] = first16[...]
-    out16[n - 1] = last16[...]
+    out16[0] = ends16[0]
+    out16[n - 1] = ends16[1]
     for b in range(1, n - 1):
         new = row_update(
             chosen_block(cols[0, b], left, right, blocks_ref),
@@ -116,53 +162,62 @@
         out16[b] = new.astype(jnp.bfloat16)
 
 
-def last_edge_kernel(cols, left_ref, right_ref, blocks_ref, field_ref, first_ref, last_ref, one_ref, two_ref, c1_ref, c2_ref, inner_ref, out16):
+def last_edge_kernel(cols, todo, in0, in1, in2, blocks_ref, field_ref, ends_ref, one_ref, two_ref, c1_ref, c2_ref, inner_ref, out16):
     n, rows, width = blocks_ref.shape
-    left, right = left_ref[...], right_ref[...]
+    left, right = halos((in0, in1, in2))
     c1, c2 = c1_ref[...], c2_ref[...]
 
-    def one_row(b, value):
-        new = row_update(
+    def again(b):
+        return row_update(
             chosen_block(cols[0, b], left, right, blocks_ref),
-            left if b == 0 else blocks_ref[b - 1],
-            right if b == n - 1 else blocks_ref[b + 1],
-            value,
+            blocks_ref[b - 1],
+            blocks_ref[b + 1],
+            field_ref[b],
             one_ref[b].reshape(-1, width),
             two_ref[b].reshape(-1, width),
             c1,
             c2,
-        )
-        out16[b] = new.astype(jnp.bfloat16)
-
-    one_row(0, first_ref[...])
-    one_row(n - 1, last_ref[...])
-    for b in range(1, n - 1):
-        @pl.when((cols[0, b] == 0) | (cols[0, b] == n + 1))
-        def _(b=b):
-            one_row(b, field_ref[b])
-
-
-def begin_kernel(action_ref, last16, first16, buffers, sems):
-    width = first16.shape[1]
+        ).astype(jnp.bfloat16)
+
+    first, last = edge_rows(
+        cols, left, right, blocks_ref, ends_ref[0], ends_ref[1], one_ref, two_ref, c1, c2
+    )
+    at = [todo[0, i] for i in range(ROUND)]
+    new = [again(b) for b in at]
+    out16[0] = first.astype(jnp.bfloat16)
+    out16[n - 1] = last.astype(jnp.bfloat16)
+    for b, value in zip(at, new):
+        out16[b] = value
+
+    @pl.when(todo[0, n - 1] > ROUND)
+    def _():
+        @pl.loop(ROUND, todo[0, n - 1])
+        def _(i):
+            b = todo[0, i]
+            out16[b] = again(b)
+
+
+def begin_kernel(action_ref, out0, out1, out2, buffers, sems):
+    width = out0.shape[1]
     cells = action_ref.shape[1]
     copies = [
-        pltpu.make_async_copy(action_ref.at[:, pl.ds(cells - width, width)], buffers.at[0], sems.at[0]),
-        pltpu.make_async_copy(action_ref.at[:, pl.ds(0, width)], buffers.at[1], sems.at[1]),
+        pltpu.make_async_copy(action_ref.at[:, pl.ds(at, width)], buffers.at[i], sems.at[i])
+        for i, at in enumerate((0, cells - width))
     ]
     for copy in copies:
         copy.start()
-    for copy, out, i in zip(copies, (last16, first16), (0, 1)):
+    for copy in copies:
         copy.wait()
-        out[...] = buffers[i].astype(jnp.bfloat16)
+    send((out0, out1, out2), buffers[0].astype(jnp.bfloat16), buffers[1].astype(jnp.bfloat16))
 
 
 def load_kernel(action_ref, coef_one_hbm, coef_two_hbm, two_hbm, cols_hbm, *refs):
-    cols, out16, out32, first32, last32, two, c1, c2, coefs, sems = refs
+    cols, todo, out16, out32, ends32, two, c1, c2, coefs, sems = refs
     n, rows, width = out16.shape
     small = [
+        pltpu.make_async_copy(cols_hbm, cols, sems.at[n + 2]),
         pltpu.make_async_copy(coef_one_hbm, coefs.at[0], sems.at[n]),
         pltpu.make_async_copy(coef_two_hbm, coefs.at[1], sems.at[n + 1]),
-        pltpu.make_async_copy(cols_hbm, cols, sems.at[n + 2]),
     ]
     blocks = [
         pltpu.make_async_copy(action_ref.at[:, pl.ds(b * width, width)], out32.at[b], sems.at[b])
@@ -173,13 +228,26 @@
         copy.start()
     for copy in small:
         copy.wait()
+    for i in range(n):
+        todo[0, i] = 1
+    count = jnp.int32(0)
+    for b in range(1, n - 1):
+        e = cols[0, b]
+        reads_halo = (e == 0) | (e == n + 1)
+
+        @pl.when(reads_halo)
+        def _(b=b, count=count):
+            todo[0, count] = b
+
+        count = count + reads_halo.astype(jnp.int32)
+    todo[0, n - 1] = count
     c1[...] = jnp.broadcast_to(coefs[0], (width, rows)).T
     c2[...] = jnp.broadcast_to(coefs[1], (width, rows)).T
     for b in range(n):
         blocks[b].wait()
         out16[b] = out32[b].astype(jnp.bfloat16)
-    first32[...] = out32[0]
-    last32[...] = out32[n - 1]
+    ends32[0] = out32[0]
+    ends32[1] = out32[n - 1]
     weights.wait()
 
 
@@ -224,24 +292,26 @@
     rows, cells_dev = action.shape
     n, nnz, width, _ = transport_one.shape
     dom = lax.axis_size("dom")
-    up = [(i, i + 1) for i in range(dom - 1)]
-    down = [(i + 1, i) for i in range(dom - 1)]
     bf16, f32 = jnp.bfloat16, jnp.float32
-    block, blocks, weights = (rows, width), (n, rows, width), (n, nnz, width, width)
-
+    block, blocks, ends, weights = (rows, width), (n, rows, width), (2, rows, width), (n, nnz, width, width)
     vm = lambda shape, dtype: (pltpu.VMEM, shape, dtype)
-    last, first = call(
-        begin_kernel,
-        [vm(block, bf16), vm(block, bf16)],
-        [hbm()],
-        "begin",
-        [pltpu.VMEM((2, rows, width), f32), pltpu.SemaphoreType.DMA((2,))],
-    )(in_hbm(action))
-    left = lax.ppermute(last, "dom", up)
-    right = lax.ppermute(first, "dom", down)
-    cols, value16, value32, first32, last32, two, c1, c2 = call(
+    sm = lambda shape: (pltpu.SMEM, shape, jnp.int32)
+    exchange = lambda parts: [
+        in_vmem(lax.ppermute(x, "dom", pairs_of(i, dom))) for i, x in enumerate(parts)
+    ]
+
+    received = exchange(
+        call(
+            begin_kernel,
+            [vm(block, bf16)] * 3,
+            [hbm()],
+            "begin",
+            [pltpu.VMEM((2, rows, width), f32), pltpu.SemaphoreType.DMA((2,))],
+        )(in_hbm(action))
+    )
+    cols, todo, value16, value32, ends32, two, c1, c2 = call(
         load_kernel,
-        [(pltpu.SMEM, (nnz, n), jnp.int32), vm(blocks, bf16), vm(blocks, f32), vm(block, f32), vm(block, f32)]
+        [sm((nnz, n)), sm((1, n)), vm(blocks, bf16), vm(blocks, f32), vm(ends, f32)]
         + [vm(weights, bf16), vm(block, f32), vm(block, f32)],
         [hbm()] * 5,
         "load",
@@ -255,24 +325,23 @@
     )
     one = in_vmem(transport_one)
     for substep in range(SUBSTEPS - 1):
-        last, first, last32, first32 = call(
+        *parts, ends16, ends32 = call(
             edge_kernel,
-            [vm(block, bf16), vm(block, bf16), vm(block, f32), vm(block, f32)],
+            [vm(block, bf16)] * 3 + [vm(ends, bf16), vm(ends, f32)],
             [smem()] + [vmem()] * 9,
             "edges",
-        )(cols, in_vmem(left), in_vmem(right), value16, first32, last32, one, two, c1, c2)
-        new_left = lax.ppermute(last, "dom", up)
-        new_right = lax.ppermute(first, "dom", down)
+        )(cols, *received, value16, ends32, one, two, c1, c2)
+        new_received = exchange(parts)
         value16, value32 = call(
             inner_kernel, [vm(blocks, bf16), vm(blocks, f32)], [smem()] + [vmem()] * 10, "inner"
-        )(cols, in_vmem(left), in_vmem(right), value16, value32, first, last, one, two, c1, c2)
-        left, right = new_left, new_right
+        )(cols, *received, value16, value32, ends16, one, two, c1, c2)
+        received = new_received
     (final,) = call(last_inner_kernel, [vm(blocks, bf16)], [smem()] + [vmem()] * 6, "last_inner")(
         cols, value16, value32, one, two, c1, c2
     )
     (final,) = call(
-        last_edge_kernel, [vm(blocks, bf16)], [smem()] + [vmem()] * 11, "last_edge", aliases={11: 0}
-    )(cols, in_vmem(left), in_vmem(right), value16, value32, first32, last32, one, two, c1, c2, final)
+        last_edge_kernel, [vm(blocks, bf16)], [smem()] * 2 + [vmem()] * 11, "last_edge", aliases={12: 0}
+    )(cols, todo, *received, value16, value32, ends32, one, two, c1, c2, final)
     exchanged = lax.all_to_all(final, "comp", split_axis=0, concat_axis=0, tiled=True)
     return source_terms(exchanged.reshape(n * rows, width), quad_one, quad_two)
 

time: 76.4 us -> 76.1 us (level)
  starting transfers between devices: 40.8 us -> 38 us
  waiting for transfers between devices: 1.57 us -> 3.98 us
    ppermute x8 -> x12, starting transfers between devices: 40.8 us -> 38 us  [per_device(): lax.ppermute(x, 'dom', pairs_of(i, dom))]
    ppermute x8 -> x12, waiting for transfers between devices: 1.57 us -> 3.98 us  [per_device(): lax.ppermute(x, 'dom', pairs_of(i, dom))]
  transfers between devices with their start and end apart: 8 -> 12, of which waited for: 3 -> 3; matrix products, arithmetic and copies ran while one was open for 0% -> 0% of each run, Pallas kernels for 6% -> 6%
where the time goes in v5:
time: 76.1 us; the launch traced here: 75.7 us
  starting transfers between devices  38 us (50%)
  blocking collectives  25.2 us (33%)
  Pallas kernels  8.34 us (11%)
  waiting for transfers between devices  3.98 us (5%)
    ppermute x12, starting transfers between devices, per_device(): lax.ppermute(x, 'dom', pairs_of(i, dom))  38 us
    all_to_all x1, blocking collectives, per_device(): lax.all_to_all(final, 'comp', split_axis=0, concat_axis=0, tiled=True)  25.2 us
    ppermute x12, waiting for transfers between devices, per_device(): lax.ppermute(x, 'dom', pairs_of(i, dom))  3.98 us
    pallas_call x3, Pallas kernels, per_device(): call(inner_kernel, [vm(blocks, bf16), vm(blocks, f32)], [smem()] + [vmem(...  2.12 us
    pallas_call x1, Pallas kernels, per_device(): call(load_kernel, [sm((nnz, n)), sm((1, n)), vm(blocks, bf16), vm(blocks,...  1.95 us
    pallas_call x1, Pallas kernels, source_terms(): pl.pallas_call(source_kernel, out_shape=jax.ShapeDtypeStruct((1, cells, c...  1.68 us
  transfers between devices with their start and end apart: 12, of which 3 were waited for; matrix products, arithmetic and copies ran while one was open for 0% of the time, Pallas kernels for 6%

profile of v5, /device:TPU:8, one launch (start us, length us, event | category | flops | bytes accessed | tf_op | source)
XLA Modules:
  0.0 75.7 jit_solution(16279275128122940477)
XLA Ops:
  0.0 0.9 %begin.1 = (bf16[72,128]{1,0:T(8,128)(2,1)S(1)}, bf16[72,128]{1,0:T(8,128)(2,1)S(1)}, bf16[72,128]{1,0:T(8,128)(2,1)S(1)}) custom-call(f32[72,2048]{1,0:T(8,128)} %action_ref.3), custom_call_target="tpu_custom_call" | custom-call | tf_op jit(solution)/shard_map/begin/pallas_call | solution.py:304
  0.9 4.3 %collective-permute-start = (bf16[72,128]{1,0:T(8,128)(2,1)S(1)}, bf16[72,128]{1,0:T(8,128)(2,1)S(1)}, u32[]{:S(2)}, u32[]{:S(2)}) collective-permute-start(bf16[72,128]{1,0:T(8,128)(2,1)S(1)} %get-tuple-element.39), channel_id=1, source_target_pairs={{0,1},{1,0},{2,3},{3,2},{4,5},{5,4},{6,7},{7,6},{8,9},{9,8},{12,13... | collective-permute-start | bytes 55304 | tf_op jit(solution)/shard_map/ppermute | solution.py:300
  5.2 10.9 %collective-permute-start.1 = (bf16[72,128]{1,0:T(8,128)(2,1)S(1)}, bf16[72,128]{1,0:T(8,128)(2,1)S(1)}, u32[]{:S(2)}, u32[]{:S(2)}) collective-permute-start(bf16[72,128]{1,0:T(8,128)(2,1)S(1)} %get-tuple-element.40), channel_id=1, source_target_pairs={{1,2},{2,1},{3,4},{4,3},{5,6},{6,5},{7,8},{8,7},{9,10},{10,9},{11,... | collective-permute-start | bytes 55304 | tf_op jit(solution)/shard_map/ppermute | solution.py:300
  16.1 0.7 collective-permute-start.2
  16.8 1.9 %load.1 = (s32[3,16]{1,0:T(4,128)S(4)}, s32[1,16]{1,0:T(1,128)S(4)}, bf16[16,72,128]{2,1,0:T(8,128)(2,1)S(1)}, f32[16,72,128]{2,1,0:T(8,128)S(1)}, f32[2,72,128]...) custom-call(f32[72,2048]{1,0:T(8,128)} %action_ref.3, ...), custom_call_target="tpu_custom_call" | custom-call | tf_op jit(solution)/shard_map/load/pallas_call | solution.py:312
  19.0 1.9 %collective-permute-start.3 = (bf16[72,128]{1,0:T(8,128)(2,1)S(1)}, bf16[72,128]{1,0:T(8,128)(2,1)S(1)}, u32[]{:S(2)}, u32[]{:S(2)}) collective-permute-start(bf16[72,128]{1,0:T(8,128)(2,1)S(1)} %get-tuple-element.47), channel_id=1, source_target_pairs={{0,1},{1,0},{2,3},{3,2},{4,5},{5,4},{6,7},{7,6},{8,9},{9,8},{12,13... | collective-permute-start | bytes 55304 | tf_op jit(solution)/shard_map/ppermute | solution.py:300
  20.9 4.8 %collective-permute-start.4 = (bf16[72,128]{1,0:T(8,128)(2,1)S(1)}, bf16[72,128]{1,0:T(8,128)(2,1)S(1)}, u32[]{:S(2)}, u32[]{:S(2)}) collective-permute-start(bf16[72,128]{1,0:T(8,128)(2,1)S(1)} %get-tuple-element.48), channel_id=1, source_target_pairs={{1,2},{2,1},{3,4},{4,3},{5,6},{6,5},{7,8},{8,7},{9,10},{10,9},{11,... | collective-permute-start | bytes 55304 | tf_op jit(solution)/shard_map/ppermute | solution.py:300
  25.7 0.7 collective-permute-start.5
  26.4 0.7 inner.3
  27.1 1.6 %collective-permute-done.4.in1 = bf16[72,128]{1,0:T(8,128)(2,1)S(1)} collective-permute-done((bf16[72,128]{1,0:T(8,128)(2,1)S(1)}, bf16[72,128]{1,0:T(8,128)(2,1)S(1)}, u32[]{:S(2)}, u32[]{:S(2)}) %collective-permute-start.4) | collective-permute-done | bytes 18464 | tf_op jit(solution)/shard_map/ppermute | solution.py:300
  28.9 1.9 %collective-permute-start.6 = (bf16[72,128]{1,0:T(8,128)(2,1)S(1)}, bf16[72,128]{1,0:T(8,128)(2,1)S(1)}, u32[]{:S(2)}, u32[]{:S(2)}) collective-permute-start(bf16[72,128]{1,0:T(8,128)(2,1)S(1)} %get-tuple-element.54), channel_id=1, source_target_pairs={{0,1},{1,0},{2,3},{3,2},{4,5},{5,4},{6,7},{7,6},{8,9},{9,8},{12,13... | collective-permute-start | bytes 55304 | tf_op jit(solution)/shard_map/ppermute | solution.py:300
  30.8 5.1 %collective-permute-start.7 = (bf16[72,128]{1,0:T(8,128)(2,1)S(1)}, bf16[72,128]{1,0:T(8,128)(2,1)S(1)}, u32[]{:S(2)}, u32[]{:S(2)}) collective-permute-start(bf16[72,128]{1,0:T(8,128)(2,1)S(1)} %get-tuple-element.55), channel_id=1, source_target_pairs={{1,2},{2,1},{3,4},{4,3},{5,6},{6,5},{7,8},{8,7},{9,10},{10,9},{11,... | collective-permute-start | bytes 55304 | tf_op jit(solution)/shard_map/ppermute | solution.py:300
  35.9 0.7 collective-permute-start.8
  36.6 0.7 inner.4
  37.3 1.3 %collective-permute-done.7.in1 = bf16[72,128]{1,0:T(8,128)(2,1)S(1)} collective-permute-done((bf16[72,128]{1,0:T(8,128)(2,1)S(1)}, bf16[72,128]{1,0:T(8,128)(2,1)S(1)}, u32[]{:S(2)}, u32[]{:S(2)}) %collective-permute-start.7) | collective-permute-done | bytes 18464 | tf_op jit(solution)/shard_map/ppermute | solution.py:300
  38.8 1.9 %collective-permute-start.9 = (bf16[72,128]{1,0:T(8,128)(2,1)S(1)}, bf16[72,128]{1,0:T(8,128)(2,1)S(1)}, u32[]{:S(2)}, u32[]{:S(2)}) collective-permute-start(bf16[72,128]{1,0:T(8,128)(2,1)S(1)} %get-tuple-element.61), channel_id=1, source_target_pairs={{0,1},{1,0},{2,3},{3,2},{4,5},{5,4},{6,7},{7,6},{8,9},{9,8},{12,13... | collective-permute-start | bytes 55304 | tf_op jit(solution)/shard_map/ppermute | solution.py:300
  40.8 4.6 %collective-permute-start.10 = (bf16[72,128]{1,0:T(8,128)(2,1)S(1)}, bf16[72,128]{1,0:T(8,128)(2,1)S(1)}, u32[]{:S(2)}, u32[]{:S(2)}) collective-permute-start(bf16[72,128]{1,0:T(8,128)(2,1)S(1)} %get-tuple-element.62), channel_id=1, source_target_pairs={{1,2},{2,1},{3,4},{4,3},{5,6},{6,5},{7,8},{8,7},{9,10},{10,9},{11,... | collective-permute-start | bytes 55304 | tf_op jit(solution)/shard_map/ppermute | solution.py:300
  45.4 0.7 collective-permute-start.11
  46.0 0.7 inner.5
  46.7 0.7 last_inner.1.inner_ref
  47.4 1.1 %collective-permute-done.10.in1 = bf16[72,128]{1,0:T(8,128)(2,1)S(1)} collective-permute-done((bf16[72,128]{1,0:T(8,128)(2,1)S(1)}, bf16[72,128]{1,0:T(8,128)(2,1)S(1)}, u32[]{:S(2)}, u32[]{:S(2)}) %collective-permute-start.10) | collective-permute-done | bytes 18464 | tf_op jit(solution)/shard_map/ppermute | solution.py:300
  48.5 0.3 last_edge.1
  48.9 25.2 %all_to_all.5 = bf16[16,72,128]{2,1,0:T(8,128)(2,1)S(1)} all-to-all(bf16[16,72,128]{2,1,0:T(8,128)(2,1)S(1)} %last_edge.1), channel_id=1, replica_groups=mesh['comp'=16,'dom'=48] {'comp'}, dimensions={0} | all-to-all | bytes 589824 | tf_op jit(solution)/shard_map/all_to_all | solution.py:345
  74.0 1.7 %source_terms.1 = f32[1,128,1152]{2,1,0:T(8,128)} custom-call(bf16[1152,128]{1,0:T(8,128)(2,1)S(1)} %bitcast.4, bf16[1152,1152]{1,0:T(8,128)(2,1)S(1)} %copy-done.1, bf16[1152,1152]{1,0:T(8,128)(2,1)S(1)} %copy-done.2), custom_call_target="tpu_custom_call" | custom-call | tf_op jit(solution)/shard_map/source_terms/pallas_call | solution.py:275
  (18 shorter events, 0.7 us)
Async XLA Ops:
  0.0 18.8 %copy-start = (bf16[16,3,128,128]{3,2,1,0:T(8,128)(2,1)S(1)}, bf16[16,3,128,128]{3,2,1,0:T(8,128)(2,1)}, u32[]{:S(2)}) copy-start(bf16[16,3,128,128]{3,2,1,0:T(8,128)(2,1)} %one_ref.16) | copy-start | bytes 4718596
  0.9 17.8 %collective-permute-start = (bf16[72,128]{1,0:T(8,128)(2,1)S(1)}, bf16[72,128]{1,0:T(8,128)(2,1)S(1)}, u32[]{:S(2)}, u32[]{:S(2)}) collective-permute-start(bf16[72,128]{1,0:T(8,128)(2,1)S(1)} %get-tuple-element.39), channel_id=1, source_target_pairs={{0,1},{1,0},{2,3},{3,2},{4,5},{5,4},{6,7},{7,6},{8,9},{9,8},{12,13... | collective-permute-start | bytes 55304 | tf_op jit(solution)/shard_map/ppermute | solution.py:300
  5.2 13.5 %collective-permute-start.1 = (bf16[72,128]{1,0:T(8,128)(2,1)S(1)}, bf16[72,128]{1,0:T(8,128)(2,1)S(1)}, u32[]{:S(2)}, u32[]{:S(2)}) collective-permute-start(bf16[72,128]{1,0:T(8,128)(2,1)S(1)} %get-tuple-element.40), channel_id=1, source_target_pairs={{1,2},{2,1},{3,4},{4,3},{5,6},{6,5},{7,8},{8,7},{9,10},{10,9},{11,... | collective-permute-start | bytes 55304 | tf_op jit(solution)/shard_map/ppermute | solution.py:300
  16.1 2.6 %collective-permute-start.2 = (bf16[72,128]{1,0:T(8,128)(2,1)S(1)}, bf16[72,128]{1,0:T(8,128)(2,1)S(1)}, u32[]{:S(2)}, u32[]{:S(2)}) collective-permute-start(bf16[72,128]{1,0:T(8,128)(2,1)S(1)} %get-tuple-element.41), channel_id=1, source_target_pairs={{10,11},{11,10},{22,23},{23,22},{34,35},{35,34},{46,47},{47,46},{5... | collective-permute-start | bytes 55304 | tf_op jit(solution)/shard_map/ppermute | solution.py:300
  19.0 8.1 %collective-permute-start.3 = (bf16[72,128]{1,0:T(8,128)(2,1)S(1)}, bf16[72,128]{1,0:T(8,128)(2,1)S(1)}, u32[]{:S(2)}, u32[]{:S(2)}) collective-permute-start(bf16[72,128]{1,0:T(8,128)(2,1)S(1)} %get-tuple-element.47), channel_id=1, source_target_pairs={{0,1},{1,0},{2,3},{3,2},{4,5},{5,4},{6,7},{7,6},{8,9},{9,8},{12,13... | collective-permute-start | bytes 55304 | tf_op jit(solution)/shard_map/ppermute | solution.py:300
  20.9 7.8 %collective-permute-start.4 = (bf16[72,128]{1,0:T(8,128)(2,1)S(1)}, bf16[72,128]{1,0:T(8,128)(2,1)S(1)}, u32[]{:S(2)}, u32[]{:S(2)}) collective-permute-start(bf16[72,128]{1,0:T(8,128)(2,1)S(1)} %get-tuple-element.48), channel_id=1, source_target_pairs={{1,2},{2,1},{3,4},{4,3},{5,6},{6,5},{7,8},{8,7},{9,10},{10,9},{11,... | collective-permute-start | bytes 55304 | tf_op jit(solution)/shard_map/ppermute | solution.py:300
  25.7 3.0 %collective-permute-start.5 = (bf16[72,128]{1,0:T(8,128)(2,1)S(1)}, bf16[72,128]{1,0:T(8,128)(2,1)S(1)}, u32[]{:S(2)}, u32[]{:S(2)}) collective-permute-start(bf16[72,128]{1,0:T(8,128)(2,1)S(1)} %get-tuple-element.49), channel_id=1, source_target_pairs={{10,11},{11,10},{22,23},{23,22},{34,35},{35,34},{46,47},{47,46},{5... | collective-permute-start | bytes 55304 | tf_op jit(solution)/shard_map/ppermute | solution.py:300
  28.9 8.4 %collective-permute-start.6 = (bf16[72,128]{1,0:T(8,128)(2,1)S(1)}, bf16[72,128]{1,0:T(8,128)(2,1)S(1)}, u32[]{:S(2)}, u32[]{:S(2)}) collective-permute-start(bf16[72,128]{1,0:T(8,128)(2,1)S(1)} %get-tuple-element.54), channel_id=1, source_target_pairs={{0,1},{1,0},{2,3},{3,2},{4,5},{5,4},{6,7},{7,6},{8,9},{9,8},{12,13... | collective-permute-start | bytes 55304 | tf_op jit(solution)/shard_map/ppermute | solution.py:300
  30.8 7.8 %collective-permute-start.7 = (bf16[72,128]{1,0:T(8,128)(2,1)S(1)}, bf16[72,128]{1,0:T(8,128)(2,1)S(1)}, u32[]{:S(2)}, u32[]{:S(2)}) collective-permute-start(bf16[72,128]{1,0:T(8,128)(2,1)S(1)} %get-tuple-element.55), channel_id=1, source_target_pairs={{1,2},{2,1},{3,4},{4,3},{5,6},{6,5},{7,8},{8,7},{9,10},{10,9},{11,... | collective-permute-start | bytes 55304 | tf_op jit(solution)/shard_map/ppermute | solution.py:300
  35.9 2.7 %collective-permute-start.8 = (bf16[72,128]{1,0:T(8,128)(2,1)S(1)}, bf16[72,128]{1,0:T(8,128)(2,1)S(1)}, u32[]{:S(2)}, u32[]{:S(2)}) collective-permute-start(bf16[72,128]{1,0:T(8,128)(2,1)S(1)} %get-tuple-element.56), channel_id=1, source_target_pairs={{10,11},{11,10},{22,23},{23,22},{34,35},{35,34},{46,47},{47,46},{5... | collective-permute-start | bytes 55304 | tf_op jit(solution)/shard_map/ppermute | solution.py:300
  38.8 8.6 %collective-permute-start.9 = (bf16[72,128]{1,0:T(8,128)(2,1)S(1)}, bf16[72,128]{1,0:T(8,128)(2,1)S(1)}, u32[]{:S(2)}, u32[]{:S(2)}) collective-permute-start(bf16[72,128]{1,0:T(8,128)(2,1)S(1)} %get-tuple-element.61), channel_id=1, source_target_pairs={{0,1},{1,0},{2,3},{3,2},{4,5},{5,4},{6,7},{7,6},{8,9},{9,8},{12,13... | collective-permute-start | bytes 55304 | tf_op jit(solution)/shard_map/ppermute | solution.py:300
  40.8 7.8 %collective-permute-start.10 = (bf16[72,128]{1,0:T(8,128)(2,1)S(1)}, bf16[72,128]{1,0:T(8,128)(2,1)S(1)}, u32[]{:S(2)}, u32[]{:S(2)}) collective-permute-start(bf16[72,128]{1,0:T(8,128)(2,1)S(1)} %get-tuple-element.62), channel_id=1, source_target_pairs={{1,2},{2,1},{3,4},{4,3},{5,6},{6,5},{7,8},{8,7},{9,10},{10,9},{11,... | collective-permute-start | bytes 55304 | tf_op jit(solution)/shard_map/ppermute | solution.py:300
  45.4 3.2 %collective-permute-start.11 = (bf16[72,128]{1,0:T(8,128)(2,1)S(1)}, bf16[72,128]{1,0:T(8,128)(2,1)S(1)}, u32[]{:S(2)}, u32[]{:S(2)}) collective-permute-start(bf16[72,128]{1,0:T(8,128)(2,1)S(1)} %get-tuple-element.63), channel_id=1, source_target_pairs={{10,11},{11,10},{22,23},{23,22},{34,35},{35,34},{46,47},{47,46},{5... | collective-permute-start | bytes 55304 | tf_op jit(solution)/shard_map/ppermute | solution.py:300
  48.5 25.5 %copy-start.1 = (bf16[1152,1152]{1,0:T(8,128)(2,1)S(1)}, bf16[1152,1152]{1,0:T(8,128)(2,1)}, u32[]{:S(2)}) copy-start(bf16[1152,1152]{1,0:T(8,128)(2,1)} %one_ref.17) | copy-start | bytes 7962628
  48.5 25.5 %copy-start.2 = (bf16[1152,1152]{1,0:T(8,128)(2,1)S(1)}, bf16[1152,1152]{1,0:T(8,128)(2,1)}, u32[]{:S(2)}) copy-start(bf16[1152,1152]{1,0:T(8,128)(2,1)} %two_ref.1) | copy-start | bytes 7962628

commit v6 on v5

--- a/solution.py
+++ b/solution.py
@@ -53,37 +53,38 @@
     return jnp.maximum(moved, KEEP * value)
 
 
-def exchange_of(edge):
+def up_of(edge):
     place = edge % CHAIN
-    return jnp.where(place == CHAIN - 1, 1, jnp.where(place == CHAIN - 2, 2, place % 2))
+    return 2 * (place < 5) + 1 * (place == 5) + 1 * (place == CHAIN - 1)
+
+
+def down_of(edge):
+    place = edge % CHAIN
+    return 1 * (place == 5) + 1 * (place == CHAIN - 1) + 2 * (place > 5) * (place < CHAIN - 1)
 
 
 def pairs_of(exchange, dom):
-    def carries(edge):
-        place = edge % CHAIN
-        return (1 if place == CHAIN - 1 else 2 if place == CHAIN - 2 else place % 2) == exchange
-
-    edges = [d for d in range(dom - 1) if carries(d)]
-    return [p for d in edges for p in ((d, d + 1), (d + 1, d))]
-
-
-def sides():
-    own = lax.axis_index("dom")
-    return exchange_of(own + CHAIN - 1), exchange_of(own)
+    edges = range(dom - 1)
+    return [(d, d + 1) for d in edges if up_of(d) == exchange] + [
+        (d + 1, d) for d in edges if down_of(d) == exchange
+    ]
 
 
 def pick(which, parts):
-    return jnp.where(which == 0, parts[0], jnp.where(which == 1, parts[1], parts[2]))
+    picked = parts[-1]
+    for exchange in range(len(parts) - 2, -1, -1):
+        picked = jnp.where(which == exchange, parts[exchange], picked)
+    return picked
 
 
 def halos(received):
     parts = [r[...] for r in received]
-    to_left, to_right = sides()
-    return pick(to_left, parts), pick(to_right, parts)
+    own = lax.axis_index("dom")
+    return pick(up_of(own + CHAIN - 1), parts), pick(down_of(own), parts)
 
 
 def send(outs, first, last):
-    to_left, _ = sides()
+    to_left = down_of(lax.axis_index("dom") + CHAIN - 1)
     for exchange, out in enumerate(outs):
         out[...] = jnp.where(to_left == exchange, first, last)
 

time: 76.1 us -> 75.5 us (level)
  waiting for transfers between devices: 3.98 us -> 3.21 us
    ppermute x12, waiting for transfers between devices: 3.98 us -> 3.21 us  [per_device(): lax.ppermute(x, 'dom', pairs_of(i, dom))]
where the time goes in v6:
time: 75.5 us; the launch traced here: 75.1 us
  starting transfers between devices  38.2 us (51%)
  blocking collectives  25.2 us (33%)
  Pallas kernels  8.31 us (11%)
  waiting for transfers between devices  3.21 us (4%)
    ppermute x12, starting transfers between devices, per_device(): lax.ppermute(x, 'dom', pairs_of(i, dom))  38.2 us
    all_to_all x1, blocking collectives, per_device(): lax.all_to_all(final, 'comp', split_axis=0, concat_axis=0, tiled=True)  25.2 us
    ppermute x12, waiting for transfers between devices, per_device(): lax.ppermute(x, 'dom', pairs_of(i, dom))  3.21 us
    pallas_call x3, Pallas kernels, per_device(): call(inner_kernel, [vm(blocks, bf16), vm(blocks, f32)], [smem()] + [vmem(...  2.1 us
    pallas_call x1, Pallas kernels, per_device(): call(load_kernel, [sm((nnz, n)), sm((1, n)), vm(blocks, bf16), vm(blocks,...  1.95 us
    pallas_call x1, Pallas kernels, source_terms(): pl.pallas_call(source_kernel, out_shape=jax.ShapeDtypeStruct((1, cells, c...  1.68 us
  transfers between devices with their start and end apart: 12, of which 3 were waited for; matrix products, arithmetic and copies ran while one was open for 0% of the time, Pallas kernels for 6%

profile of v6, /device:TPU:8, one launch (start us, length us, event | category | flops | bytes accessed | tf_op | source)
XLA Modules:
  0.0 75.1 jit_solution(1313244216911340114)
XLA Ops:
  0.0 0.9 %begin.1 = (bf16[72,128]{1,0:T(8,128)(2,1)S(1)}, bf16[72,128]{1,0:T(8,128)(2,1)S(1)}, bf16[72,128]{1,0:T(8,128)(2,1)S(1)}) custom-call(f32[72,2048]{1,0:T(8,128)} %action_ref.3), custom_call_target="tpu_custom_call" | custom-call | tf_op jit(solution)/shard_map/begin/pallas_call | solution.py:305
  0.9 1.3 %collective-permute-start = (bf16[72,128]{1,0:T(8,128)(2,1)S(1)}, bf16[72,128]{1,0:T(8,128)(2,1)S(1)}, u32[]{:S(2)}, u32[]{:S(2)}) collective-permute-start(bf16[72,128]{1,0:T(8,128)(2,1)S(1)} %get-tuple-element.39), channel_id=1, source_target_pairs={{6,7},{7,8},{8,9},{9,10},{10,11},{18,19},{19,20},{20,21},{21,22},{... | collective-permute-start | bytes 55304 | tf_op jit(solution)/shard_map/ppermute | solution.py:301
  2.2 14.5 %collective-permute-start.1 = (bf16[72,128]{1,0:T(8,128)(2,1)S(1)}, bf16[72,128]{1,0:T(8,128)(2,1)S(1)}, u32[]{:S(2)}, u32[]{:S(2)}) collective-permute-start(bf16[72,128]{1,0:T(8,128)(2,1)S(1)} %get-tuple-element.40), channel_id=1, source_target_pairs={{5,6},{11,12},{17,18},{23,24},{29,30},{35,36},{41,42},{6,5},{12,11... | collective-permute-start | bytes 55304 | tf_op jit(solution)/shard_map/ppermute | solution.py:301
  16.7 1.3 %collective-permute-start.2 = (bf16[72,128]{1,0:T(8,128)(2,1)S(1)}, bf16[72,128]{1,0:T(8,128)(2,1)S(1)}, u32[]{:S(2)}, u32[]{:S(2)}) collective-permute-start(bf16[72,128]{1,0:T(8,128)(2,1)S(1)} %get-tuple-element.41), channel_id=1, source_target_pairs={{0,1},{1,2},{2,3},{3,4},{4,5},{12,13},{13,14},{14,15},{15,16},{16,... | collective-permute-start | bytes 55304 | tf_op jit(solution)/shard_map/ppermute | solution.py:301
  18.0 1.9 %load.1 = (s32[3,16]{1,0:T(4,128)S(4)}, s32[1,16]{1,0:T(1,128)S(4)}, bf16[16,72,128]{2,1,0:T(8,128)(2,1)S(1)}, f32[16,72,128]{2,1,0:T(8,128)S(1)}, f32[2,72,128]...) custom-call(f32[72,2048]{1,0:T(8,128)} %action_ref.3, ...), custom_call_target="tpu_custom_call" | custom-call | tf_op jit(solution)/shard_map/load/pallas_call | solution.py:313
  20.3 1.3 %collective-permute-start.3 = (bf16[72,128]{1,0:T(8,128)(2,1)S(1)}, bf16[72,128]{1,0:T(8,128)(2,1)S(1)}, u32[]{:S(2)}, u32[]{:S(2)}) collective-permute-start(bf16[72,128]{1,0:T(8,128)(2,1)S(1)} %get-tuple-element.47), channel_id=1, source_target_pairs={{6,7},{7,8},{8,9},{9,10},{10,11},{18,19},{19,20},{20,21},{21,22},{... | collective-permute-start | bytes 55304 | tf_op jit(solution)/shard_map/ppermute | solution.py:301
  21.6 4.5 %collective-permute-start.4 = (bf16[72,128]{1,0:T(8,128)(2,1)S(1)}, bf16[72,128]{1,0:T(8,128)(2,1)S(1)}, u32[]{:S(2)}, u32[]{:S(2)}) collective-permute-start(bf16[72,128]{1,0:T(8,128)(2,1)S(1)} %get-tuple-element.48), channel_id=1, source_target_pairs={{5,6},{11,12},{17,18},{23,24},{29,30},{35,36},{41,42},{6,5},{12,11... | collective-permute-start | bytes 55304 | tf_op jit(solution)/shard_map/ppermute | solution.py:301
  26.0 1.3 %collective-permute-start.5 = (bf16[72,128]{1,0:T(8,128)(2,1)S(1)}, bf16[72,128]{1,0:T(8,128)(2,1)S(1)}, u32[]{:S(2)}, u32[]{:S(2)}) collective-permute-start(bf16[72,128]{1,0:T(8,128)(2,1)S(1)} %get-tuple-element.49), channel_id=1, source_target_pairs={{0,1},{1,2},{2,3},{3,4},{4,5},{12,13},{13,14},{14,15},{15,16},{16,... | collective-permute-start | bytes 55304 | tf_op jit(solution)/shard_map/ppermute | solution.py:301
  27.3 0.7 inner.3
  28.0 1.3 %collective-permute-done.4.in1 = bf16[72,128]{1,0:T(8,128)(2,1)S(1)} collective-permute-done((bf16[72,128]{1,0:T(8,128)(2,1)S(1)}, bf16[72,128]{1,0:T(8,128)(2,1)S(1)}, u32[]{:S(2)}, u32[]{:S(2)}) %collective-permute-start.4) | collective-permute-done | bytes 18464 | tf_op jit(solution)/shard_map/ppermute | solution.py:301
  29.6 1.3 %collective-permute-start.6 = (bf16[72,128]{1,0:T(8,128)(2,1)S(1)}, bf16[72,128]{1,0:T(8,128)(2,1)S(1)}, u32[]{:S(2)}, u32[]{:S(2)}) collective-permute-start(bf16[72,128]{1,0:T(8,128)(2,1)S(1)} %get-tuple-element.54), channel_id=1, source_target_pairs={{6,7},{7,8},{8,9},{9,10},{10,11},{18,19},{19,20},{20,21},{21,22},{... | collective-permute-start | bytes 55304 | tf_op jit(solution)/shard_map/ppermute | solution.py:301
  30.9 4.5 %collective-permute-start.7 = (bf16[72,128]{1,0:T(8,128)(2,1)S(1)}, bf16[72,128]{1,0:T(8,128)(2,1)S(1)}, u32[]{:S(2)}, u32[]{:S(2)}) collective-permute-start(bf16[72,128]{1,0:T(8,128)(2,1)S(1)} %get-tuple-element.55), channel_id=1, source_target_pairs={{5,6},{11,12},{17,18},{23,24},{29,30},{35,36},{41,42},{6,5},{12,11... | collective-permute-start | bytes 55304 | tf_op jit(solution)/shard_map/ppermute | solution.py:301
  35.3 1.3 %collective-permute-start.8 = (bf16[72,128]{1,0:T(8,128)(2,1)S(1)}, bf16[72,128]{1,0:T(8,128)(2,1)S(1)}, u32[]{:S(2)}, u32[]{:S(2)}) collective-permute-start(bf16[72,128]{1,0:T(8,128)(2,1)S(1)} %get-tuple-element.56), channel_id=1, source_target_pairs={{0,1},{1,2},{2,3},{3,4},{4,5},{12,13},{13,14},{14,15},{15,16},{16,... | collective-permute-start | bytes 55304 | tf_op jit(solution)/shard_map/ppermute | solution.py:301
  36.6 0.7 inner.4
  37.3 1.3 %collective-permute-done.7.in1 = bf16[72,128]{1,0:T(8,128)(2,1)S(1)} collective-permute-done((bf16[72,128]{1,0:T(8,128)(2,1)S(1)}, bf16[72,128]{1,0:T(8,128)(2,1)S(1)}, u32[]{:S(2)}, u32[]{:S(2)}) %collective-permute-start.7) | collective-permute-done | bytes 18464 | tf_op jit(solution)/shard_map/ppermute | solution.py:301
  38.8 1.3 %collective-permute-start.9 = (bf16[72,128]{1,0:T(8,128)(2,1)S(1)}, bf16[72,128]{1,0:T(8,128)(2,1)S(1)}, u32[]{:S(2)}, u32[]{:S(2)}) collective-permute-start(bf16[72,128]{1,0:T(8,128)(2,1)S(1)} %get-tuple-element.61), channel_id=1, source_target_pairs={{6,7},{7,8},{8,9},{9,10},{10,11},{18,19},{19,20},{20,21},{21,22},{... | collective-permute-start | bytes 55304 | tf_op jit(solution)/shard_map/ppermute | solution.py:301
  40.1 4.5 %collective-permute-start.10 = (bf16[72,128]{1,0:T(8,128)(2,1)S(1)}, bf16[72,128]{1,0:T(8,128)(2,1)S(1)}, u32[]{:S(2)}, u32[]{:S(2)}) collective-permute-start(bf16[72,128]{1,0:T(8,128)(2,1)S(1)} %get-tuple-element.62), channel_id=1, source_target_pairs={{5,6},{11,12},{17,18},{23,24},{29,30},{35,36},{41,42},{6,5},{12,11... | collective-permute-start | bytes 55304 | tf_op jit(solution)/shard_map/ppermute | solution.py:301
  44.6 1.3 %collective-permute-start.11 = (bf16[72,128]{1,0:T(8,128)(2,1)S(1)}, bf16[72,128]{1,0:T(8,128)(2,1)S(1)}, u32[]{:S(2)}, u32[]{:S(2)}) collective-permute-start(bf16[72,128]{1,0:T(8,128)(2,1)S(1)} %get-tuple-element.63), channel_id=1, source_target_pairs={{0,1},{1,2},{2,3},{3,4},{4,5},{12,13},{13,14},{14,15},{15,16},{16,... | collective-permute-start | bytes 55304 | tf_op jit(solution)/shard_map/ppermute | solution.py:301
  45.9 0.7 inner.5
  46.6 0.7 last_inner.1.inner_ref
  47.3 0.6 collective-permute-done.10.in1
  47.9 0.3 last_edge.1
  48.2 25.2 %all_to_all.5 = bf16[16,72,128]{2,1,0:T(8,128)(2,1)S(1)} all-to-all(bf16[16,72,128]{2,1,0:T(8,128)(2,1)S(1)} %last_edge.1), channel_id=1, replica_groups=mesh['comp'=16,'dom'=48] {'comp'}, dimensions={0} | all-to-all | bytes 589824 | tf_op jit(solution)/shard_map/all_to_all | solution.py:346
  73.4 1.7 %source_terms.1 = f32[1,128,1152]{2,1,0:T(8,128)} custom-call(bf16[1152,128]{1,0:T(8,128)(2,1)S(1)} %bitcast.4, bf16[1152,1152]{1,0:T(8,128)(2,1)S(1)} %copy-done.1, bf16[1152,1152]{1,0:T(8,128)(2,1)S(1)} %copy-done.2), custom_call_target="tpu_custom_call" | custom-call | tf_op jit(solution)/shard_map/source_terms/pallas_call | solution.py:276
  (18 shorter events, 0.7 us)
Async XLA Ops:
  0.0 20.0 %copy-start = (bf16[16,3,128,128]{3,2,1,0:T(8,128)(2,1)S(1)}, bf16[16,3,128,128]{3,2,1,0:T(8,128)(2,1)}, u32[]{:S(2)}) copy-start(bf16[16,3,128,128]{3,2,1,0:T(8,128)(2,1)} %one_ref.16) | copy-start | bytes 4718596
  0.9 19.0 %collective-permute-start = (bf16[72,128]{1,0:T(8,128)(2,1)S(1)}, bf16[72,128]{1,0:T(8,128)(2,1)S(1)}, u32[]{:S(2)}, u32[]{:S(2)}) collective-permute-start(bf16[72,128]{1,0:T(8,128)(2,1)S(1)} %get-tuple-element.39), channel_id=1, source_target_pairs={{6,7},{7,8},{8,9},{9,10},{10,11},{18,19},{19,20},{20,21},{21,22},{... | collective-permute-start | bytes 55304 | tf_op jit(solution)/shard_map/ppermute | solution.py:301
  2.2 17.7 %collective-permute-start.1 = (bf16[72,128]{1,0:T(8,128)(2,1)S(1)}, bf16[72,128]{1,0:T(8,128)(2,1)S(1)}, u32[]{:S(2)}, u32[]{:S(2)}) collective-permute-start(bf16[72,128]{1,0:T(8,128)(2,1)S(1)} %get-tuple-element.40), channel_id=1, source_target_pairs={{5,6},{11,12},{17,18},{23,24},{29,30},{35,36},{41,42},{6,5},{12,11... | collective-permute-start | bytes 55304 | tf_op jit(solution)/shard_map/ppermute | solution.py:301
  16.7 3.3 %collective-permute-start.2 = (bf16[72,128]{1,0:T(8,128)(2,1)S(1)}, bf16[72,128]{1,0:T(8,128)(2,1)S(1)}, u32[]{:S(2)}, u32[]{:S(2)}) collective-permute-start(bf16[72,128]{1,0:T(8,128)(2,1)S(1)} %get-tuple-element.41), channel_id=1, source_target_pairs={{0,1},{1,2},{2,3},{3,4},{4,5},{12,13},{13,14},{14,15},{15,16},{16,... | collective-permute-start | bytes 55304 | tf_op jit(solution)/shard_map/ppermute | solution.py:301
  20.3 7.8 %collective-permute-start.3 = (bf16[72,128]{1,0:T(8,128)(2,1)S(1)}, bf16[72,128]{1,0:T(8,128)(2,1)S(1)}, u32[]{:S(2)}, u32[]{:S(2)}) collective-permute-start(bf16[72,128]{1,0:T(8,128)(2,1)S(1)} %get-tuple-element.47), channel_id=1, source_target_pairs={{6,7},{7,8},{8,9},{9,10},{10,11},{18,19},{19,20},{20,21},{21,22},{... | collective-permute-start | bytes 55304 | tf_op jit(solution)/shard_map/ppermute | solution.py:301
  21.6 7.8 %collective-permute-start.4 = (bf16[72,128]{1,0:T(8,128)(2,1)S(1)}, bf16[72,128]{1,0:T(8,128)(2,1)S(1)}, u32[]{:S(2)}, u32[]{:S(2)}) collective-permute-start(bf16[72,128]{1,0:T(8,128)(2,1)S(1)} %get-tuple-element.48), channel_id=1, source_target_pairs={{5,6},{11,12},{17,18},{23,24},{29,30},{35,36},{41,42},{6,5},{12,11... | collective-permute-start | bytes 55304 | tf_op jit(solution)/shard_map/ppermute | solution.py:301
  26.0 3.3 %collective-permute-start.5 = (bf16[72,128]{1,0:T(8,128)(2,1)S(1)}, bf16[72,128]{1,0:T(8,128)(2,1)S(1)}, u32[]{:S(2)}, u32[]{:S(2)}) collective-permute-start(bf16[72,128]{1,0:T(8,128)(2,1)S(1)} %get-tuple-element.49), channel_id=1, source_target_pairs={{0,1},{1,2},{2,3},{3,4},{4,5},{12,13},{13,14},{14,15},{15,16},{16,... | collective-permute-start | bytes 55304 | tf_op jit(solution)/shard_map/ppermute | solution.py:301
  29.6 7.8 %collective-permute-start.6 = (bf16[72,128]{1,0:T(8,128)(2,1)S(1)}, bf16[72,128]{1,0:T(8,128)(2,1)S(1)}, u32[]{:S(2)}, u32[]{:S(2)}) collective-permute-start(bf16[72,128]{1,0:T(8,128)(2,1)S(1)} %get-tuple-element.54), channel_id=1, source_target_pairs={{6,7},{7,8},{8,9},{9,10},{10,11},{18,19},{19,20},{20,21},{21,22},{... | collective-permute-start | bytes 55304 | tf_op jit(solution)/shard_map/ppermute | solution.py:301
  30.9 7.8 %collective-permute-start.7 = (bf16[72,128]{1,0:T(8,128)(2,1)S(1)}, bf16[72,128]{1,0:T(8,128)(2,1)S(1)}, u32[]{:S(2)}, u32[]{:S(2)}) collective-permute-start(bf16[72,128]{1,0:T(8,128)(2,1)S(1)} %get-tuple-element.55), channel_id=1, source_target_pairs={{5,6},{11,12},{17,18},{23,24},{29,30},{35,36},{41,42},{6,5},{12,11... | collective-permute-start | bytes 55304 | tf_op jit(solution)/shard_map/ppermute | solution.py:301
  35.3 3.3 %collective-permute-start.8 = (bf16[72,128]{1,0:T(8,128)(2,1)S(1)}, bf16[72,128]{1,0:T(8,128)(2,1)S(1)}, u32[]{:S(2)}, u32[]{:S(2)}) collective-permute-start(bf16[72,128]{1,0:T(8,128)(2,1)S(1)} %get-tuple-element.56), channel_id=1, source_target_pairs={{0,1},{1,2},{2,3},{3,4},{4,5},{12,13},{13,14},{14,15},{15,16},{16,... | collective-permute-start | bytes 55304 | tf_op jit(solution)/shard_map/ppermute | solution.py:301
  38.8 8.4 %collective-permute-start.9 = (bf16[72,128]{1,0:T(8,128)(2,1)S(1)}, bf16[72,128]{1,0:T(8,128)(2,1)S(1)}, u32[]{:S(2)}, u32[]{:S(2)}) collective-permute-start(bf16[72,128]{1,0:T(8,128)(2,1)S(1)} %get-tuple-element.61), channel_id=1, source_target_pairs={{6,7},{7,8},{8,9},{9,10},{10,11},{18,19},{19,20},{20,21},{21,22},{... | collective-permute-start | bytes 55304 | tf_op jit(solution)/shard_map/ppermute | solution.py:301
  40.1 7.8 %collective-permute-start.10 = (bf16[72,128]{1,0:T(8,128)(2,1)S(1)}, bf16[72,128]{1,0:T(8,128)(2,1)S(1)}, u32[]{:S(2)}, u32[]{:S(2)}) collective-permute-start(bf16[72,128]{1,0:T(8,128)(2,1)S(1)} %get-tuple-element.62), channel_id=1, source_target_pairs={{5,6},{11,12},{17,18},{23,24},{29,30},{35,36},{41,42},{6,5},{12,11... | collective-permute-start | bytes 55304 | tf_op jit(solution)/shard_map/ppermute | solution.py:301
  44.6 3.3 %collective-permute-start.11 = (bf16[72,128]{1,0:T(8,128)(2,1)S(1)}, bf16[72,128]{1,0:T(8,128)(2,1)S(1)}, u32[]{:S(2)}, u32[]{:S(2)}) collective-permute-start(bf16[72,128]{1,0:T(8,128)(2,1)S(1)} %get-tuple-element.63), channel_id=1, source_target_pairs={{0,1},{1,2},{2,3},{3,4},{4,5},{12,13},{13,14},{14,15},{15,16},{16,... | collective-permute-start | bytes 55304 | tf_op jit(solution)/shard_map/ppermute | solution.py:301
  47.9 25.5 %copy-start.1 = (bf16[1152,1152]{1,0:T(8,128)(2,1)S(1)}, bf16[1152,1152]{1,0:T(8,128)(2,1)}, u32[]{:S(2)}) copy-start(bf16[1152,1152]{1,0:T(8,128)(2,1)} %one_ref.17) | copy-start | bytes 7962628
  47.9 25.5 %copy-start.2 = (bf16[1152,1152]{1,0:T(8,128)(2,1)S(1)}, bf16[1152,1152]{1,0:T(8,128)(2,1)}, u32[]{:S(2)}) copy-start(bf16[1152,1152]{1,0:T(8,128)(2,1)} %two_ref.1) | copy-start | bytes 7962628

commit v7 on v6

--- a/solution.py
+++ b/solution.py
@@ -1,3 +1,5 @@
+import functools
+
 import jax
 import jax.numpy as jnp
 from jax import lax
@@ -9,6 +11,8 @@
 KEEP = 0.25
 CHAIN = 12
 ROUND = 3
+LOADS = 5
+MADE = 8
 
 
 def in_vmem(x):
@@ -53,20 +57,24 @@
     return jnp.maximum(moved, KEEP * value)
 
 
-def up_of(edge):
+def up_of(edge, opening):
     place = edge % CHAIN
+    if opening:
+        return 1 * (place == CHAIN - 1) + 2 * (place == CHAIN - 2) + (place % 2) * (place < CHAIN - 2)
     return 2 * (place < 5) + 1 * (place == 5) + 1 * (place == CHAIN - 1)
 
 
-def down_of(edge):
+def down_of(edge, opening):
     place = edge % CHAIN
+    if opening:
+        return up_of(edge, opening)
     return 1 * (place == 5) + 1 * (place == CHAIN - 1) + 2 * (place > 5) * (place < CHAIN - 1)
 
 
-def pairs_of(exchange, dom):
+def pairs_of(exchange, dom, opening):
     edges = range(dom - 1)
-    return [(d, d + 1) for d in edges if up_of(d) == exchange] + [
-        (d + 1, d) for d in edges if down_of(d) == exchange
+    return [(d, d + 1) for d in edges if up_of(d, opening) == exchange] + [
+        (d + 1, d) for d in edges if down_of(d, opening) == exchange
     ]
 
 
@@ -77,14 +85,14 @@
     return picked
 
 
-def halos(received):
+def halos(received, opening):
     parts = [r[...] for r in received]
     own = lax.axis_index("dom")
-    return pick(up_of(own + CHAIN - 1), parts), pick(down_of(own), parts)
-
-
-def send(outs, first, last):
-    to_left = down_of(lax.axis_index("dom") + CHAIN - 1)
+    return pick(up_of(own + CHAIN - 1, opening), parts), pick(down_of(own, opening), parts)
+
+
+def send(outs, first, last, opening):
+    to_left = down_of(lax.axis_index("dom") + CHAIN - 1, opening)
     for exchange, out in enumerate(outs):
         out[...] = jnp.where(to_left == exchange, first, last)
 
@@ -112,22 +120,22 @@
     ]
 
 
-def edge_kernel(cols, in0, in1, in2, blocks_ref, ends_ref, one_ref, two_ref, c1_ref, c2_ref, *outs):
+def edge_kernel(opening, cols, in0, in1, in2, blocks_ref, ends_ref, one_ref, two_ref, c1_ref, c2_ref, *outs):
     out0, out1, out2, ends16, ends32 = outs
-    left, right = halos((in0, in1, in2))
+    left, right = halos((in0, in1, in2), opening)
     first, last = edge_rows(
         cols, left, right, blocks_ref, ends_ref[0], ends_ref[1], one_ref, two_ref, c1_ref[...], c2_ref[...]
     )
     ends32[0], ends32[1] = first, last
     first, last = first.astype(jnp.bfloat16), last.astype(jnp.bfloat16)
     ends16[0], ends16[1] = first, last
-    send((out0, out1, out2), first, last)
-
-
-def inner_kernel(cols, in0, in1, in2, blocks_ref, field_ref, ends16, one_ref, two_ref, c1_ref, c2_ref, *outs):
+    send((out0, out1, out2), first, last, False)
+
+
+def inner_kernel(opening, cols, in0, in1, in2, blocks_ref, field_ref, ends16, one_ref, two_ref, c1_ref, c2_ref, *outs):
     out16, out32 = outs
     n, rows, width = blocks_ref.shape
-    left, right = halos((in0, in1, in2))
+    left, right = halos((in0, in1, in2), opening)
     c1, c2 = c1_ref[...], c2_ref[...]
     out16[0] = ends16[0]
     out16[n - 1] = ends16[1]
@@ -165,7 +173,7 @@
 
 def last_edge_kernel(cols, todo, in0, in1, in2, blocks_ref, field_ref, ends_ref, one_ref, two_ref, c1_ref, c2_ref, inner_ref, out16):
     n, rows, width = blocks_ref.shape
-    left, right = halos((in0, in1, in2))
+    left, right = halos((in0, in1, in2), False)
     c1, c2 = c1_ref[...], c2_ref[...]
 
     def again(b):
@@ -209,11 +217,12 @@
         copy.start()
     for copy in copies:
         copy.wait()
-    send((out0, out1, out2), buffers[0].astype(jnp.bfloat16), buffers[1].astype(jnp.bfloat16))
-
-
-def load_kernel(action_ref, coef_one_hbm, coef_two_hbm, two_hbm, cols_hbm, *refs):
-    cols, todo, out16, out32, ends32, two, c1, c2, coefs, sems = refs
+    send((out0, out1, out2), buffers[0].astype(jnp.bfloat16), buffers[1].astype(jnp.bfloat16), True)
+
+
+def load(sources, outs, coefs, sems):
+    action_ref, coef_one_hbm, coef_two_hbm, two_hbm, cols_hbm = sources
+    cols, todo, out16, out32, ends32, two, c1, c2 = outs
     n, rows, width = out16.shape
     small = [
         pltpu.make_async_copy(cols_hbm, cols, sems.at[n + 2]),
@@ -250,6 +259,22 @@
     ends32[0] = out32[0]
     ends32[1] = out32[n - 1]
     weights.wait()
+
+
+def load_early_kernel(*refs):
+    sources, outs, (coefs, sems) = refs[:LOADS], refs[LOADS + 2 : -4], refs[-2:]
+
+    @pl.when(lax.axis_index("dom") % CHAIN == 0)
+    def _():
+        load(sources, outs, coefs, sems)
+
+
+def load_late_kernel(*refs):
+    sources, outs, (coefs, sems) = refs[:LOADS], refs[LOADS + MADE : -2], refs[-2:]
+
+    @pl.when(lax.axis_index("dom") % CHAIN != 0)
+    def _():
+        load(sources, outs, coefs, sems)
 
 
 def source_kernel(cells_ref, one_ref, two_ref, out_hbm, buffers, sems):
@@ -297,44 +322,58 @@
     block, blocks, ends, weights = (rows, width), (n, rows, width), (2, rows, width), (n, nnz, width, width)
     vm = lambda shape, dtype: (pltpu.VMEM, shape, dtype)
     sm = lambda shape: (pltpu.SMEM, shape, jnp.int32)
-    exchange = lambda parts: [
-        in_vmem(lax.ppermute(x, "dom", pairs_of(i, dom))) for i, x in enumerate(parts)
-    ]
-
-    received = exchange(
-        call(
-            begin_kernel,
-            [vm(block, bf16)] * 3,
-            [hbm()],
-            "begin",
-            [pltpu.VMEM((2, rows, width), f32), pltpu.SemaphoreType.DMA((2,))],
-        )(in_hbm(action))
-    )
+    exchange = lambda parts, opening: [
+        in_vmem(lax.ppermute(x, "dom", pairs_of(i, dom, opening))) for i, x in enumerate(parts)
+    ]
+
+    out_part, boundary_part, back_part = call(
+        begin_kernel,
+        [vm(block, bf16)] * 3,
+        [hbm()],
+        "begin",
+        [pltpu.VMEM((2, rows, width), f32), pltpu.SemaphoreType.DMA((2,))],
+    )(in_hbm(action))
+    sources = [
+        in_hbm(x)
+        for x in (
+            action,
+            coef_one.reshape(1, rows),
+            coef_two.reshape(1, rows),
+            transport_two,
+            block_cols.T,
+        )
+    ]
+    made = [sm((nnz, n)), sm((1, n)), vm(blocks, bf16), vm(blocks, f32), vm(ends, f32)]
+    made += [vm(weights, bf16)] + [vm(block, f32)] * 2
+    room = [pltpu.VMEM((2, 1, rows), f32), pltpu.SemaphoreType.DMA((n + 4,))]
+    *loaded, boundary_part, back_part = call(
+        load_early_kernel,
+        made + [vm(block, bf16)] * 2,
+        [hbm()] * LOADS + [vmem()] * 2,
+        "load_early",
+        room,
+        aliases={LOADS: MADE, LOADS + 1: MADE + 1},
+    )(*sources, boundary_part, back_part)
+    received = exchange((out_part, boundary_part, back_part), True)
     cols, todo, value16, value32, ends32, two, c1, c2 = call(
-        load_kernel,
-        [sm((nnz, n)), sm((1, n)), vm(blocks, bf16), vm(blocks, f32), vm(ends, f32)]
-        + [vm(weights, bf16), vm(block, f32), vm(block, f32)],
-        [hbm()] * 5,
-        "load",
-        [pltpu.VMEM((2, 1, rows), f32), pltpu.SemaphoreType.DMA((n + 4,))],
-    )(
-        in_hbm(action),
-        in_hbm(coef_one.reshape(1, rows)),
-        in_hbm(coef_two.reshape(1, rows)),
-        in_hbm(transport_two),
-        in_hbm(block_cols.T),
-    )
+        load_late_kernel,
+        made,
+        [hbm()] * LOADS + [smem()] * 2 + [vmem()] * (MADE - 2),
+        "load_late",
+        room,
+        aliases={LOADS + i: i for i in range(MADE)},
+    )(*sources, *loaded)
     one = in_vmem(transport_one)
     for substep in range(SUBSTEPS - 1):
         *parts, ends16, ends32 = call(
-            edge_kernel,
+            functools.partial(edge_kernel, substep == 0),
             [vm(block, bf16)] * 3 + [vm(ends, bf16), vm(ends, f32)],
             [smem()] + [vmem()] * 9,
             "edges",
         )(cols, *received, value16, ends32, one, two, c1, c2)
-        new_received = exchange(parts)
+        new_received = exchange(parts, False)
         value16, value32 = call(
-            inner_kernel, [vm(blocks, bf16), vm(blocks, f32)], [smem()] + [vmem()] * 10, "inner"
+            functools.partial(inner_kernel, substep == 0), [vm(blocks, bf16), vm(blocks, f32)], [smem()] + [vmem()] * 10, "inner"
         )(cols, *received, value16, value32, ends16, one, two, c1, c2)
         received = new_received
     (final,) = call(last_inner_kernel, [vm(blocks, bf16)], [smem()] + [vmem()] * 6, "last_inner")(

time: 75.5 us -> 75.6 us (level)
  waiting for transfers between devices: 3.21 us -> 2.33 us
    ppermute x12, waiting for transfers between devices: 3.21 us -> 2.33 us  [per_device(): lax.ppermute(x, 'dom', pairs_of(i, dom, opening))]
    pallas_call x7 -> x8, Pallas kernels: 4.71 us -> 4.95 us  [the longest x3 2.11 us: per_device(): call(functools.partial(inner_kernel, substep == 0), [vm(blocks, bf16), vm...]
  transfers between devices with their start and end apart: 12 -> 12, of which waited for: 3 -> 4; matrix products, arithmetic and copies ran while one was open for 0% -> 0% of each run, Pallas kernels for 6% -> 7%
where the time goes in v7:
time: 75.6 us; the launch traced here: 75.2 us
  starting transfers between devices  38.7 us (51%)
  blocking collectives  25.2 us (33%)
  Pallas kernels  8.43 us (11%)
  waiting for transfers between devices  2.33 us (3%)
    ppermute x12, starting transfers between devices, per_device(): lax.ppermute(x, 'dom', pairs_of(i, dom, opening))  38.7 us
    all_to_all x1, blocking collectives, per_device(): lax.all_to_all(final, 'comp', split_axis=0, concat_axis=0, tiled=True)  25.2 us
    ppermute x12, waiting for transfers between devices, per_device(): lax.ppermute(x, 'dom', pairs_of(i, dom, opening))  2.33 us
    pallas_call x3, Pallas kernels, per_device(): call(functools.partial(inner_kernel, substep == 0), [vm(blocks, bf16), vm...  2.11 us
    pallas_call x1, Pallas kernels, per_device(): call(load_early_kernel, made + [vm(block, bf16)] * 2, [hbm()] * LOADS + [...  1.97 us
    pallas_call x1, Pallas kernels, source_terms(): pl.pallas_call(source_kernel, out_shape=jax.ShapeDtypeStruct((1, cells, c...  1.68 us
  transfers between devices with their start and end apart: 12, of which 4 were waited for; matrix products, arithmetic and copies ran while one was open for 0% of the time, Pallas kernels for 7%

profile of v7, /device:TPU:8, one launch (start us, length us, event | category | flops | bytes accessed | tf_op | source)
XLA Modules:
  0.0 75.2 jit_solution(10261362663264611299)
XLA Ops:
  0.0 0.8 %begin.1 = (bf16[72,128]{1,0:T(8,128)(2,1)S(1)}, bf16[72,128]{1,0:T(8,128)(2,1)S(1)}, bf16[72,128]{1,0:T(8,128)(2,1)S(1)}) custom-call(f32[72,2048]{1,0:T(8,128)} %refs_0_.3), custom_call_target="tpu_custom_call" | custom-call | tf_op jit(solution)/shard_map/begin/pallas_call | solution.py:329
  0.8 4.3 %collective-permute-start = (bf16[72,128]{1,0:T(8,128)(2,1)S(1)}, bf16[72,128]{1,0:T(8,128)(2,1)S(1)}, u32[]{:S(2)}, u32[]{:S(2)}) collective-permute-start(bf16[72,128]{1,0:T(8,128)(2,1)S(1)} %get-tuple-element.59), channel_id=1, source_target_pairs={{0,1},{2,3},{4,5},{6,7},{8,9},{12,13},{14,15},{16,17},{18,19},{20,... | collective-permute-start | bytes 55304 | tf_op jit(solution)/shard_map/ppermute | solution.py:326
  5.1 2.0 %load_early.1 = (s32[3,16]{1,0:T(4,128)S(4)}, s32[1,16]{1,0:T(1,128)S(4)}, bf16[16,72,128]{2,1,0:T(8,128)(2,1)S(1)}, f32[16,72,128]{2,1,0:T(8,128)S(1)}, f32[2,7...) custom-call(f32[72,2048]{1,0:T(8,128)} %refs_0_.3, ...), custom_call_target="tpu_custom_call", output_to_operand_aliasing={{8}: (5, {}), {9}: (6, {})} | custom-call | tf_op jit(solution)/shard_map/load_early/pallas_call | solution.py:349
  7.1 9.1 %collective-permute-start.1 = (bf16[72,128]{1,0:T(8,128)(2,1)S(1)}, bf16[72,128]{1,0:T(8,128)(2,1)S(1)}, u32[]{:S(2)}, u32[]{:S(2)}) collective-permute-start(bf16[72,128]{1,0:T(8,128)(2,1)S(1)} %get-tuple-element.60), channel_id=1, source_target_pairs={{1,2},{3,4},{5,6},{7,8},{9,10},{11,12},{13,14},{15,16},{17,18},{19... | collective-permute-start | bytes 55304 | tf_op jit(solution)/shard_map/ppermute | solution.py:326
  16.2 0.7 collective-permute-start.2
  17.1 0.8 %collective-permute-done.1.in1 = bf16[72,128]{1,0:T(8,128)(2,1)S(1)} collective-permute-done((bf16[72,128]{1,0:T(8,128)(2,1)S(1)}, bf16[72,128]{1,0:T(8,128)(2,1)S(1)}, u32[]{:S(2)}, u32[]{:S(2)}) %collective-permute-start.1) | collective-permute-done | bytes 18464 | tf_op jit(solution)/shard_map/ppermute | solution.py:326
  17.9 0.4 copy-done
  18.5 1.3 %collective-permute-start.3 = (bf16[72,128]{1,0:T(8,128)(2,1)S(1)}, bf16[72,128]{1,0:T(8,128)(2,1)S(1)}, u32[]{:S(2)}, u32[]{:S(2)}) collective-permute-start(bf16[72,128]{1,0:T(8,128)(2,1)S(1)} %get-tuple-element.67), channel_id=1, source_target_pairs={{6,7},{7,8},{8,9},{9,10},{10,11},{18,19},{19,20},{20,21},{21,22},{... | collective-permute-start | bytes 55304 | tf_op jit(solution)/shard_map/ppermute | solution.py:326
  19.8 6.8 %collective-permute-start.4 = (bf16[72,128]{1,0:T(8,128)(2,1)S(1)}, bf16[72,128]{1,0:T(8,128)(2,1)S(1)}, u32[]{:S(2)}, u32[]{:S(2)}) collective-permute-start(bf16[72,128]{1,0:T(8,128)(2,1)S(1)} %get-tuple-element.68), channel_id=1, source_target_pairs={{5,6},{11,12},{17,18},{23,24},{29,30},{35,36},{41,42},{6,5},{12,11... | collective-permute-start | bytes 55304 | tf_op jit(solution)/shard_map/ppermute | solution.py:326
  26.7 1.3 %collective-permute-start.5 = (bf16[72,128]{1,0:T(8,128)(2,1)S(1)}, bf16[72,128]{1,0:T(8,128)(2,1)S(1)}, u32[]{:S(2)}, u32[]{:S(2)}) collective-permute-start(bf16[72,128]{1,0:T(8,128)(2,1)S(1)} %get-tuple-element.69), channel_id=1, source_target_pairs={{0,1},{1,2},{2,3},{3,4},{4,5},{12,13},{13,14},{14,15},{15,16},{16,... | collective-permute-start | bytes 55304 | tf_op jit(solution)/shard_map/ppermute | solution.py:326
  28.0 0.7 inner.3
  28.7 0.7 collective-permute-done.5.in2
  29.6 1.3 %collective-permute-start.6 = (bf16[72,128]{1,0:T(8,128)(2,1)S(1)}, bf16[72,128]{1,0:T(8,128)(2,1)S(1)}, u32[]{:S(2)}, u32[]{:S(2)}) collective-permute-start(bf16[72,128]{1,0:T(8,128)(2,1)S(1)} %get-tuple-element.74), channel_id=1, source_target_pairs={{6,7},{7,8},{8,9},{9,10},{10,11},{18,19},{19,20},{20,21},{21,22},{... | collective-permute-start | bytes 55304 | tf_op jit(solution)/shard_map/ppermute | solution.py:326
  30.9 5.0 %collective-permute-start.7 = (bf16[72,128]{1,0:T(8,128)(2,1)S(1)}, bf16[72,128]{1,0:T(8,128)(2,1)S(1)}, u32[]{:S(2)}, u32[]{:S(2)}) collective-permute-start(bf16[72,128]{1,0:T(8,128)(2,1)S(1)} %get-tuple-element.75), channel_id=1, source_target_pairs={{5,6},{11,12},{17,18},{23,24},{29,30},{35,36},{41,42},{6,5},{12,11... | collective-permute-start | bytes 55304 | tf_op jit(solution)/shard_map/ppermute | solution.py:326
  36.0 1.3 %collective-permute-start.8 = (bf16[72,128]{1,0:T(8,128)(2,1)S(1)}, bf16[72,128]{1,0:T(8,128)(2,1)S(1)}, u32[]{:S(2)}, u32[]{:S(2)}) collective-permute-start(bf16[72,128]{1,0:T(8,128)(2,1)S(1)} %get-tuple-element.76), channel_id=1, source_target_pairs={{0,1},{1,2},{2,3},{3,4},{4,5},{12,13},{13,14},{14,15},{15,16},{16,... | collective-permute-start | bytes 55304 | tf_op jit(solution)/shard_map/ppermute | solution.py:326
  37.3 0.7 inner.4
  38.0 0.7 collective-permute-done.7.in1
  38.9 1.3 %collective-permute-start.9 = (bf16[72,128]{1,0:T(8,128)(2,1)S(1)}, bf16[72,128]{1,0:T(8,128)(2,1)S(1)}, u32[]{:S(2)}, u32[]{:S(2)}) collective-permute-start(bf16[72,128]{1,0:T(8,128)(2,1)S(1)} %get-tuple-element.81), channel_id=1, source_target_pairs={{6,7},{7,8},{8,9},{9,10},{10,11},{18,19},{19,20},{20,21},{21,22},{... | collective-permute-start | bytes 55304 | tf_op jit(solution)/shard_map/ppermute | solution.py:326
  40.2 5.0 %collective-permute-start.10 = (bf16[72,128]{1,0:T(8,128)(2,1)S(1)}, bf16[72,128]{1,0:T(8,128)(2,1)S(1)}, u32[]{:S(2)}, u32[]{:S(2)}) collective-permute-start(bf16[72,128]{1,0:T(8,128)(2,1)S(1)} %get-tuple-element.82), channel_id=1, source_target_pairs={{5,6},{11,12},{17,18},{23,24},{29,30},{35,36},{41,42},{6,5},{12,11... | collective-permute-start | bytes 55304 | tf_op jit(solution)/shard_map/ppermute | solution.py:326
  45.2 1.3 %collective-permute-start.11 = (bf16[72,128]{1,0:T(8,128)(2,1)S(1)}, bf16[72,128]{1,0:T(8,128)(2,1)S(1)}, u32[]{:S(2)}, u32[]{:S(2)}) collective-permute-start(bf16[72,128]{1,0:T(8,128)(2,1)S(1)} %get-tuple-element.83), channel_id=1, source_target_pairs={{0,1},{1,2},{2,3},{3,4},{4,5},{12,13},{13,14},{14,15},{15,16},{16,... | collective-permute-start | bytes 55304 | tf_op jit(solution)/shard_map/ppermute | solution.py:326
  46.5 0.7 inner.5
  47.2 0.7 last_inner.1.inner_ref
  48.3 25.2 %all_to_all.5 = bf16[16,72,128]{2,1,0:T(8,128)(2,1)S(1)} all-to-all(bf16[16,72,128]{2,1,0:T(8,128)(2,1)S(1)} %last_edge.1), channel_id=1, replica_groups=mesh['comp'=16,'dom'=48] {'comp'}, dimensions={0} | all-to-all | bytes 589824 | tf_op jit(solution)/shard_map/all_to_all | solution.py:385
  73.5 1.7 %source_terms.1 = f32[1,128,1152]{2,1,0:T(8,128)} custom-call(bf16[1152,128]{1,0:T(8,128)(2,1)S(1)} %bitcast.4, bf16[1152,1152]{1,0:T(8,128)(2,1)S(1)} %copy-done.1, bf16[1152,1152]{1,0:T(8,128)(2,1)S(1)} %copy-done.2), custom_call_target="tpu_custom_call" | custom-call | tf_op jit(solution)/shard_map/source_terms/pallas_call | solution.py:301
  (19 shorter events, 1.3 us)
Async XLA Ops:
  0.8 16.3 %collective-permute-start = (bf16[72,128]{1,0:T(8,128)(2,1)S(1)}, bf16[72,128]{1,0:T(8,128)(2,1)S(1)}, u32[]{:S(2)}, u32[]{:S(2)}) collective-permute-start(bf16[72,128]{1,0:T(8,128)(2,1)S(1)} %get-tuple-element.59), channel_id=1, source_target_pairs={{0,1},{2,3},{4,5},{6,7},{8,9},{12,13},{14,15},{16,17},{18,19},{20,... | collective-permute-start | bytes 55304 | tf_op jit(solution)/shard_map/ppermute | solution.py:326
  7.1 10.8 %collective-permute-start.1 = (bf16[72,128]{1,0:T(8,128)(2,1)S(1)}, bf16[72,128]{1,0:T(8,128)(2,1)S(1)}, u32[]{:S(2)}, u32[]{:S(2)}) collective-permute-start(bf16[72,128]{1,0:T(8,128)(2,1)S(1)} %get-tuple-element.60), channel_id=1, source_target_pairs={{1,2},{3,4},{5,6},{7,8},{9,10},{11,12},{13,14},{15,16},{17,18},{19... | collective-permute-start | bytes 55304 | tf_op jit(solution)/shard_map/ppermute | solution.py:326
  16.2 1.7 %collective-permute-start.2 = (bf16[72,128]{1,0:T(8,128)(2,1)S(1)}, bf16[72,128]{1,0:T(8,128)(2,1)S(1)}, u32[]{:S(2)}, u32[]{:S(2)}) collective-permute-start(bf16[72,128]{1,0:T(8,128)(2,1)S(1)} %get-tuple-element.61), channel_id=1, source_target_pairs={{10,11},{22,23},{34,35},{46,47},{11,10},{23,22},{35,34},{47,46},{5... | collective-permute-start | bytes 55304 | tf_op jit(solution)/shard_map/ppermute | solution.py:326
  16.9 1.4 %copy-start = (bf16[16,3,128,128]{3,2,1,0:T(8,128)(2,1)S(1)}, bf16[16,3,128,128]{3,2,1,0:T(8,128)(2,1)}, u32[]{:S(2)}) copy-start(bf16[16,3,128,128]{3,2,1,0:T(8,128)(2,1)} %one_ref.16) | copy-start | bytes 4718596
  18.5 10.2 %collective-permute-start.3 = (bf16[72,128]{1,0:T(8,128)(2,1)S(1)}, bf16[72,128]{1,0:T(8,128)(2,1)S(1)}, u32[]{:S(2)}, u32[]{:S(2)}) collective-permute-start(bf16[72,128]{1,0:T(8,128)(2,1)S(1)} %get-tuple-element.67), channel_id=1, source_target_pairs={{6,7},{7,8},{8,9},{9,10},{10,11},{18,19},{19,20},{20,21},{21,22},{... | collective-permute-start | bytes 55304 | tf_op jit(solution)/shard_map/ppermute | solution.py:326
  19.8 8.9 %collective-permute-start.4 = (bf16[72,128]{1,0:T(8,128)(2,1)S(1)}, bf16[72,128]{1,0:T(8,128)(2,1)S(1)}, u32[]{:S(2)}, u32[]{:S(2)}) collective-permute-start(bf16[72,128]{1,0:T(8,128)(2,1)S(1)} %get-tuple-element.68), channel_id=1, source_target_pairs={{5,6},{11,12},{17,18},{23,24},{29,30},{35,36},{41,42},{6,5},{12,11... | collective-permute-start | bytes 55304 | tf_op jit(solution)/shard_map/ppermute | solution.py:326
  26.7 2.7 %collective-permute-start.5 = (bf16[72,128]{1,0:T(8,128)(2,1)S(1)}, bf16[72,128]{1,0:T(8,128)(2,1)S(1)}, u32[]{:S(2)}, u32[]{:S(2)}) collective-permute-start(bf16[72,128]{1,0:T(8,128)(2,1)S(1)} %get-tuple-element.69), channel_id=1, source_target_pairs={{0,1},{1,2},{2,3},{3,4},{4,5},{12,13},{13,14},{14,15},{15,16},{16,... | collective-permute-start | bytes 55304 | tf_op jit(solution)/shard_map/ppermute | solution.py:326
  29.6 8.3 %collective-permute-start.6 = (bf16[72,128]{1,0:T(8,128)(2,1)S(1)}, bf16[72,128]{1,0:T(8,128)(2,1)S(1)}, u32[]{:S(2)}, u32[]{:S(2)}) collective-permute-start(bf16[72,128]{1,0:T(8,128)(2,1)S(1)} %get-tuple-element.74), channel_id=1, source_target_pairs={{6,7},{7,8},{8,9},{9,10},{10,11},{18,19},{19,20},{20,21},{21,22},{... | collective-permute-start | bytes 55304 | tf_op jit(solution)/shard_map/ppermute | solution.py:326
  30.9 7.8 %collective-permute-start.7 = (bf16[72,128]{1,0:T(8,128)(2,1)S(1)}, bf16[72,128]{1,0:T(8,128)(2,1)S(1)}, u32[]{:S(2)}, u32[]{:S(2)}) collective-permute-start(bf16[72,128]{1,0:T(8,128)(2,1)S(1)} %get-tuple-element.75), channel_id=1, source_target_pairs={{5,6},{11,12},{17,18},{23,24},{29,30},{35,36},{41,42},{6,5},{12,11... | collective-permute-start | bytes 55304 | tf_op jit(solution)/shard_map/ppermute | solution.py:326
  36.0 2.7 %collective-permute-start.8 = (bf16[72,128]{1,0:T(8,128)(2,1)S(1)}, bf16[72,128]{1,0:T(8,128)(2,1)S(1)}, u32[]{:S(2)}, u32[]{:S(2)}) collective-permute-start(bf16[72,128]{1,0:T(8,128)(2,1)S(1)} %get-tuple-element.76), channel_id=1, source_target_pairs={{0,1},{1,2},{2,3},{3,4},{4,5},{12,13},{13,14},{14,15},{15,16},{16,... | collective-permute-start | bytes 55304 | tf_op jit(solution)/shard_map/ppermute | solution.py:326
  38.9 9.0 %collective-permute-start.9 = (bf16[72,128]{1,0:T(8,128)(2,1)S(1)}, bf16[72,128]{1,0:T(8,128)(2,1)S(1)}, u32[]{:S(2)}, u32[]{:S(2)}) collective-permute-start(bf16[72,128]{1,0:T(8,128)(2,1)S(1)} %get-tuple-element.81), channel_id=1, source_target_pairs={{6,7},{7,8},{8,9},{9,10},{10,11},{18,19},{19,20},{20,21},{21,22},{... | collective-permute-start | bytes 55304 | tf_op jit(solution)/shard_map/ppermute | solution.py:326
  40.2 7.8 %collective-permute-start.10 = (bf16[72,128]{1,0:T(8,128)(2,1)S(1)}, bf16[72,128]{1,0:T(8,128)(2,1)S(1)}, u32[]{:S(2)}, u32[]{:S(2)}) collective-permute-start(bf16[72,128]{1,0:T(8,128)(2,1)S(1)} %get-tuple-element.82), channel_id=1, source_target_pairs={{5,6},{11,12},{17,18},{23,24},{29,30},{35,36},{41,42},{6,5},{12,11... | collective-permute-start | bytes 55304 | tf_op jit(solution)/shard_map/ppermute | solution.py:326
  45.2 2.7 %collective-permute-start.11 = (bf16[72,128]{1,0:T(8,128)(2,1)S(1)}, bf16[72,128]{1,0:T(8,128)(2,1)S(1)}, u32[]{:S(2)}, u32[]{:S(2)}) collective-permute-start(bf16[72,128]{1,0:T(8,128)(2,1)S(1)} %get-tuple-element.83), channel_id=1, source_target_pairs={{0,1},{1,2},{2,3},{3,4},{4,5},{12,13},{13,14},{14,15},{15,16},{16,... | collective-permute-start | bytes 55304 | tf_op jit(solution)/shard_map/ppermute | solution.py:326
  48.0 25.5 %copy-start.1 = (bf16[1152,1152]{1,0:T(8,128)(2,1)S(1)}, bf16[1152,1152]{1,0:T(8,128)(2,1)}, u32[]{:S(2)}) copy-start(bf16[1152,1152]{1,0:T(8,128)(2,1)} %one_ref.17) | copy-start | bytes 7962628
  48.0 25.5 %copy-start.2 = (bf16[1152,1152]{1,0:T(8,128)(2,1)S(1)}, bf16[1152,1152]{1,0:T(8,128)(2,1)}, u32[]{:S(2)}) copy-start(bf16[1152,1152]{1,0:T(8,128)(2,1)} %two_ref.1) | copy-start | bytes 7962628

commit v8 on v6

--- a/solution.py
+++ b/solution.py
@@ -1,3 +1,5 @@
+import functools
+
 import jax
 import jax.numpy as jnp
 from jax import lax
@@ -53,20 +55,24 @@
     return jnp.maximum(moved, KEEP * value)
 
 
-def up_of(edge):
+def up_of(edge, opening):
     place = edge % CHAIN
+    if opening:
+        return 1 * (place == CHAIN - 1) + 1 * (place == CHAIN - 3) + 2 * (place % 2) * (place < CHAIN - 3)
     return 2 * (place < 5) + 1 * (place == 5) + 1 * (place == CHAIN - 1)
 
 
-def down_of(edge):
+def down_of(edge, opening):
     place = edge % CHAIN
+    if opening:
+        return 1 * (place == CHAIN - 1) + 2 * (place == CHAIN - 2) + 2 * (place % 2) * (place < CHAIN - 2)
     return 1 * (place == 5) + 1 * (place == CHAIN - 1) + 2 * (place > 5) * (place < CHAIN - 1)
 
 
-def pairs_of(exchange, dom):
+def pairs_of(exchange, dom, opening):
     edges = range(dom - 1)
-    return [(d, d + 1) for d in edges if up_of(d) == exchange] + [
-        (d + 1, d) for d in edges if down_of(d) == exchange
+    return [(d, d + 1) for d in edges if up_of(d, opening) == exchange] + [
+        (d + 1, d) for d in edges if down_of(d, opening) == exchange
     ]
 
 
@@ -77,14 +83,14 @@
     return picked
 
 
-def halos(received):
+def halos(received, opening):
     parts = [r[...] for r in received]
     own = lax.axis_index("dom")
-    return pick(up_of(own + CHAIN - 1), parts), pick(down_of(own), parts)
-
-
-def send(outs, first, last):
-    to_left = down_of(lax.axis_index("dom") + CHAIN - 1)
+    return pick(up_of(own + CHAIN - 1, opening), parts), pick(down_of(own, opening), parts)
+
+
+def send(outs, first, last, opening):
+    to_left = down_of(lax.axis_index("dom") + CHAIN - 1, opening)
     for exchange, out in enumerate(outs):
         out[...] = jnp.where(to_left == exchange, first, last)
 
@@ -112,22 +118,22 @@
     ]
 
 
-def edge_kernel(cols, in0, in1, in2, blocks_ref, ends_ref, one_ref, two_ref, c1_ref, c2_ref, *outs):
+def edge_kernel(opening, cols, in0, in1, in2, blocks_ref, ends_ref, one_ref, two_ref, c1_ref, c2_ref, *outs):
     out0, out1, out2, ends16, ends32 = outs
-    left, right = halos((in0, in1, in2))
+    left, right = halos((in0, in1, in2), opening)
     first, last = edge_rows(
         cols, left, right, blocks_ref, ends_ref[0], ends_ref[1], one_ref, two_ref, c1_ref[...], c2_ref[...]
     )
     ends32[0], ends32[1] = first, last
     first, last = first.astype(jnp.bfloat16), last.astype(jnp.bfloat16)
     ends16[0], ends16[1] = first, last
-    send((out0, out1, out2), first, last)
-
-
-def inner_kernel(cols, in0, in1, in2, blocks_ref, field_ref, ends16, one_ref, two_ref, c1_ref, c2_ref, *outs):
+    send((out0, out1, out2), first, last, False)
+
+
+def inner_kernel(opening, cols, in0, in1, in2, blocks_ref, field_ref, ends16, one_ref, two_ref, c1_ref, c2_ref, *outs):
     out16, out32 = outs
     n, rows, width = blocks_ref.shape
-    left, right = halos((in0, in1, in2))
+    left, right = halos((in0, in1, in2), opening)
     c1, c2 = c1_ref[...], c2_ref[...]
     out16[0] = ends16[0]
     out16[n - 1] = ends16[1]
@@ -165,7 +171,7 @@
 
 def last_edge_kernel(cols, todo, in0, in1, in2, blocks_ref, field_ref, ends_ref, one_ref, two_ref, c1_ref, c2_ref, inner_ref, out16):
     n, rows, width = blocks_ref.shape
-    left, right = halos((in0, in1, in2))
+    left, right = halos((in0, in1, in2), False)
     c1, c2 = c1_ref[...], c2_ref[...]
 
     def again(b):
@@ -209,7 +215,7 @@
         copy.start()
     for copy in copies:
         copy.wait()
-    send((out0, out1, out2), buffers[0].astype(jnp.bfloat16), buffers[1].astype(jnp.bfloat16))
+    send((out0, out1, out2), buffers[0].astype(jnp.bfloat16), buffers[1].astype(jnp.bfloat16), True)
 
 
 def load_kernel(action_ref, coef_one_hbm, coef_two_hbm, two_hbm, cols_hbm, *refs):
@@ -297,8 +303,8 @@
     block, blocks, ends, weights = (rows, width), (n, rows, width), (2, rows, width), (n, nnz, width, width)
     vm = lambda shape, dtype: (pltpu.VMEM, shape, dtype)
     sm = lambda shape: (pltpu.SMEM, shape, jnp.int32)
-    exchange = lambda parts: [
-        in_vmem(lax.ppermute(x, "dom", pairs_of(i, dom))) for i, x in enumerate(parts)
+    exchange = lambda parts, opening: [
+        in_vmem(lax.ppermute(x, "dom", pairs_of(i, dom, opening))) for i, x in enumerate(parts)
     ]
 
     received = exchange(
@@ -308,7 +314,8 @@
             [hbm()],
             "begin",
             [pltpu.VMEM((2, rows, width), f32), pltpu.SemaphoreType.DMA((2,))],
-        )(in_hbm(action))
+        )(in_hbm(action)),
+        True,
     )
     cols, todo, value16, value32, ends32, two, c1, c2 = call(
         load_kernel,
@@ -327,14 +334,14 @@
     one = in_vmem(transport_one)
     for substep in range(SUBSTEPS - 1):
         *parts, ends16, ends32 = call(
-            edge_kernel,
+            functools.partial(edge_kernel, substep == 0),
             [vm(block, bf16)] * 3 + [vm(ends, bf16), vm(ends, f32)],
             [smem()] + [vmem()] * 9,
             "edges",
         )(cols, *received, value16, ends32, one, two, c1, c2)
-        new_received = exchange(parts)
+        new_received = exchange(parts, False)
         value16, value32 = call(
-            inner_kernel, [vm(blocks, bf16), vm(blocks, f32)], [smem()] + [vmem()] * 10, "inner"
+            functools.partial(inner_kernel, substep == 0), [vm(blocks, bf16), vm(blocks, f32)], [smem()] + [vmem()] * 10, "inner"
         )(cols, *received, value16, value32, ends16, one, two, c1, c2)
         received = new_received
     (final,) = call(last_inner_kernel, [vm(blocks, bf16)], [smem()] + [vmem()] * 6, "last_inner")(

time: 75.5 us -> 75.4 us (level)
  the two profiles are of different devices: /device:TPU:8 before, /device:TPU:264 now
where the time goes in v8:
time: 75.4 us; the launch traced here: 75 us
  starting transfers between devices  37.7 us (50%)
  blocking collectives  24.3 us (32%)
  Pallas kernels  8.31 us (11%)
  waiting for transfers between devices  4.46 us (6%)
    ppermute x12, starting transfers between devices, per_device(): lax.ppermute(x, 'dom', pairs_of(i, dom, opening))  37.7 us
    all_to_all x1, blocking collectives, per_device(): lax.all_to_all(final, 'comp', split_axis=0, concat_axis=0, tiled=True)  24.3 us
    ppermute x12, waiting for transfers between devices, per_device(): lax.ppermute(x, 'dom', pairs_of(i, dom, opening))  4.46 us
    pallas_call x3, Pallas kernels, per_device(): call(functools.partial(inner_kernel, substep == 0), [vm(blocks, bf16), vm...  2.09 us
    pallas_call x1, Pallas kernels, per_device(): call(load_kernel, [sm((nnz, n)), sm((1, n)), vm(blocks, bf16), vm(blocks,...  1.95 us
    pallas_call x1, Pallas kernels, source_terms(): pl.pallas_call(source_kernel, out_shape=jax.ShapeDtypeStruct((1, cells, c...  1.68 us
  transfers between devices with their start and end apart: 12, of which 3 were waited for; matrix products, arithmetic and copies ran while one was open for 0% of the time, Pallas kernels for 6%

profile of v8, /device:TPU:264, one launch (start us, length us, event | category | flops | bytes accessed | tf_op | source)
XLA Modules:
  0.0 75.0 jit_solution(8227972754469324960)
XLA Ops:
  0.0 0.9 %begin.1 = (bf16[72,128]{1,0:T(8,128)(2,1)S(1)}, bf16[72,128]{1,0:T(8,128)(2,1)S(1)}, bf16[72,128]{1,0:T(8,128)(2,1)S(1)}) custom-call(f32[72,2048]{1,0:T(8,128)} %action_ref.3), custom_call_target="tpu_custom_call" | custom-call | tf_op jit(solution)/shard_map/begin/pallas_call | solution.py:311
  0.9 4.3 %collective-permute-start = (bf16[72,128]{1,0:T(8,128)(2,1)S(1)}, bf16[72,128]{1,0:T(8,128)(2,1)S(1)}, u32[]{:S(2)}, u32[]{:S(2)}) collective-permute-start(bf16[72,128]{1,0:T(8,128)(2,1)S(1)} %get-tuple-element.39), channel_id=1, source_target_pairs={{0,1},{2,3},{4,5},{6,7},{8,9},{10,11},{12,13},{14,15},{16,17},{18,... | collective-permute-start | bytes 55304 | tf_op jit(solution)/shard_map/ppermute | solution.py:307
  5.2 0.7 collective-permute-start.1
  5.9 1.9 %collective-permute-start.2 = (bf16[72,128]{1,0:T(8,128)(2,1)S(1)}, bf16[72,128]{1,0:T(8,128)(2,1)S(1)}, u32[]{:S(2)}, u32[]{:S(2)}) collective-permute-start(bf16[72,128]{1,0:T(8,128)(2,1)S(1)} %get-tuple-element.41), channel_id=1, source_target_pairs={{1,2},{3,4},{5,6},{7,8},{13,14},{15,16},{17,18},{19,20},{25,26},{2... | collective-permute-start | bytes 55304 | tf_op jit(solution)/shard_map/ppermute | solution.py:307
  7.8 1.9 %load.1 = (s32[3,16]{1,0:T(4,128)S(4)}, s32[1,16]{1,0:T(1,128)S(4)}, bf16[16,72,128]{2,1,0:T(8,128)(2,1)S(1)}, f32[16,72,128]{2,1,0:T(8,128)S(1)}, f32[2,72,128]...) custom-call(f32[72,2048]{1,0:T(8,128)} %action_ref.3, ...), custom_call_target="tpu_custom_call" | custom-call | tf_op jit(solution)/shard_map/load/pallas_call | solution.py:320
  9.8 3.0 %collective-permute-done.2.in2 = bf16[72,128]{1,0:T(8,128)(2,1)S(1)} collective-permute-done((bf16[72,128]{1,0:T(8,128)(2,1)S(1)}, bf16[72,128]{1,0:T(8,128)(2,1)S(1)}, u32[]{:S(2)}, u32[]{:S(2)}) %collective-permute-start.2) | collective-permute-done | bytes 18464 | tf_op jit(solution)/shard_map/ppermute | solution.py:307
  13.0 2.2 %collective-permute-start.3 = (bf16[72,128]{1,0:T(8,128)(2,1)S(1)}, bf16[72,128]{1,0:T(8,128)(2,1)S(1)}, u32[]{:S(2)}, u32[]{:S(2)}) collective-permute-start(bf16[72,128]{1,0:T(8,128)(2,1)S(1)} %get-tuple-element.47), channel_id=1, source_target_pairs={{6,7},{7,8},{8,9},{9,10},{10,11},{18,19},{19,20},{20,21},{21,22},{... | collective-permute-start | bytes 55304 | tf_op jit(solution)/shard_map/ppermute | solution.py:307
  15.2 0.7 collective-permute-start.4
  15.9 7.3 %collective-permute-start.5 = (bf16[72,128]{1,0:T(8,128)(2,1)S(1)}, bf16[72,128]{1,0:T(8,128)(2,1)S(1)}, u32[]{:S(2)}, u32[]{:S(2)}) collective-permute-start(bf16[72,128]{1,0:T(8,128)(2,1)S(1)} %get-tuple-element.49), channel_id=1, source_target_pairs={{0,1},{1,2},{2,3},{3,4},{4,5},{12,13},{13,14},{14,15},{15,16},{16,... | collective-permute-start | bytes 55304 | tf_op jit(solution)/shard_map/ppermute | solution.py:307
  23.2 0.7 inner.3
  23.9 0.7 collective-permute-done.5.in2
  24.9 1.9 %collective-permute-start.6 = (bf16[72,128]{1,0:T(8,128)(2,1)S(1)}, bf16[72,128]{1,0:T(8,128)(2,1)S(1)}, u32[]{:S(2)}, u32[]{:S(2)}) collective-permute-start(bf16[72,128]{1,0:T(8,128)(2,1)S(1)} %get-tuple-element.54), channel_id=1, source_target_pairs={{6,7},{7,8},{8,9},{9,10},{10,11},{18,19},{19,20},{20,21},{21,22},{... | collective-permute-start | bytes 55304 | tf_op jit(solution)/shard_map/ppermute | solution.py:307
  26.8 0.7 collective-permute-start.7
  27.5 8.3 %collective-permute-start.8 = (bf16[72,128]{1,0:T(8,128)(2,1)S(1)}, bf16[72,128]{1,0:T(8,128)(2,1)S(1)}, u32[]{:S(2)}, u32[]{:S(2)}) collective-permute-start(bf16[72,128]{1,0:T(8,128)(2,1)S(1)} %get-tuple-element.56), channel_id=1, source_target_pairs={{0,1},{1,2},{2,3},{3,4},{4,5},{12,13},{13,14},{14,15},{15,16},{16,... | collective-permute-start | bytes 55304 | tf_op jit(solution)/shard_map/ppermute | solution.py:307
  35.8 0.7 inner.4
  36.5 0.7 collective-permute-done.8.in2
  37.5 1.9 %collective-permute-start.9 = (bf16[72,128]{1,0:T(8,128)(2,1)S(1)}, bf16[72,128]{1,0:T(8,128)(2,1)S(1)}, u32[]{:S(2)}, u32[]{:S(2)}) collective-permute-start(bf16[72,128]{1,0:T(8,128)(2,1)S(1)} %get-tuple-element.61), channel_id=1, source_target_pairs={{6,7},{7,8},{8,9},{9,10},{10,11},{18,19},{19,20},{20,21},{21,22},{... | collective-permute-start | bytes 55304 | tf_op jit(solution)/shard_map/ppermute | solution.py:307
  39.4 0.7 collective-permute-start.10
  40.1 7.2 %collective-permute-start.11 = (bf16[72,128]{1,0:T(8,128)(2,1)S(1)}, bf16[72,128]{1,0:T(8,128)(2,1)S(1)}, u32[]{:S(2)}, u32[]{:S(2)}) collective-permute-start(bf16[72,128]{1,0:T(8,128)(2,1)S(1)} %get-tuple-element.63), channel_id=1, source_target_pairs={{0,1},{1,2},{2,3},{3,4},{4,5},{12,13},{13,14},{14,15},{15,16},{16,... | collective-permute-start | bytes 55304 | tf_op jit(solution)/shard_map/ppermute | solution.py:307
  47.3 0.7 inner.5
  48.0 0.7 last_inner.1.inner_ref
  48.7 0.3 last_edge.1
  49.0 24.3 %all_to_all.5 = bf16[16,72,128]{2,1,0:T(8,128)(2,1)S(1)} all-to-all(bf16[16,72,128]{2,1,0:T(8,128)(2,1)S(1)} %last_edge.1), channel_id=1, replica_groups=mesh['comp'=16,'dom'=48] {'comp'}, dimensions={0} | all-to-all | bytes 589824 | tf_op jit(solution)/shard_map/all_to_all | solution.py:353
  73.3 1.7 %source_terms.1 = f32[1,128,1152]{2,1,0:T(8,128)} custom-call(bf16[1152,128]{1,0:T(8,128)(2,1)S(1)} %bitcast.4, bf16[1152,1152]{1,0:T(8,128)(2,1)S(1)} %copy-done.1, bf16[1152,1152]{1,0:T(8,128)(2,1)S(1)} %copy-done.2), custom_call_target="tpu_custom_call" | custom-call | tf_op jit(solution)/shard_map/source_terms/pallas_call | solution.py:282
  (18 shorter events, 0.7 us)
Async XLA Ops:
  0.0 12.8 %copy-start = (bf16[16,3,128,128]{3,2,1,0:T(8,128)(2,1)S(1)}, bf16[16,3,128,128]{3,2,1,0:T(8,128)(2,1)}, u32[]{:S(2)}) copy-start(bf16[16,3,128,128]{3,2,1,0:T(8,128)(2,1)} %one_ref.16) | copy-start | bytes 4718596
  0.9 8.8 %collective-permute-start = (bf16[72,128]{1,0:T(8,128)(2,1)S(1)}, bf16[72,128]{1,0:T(8,128)(2,1)S(1)}, u32[]{:S(2)}, u32[]{:S(2)}) collective-permute-start(bf16[72,128]{1,0:T(8,128)(2,1)S(1)} %get-tuple-element.39), channel_id=1, source_target_pairs={{0,1},{2,3},{4,5},{6,7},{8,9},{10,11},{12,13},{14,15},{16,17},{18,... | collective-permute-start | bytes 55304 | tf_op jit(solution)/shard_map/ppermute | solution.py:307
  5.2 4.6 %collective-permute-start.1 = (bf16[72,128]{1,0:T(8,128)(2,1)S(1)}, bf16[72,128]{1,0:T(8,128)(2,1)S(1)}, u32[]{:S(2)}, u32[]{:S(2)}) collective-permute-start(bf16[72,128]{1,0:T(8,128)(2,1)S(1)} %get-tuple-element.40), channel_id=1, source_target_pairs={{9,10},{11,12},{21,22},{23,24},{33,34},{35,36},{45,46},{12,11},{24... | collective-permute-start | bytes 55304 | tf_op jit(solution)/shard_map/ppermute | solution.py:307
  5.9 6.9 %collective-permute-start.2 = (bf16[72,128]{1,0:T(8,128)(2,1)S(1)}, bf16[72,128]{1,0:T(8,128)(2,1)S(1)}, u32[]{:S(2)}, u32[]{:S(2)}) collective-permute-start(bf16[72,128]{1,0:T(8,128)(2,1)S(1)} %get-tuple-element.41), channel_id=1, source_target_pairs={{1,2},{3,4},{5,6},{7,8},{13,14},{15,16},{17,18},{19,20},{25,26},{2... | collective-permute-start | bytes 55304 | tf_op jit(solution)/shard_map/ppermute | solution.py:307
  13.0 10.9 %collective-permute-start.3 = (bf16[72,128]{1,0:T(8,128)(2,1)S(1)}, bf16[72,128]{1,0:T(8,128)(2,1)S(1)}, u32[]{:S(2)}, u32[]{:S(2)}) collective-permute-start(bf16[72,128]{1,0:T(8,128)(2,1)S(1)} %get-tuple-element.47), channel_id=1, source_target_pairs={{6,7},{7,8},{8,9},{9,10},{10,11},{18,19},{19,20},{20,21},{21,22},{... | collective-permute-start | bytes 55304 | tf_op jit(solution)/shard_map/ppermute | solution.py:307
  15.2 8.7 %collective-permute-start.4 = (bf16[72,128]{1,0:T(8,128)(2,1)S(1)}, bf16[72,128]{1,0:T(8,128)(2,1)S(1)}, u32[]{:S(2)}, u32[]{:S(2)}) collective-permute-start(bf16[72,128]{1,0:T(8,128)(2,1)S(1)} %get-tuple-element.48), channel_id=1, source_target_pairs={{5,6},{11,12},{17,18},{23,24},{29,30},{35,36},{41,42},{6,5},{12,11... | collective-permute-start | bytes 55304 | tf_op jit(solution)/shard_map/ppermute | solution.py:307
  15.9 8.8 %collective-permute-start.5 = (bf16[72,128]{1,0:T(8,128)(2,1)S(1)}, bf16[72,128]{1,0:T(8,128)(2,1)S(1)}, u32[]{:S(2)}, u32[]{:S(2)}) collective-permute-start(bf16[72,128]{1,0:T(8,128)(2,1)S(1)} %get-tuple-element.49), channel_id=1, source_target_pairs={{0,1},{1,2},{2,3},{3,4},{4,5},{12,13},{13,14},{14,15},{15,16},{16,... | collective-permute-start | bytes 55304 | tf_op jit(solution)/shard_map/ppermute | solution.py:307
  24.9 11.6 %collective-permute-start.6 = (bf16[72,128]{1,0:T(8,128)(2,1)S(1)}, bf16[72,128]{1,0:T(8,128)(2,1)S(1)}, u32[]{:S(2)}, u32[]{:S(2)}) collective-permute-start(bf16[72,128]{1,0:T(8,128)(2,1)S(1)} %get-tuple-element.54), channel_id=1, source_target_pairs={{6,7},{7,8},{8,9},{9,10},{10,11},{18,19},{19,20},{20,21},{21,22},{... | collective-permute-start | bytes 55304 | tf_op jit(solution)/shard_map/ppermute | solution.py:307
  26.8 9.7 %collective-permute-start.7 = (bf16[72,128]{1,0:T(8,128)(2,1)S(1)}, bf16[72,128]{1,0:T(8,128)(2,1)S(1)}, u32[]{:S(2)}, u32[]{:S(2)}) collective-permute-start(bf16[72,128]{1,0:T(8,128)(2,1)S(1)} %get-tuple-element.55), channel_id=1, source_target_pairs={{5,6},{11,12},{17,18},{23,24},{29,30},{35,36},{41,42},{6,5},{12,11... | collective-permute-start | bytes 55304 | tf_op jit(solution)/shard_map/ppermute | solution.py:307
  27.5 9.8 %collective-permute-start.8 = (bf16[72,128]{1,0:T(8,128)(2,1)S(1)}, bf16[72,128]{1,0:T(8,128)(2,1)S(1)}, u32[]{:S(2)}, u32[]{:S(2)}) collective-permute-start(bf16[72,128]{1,0:T(8,128)(2,1)S(1)} %get-tuple-element.56), channel_id=1, source_target_pairs={{0,1},{1,2},{2,3},{3,4},{4,5},{12,13},{13,14},{14,15},{15,16},{16,... | collective-permute-start | bytes 55304 | tf_op jit(solution)/shard_map/ppermute | solution.py:307
  37.5 11.2 %collective-permute-start.9 = (bf16[72,128]{1,0:T(8,128)(2,1)S(1)}, bf16[72,128]{1,0:T(8,128)(2,1)S(1)}, u32[]{:S(2)}, u32[]{:S(2)}) collective-permute-start(bf16[72,128]{1,0:T(8,128)(2,1)S(1)} %get-tuple-element.61), channel_id=1, source_target_pairs={{6,7},{7,8},{8,9},{9,10},{10,11},{18,19},{19,20},{20,21},{21,22},{... | collective-permute-start | bytes 55304 | tf_op jit(solution)/shard_map/ppermute | solution.py:307
  39.4 9.2 %collective-permute-start.10 = (bf16[72,128]{1,0:T(8,128)(2,1)S(1)}, bf16[72,128]{1,0:T(8,128)(2,1)S(1)}, u32[]{:S(2)}, u32[]{:S(2)}) collective-permute-start(bf16[72,128]{1,0:T(8,128)(2,1)S(1)} %get-tuple-element.62), channel_id=1, source_target_pairs={{5,6},{11,12},{17,18},{23,24},{29,30},{35,36},{41,42},{6,5},{12,11... | collective-permute-start | bytes 55304 | tf_op jit(solution)/shard_map/ppermute | solution.py:307
  40.1 8.6 %collective-permute-start.11 = (bf16[72,128]{1,0:T(8,128)(2,1)S(1)}, bf16[72,128]{1,0:T(8,128)(2,1)S(1)}, u32[]{:S(2)}, u32[]{:S(2)}) collective-permute-start(bf16[72,128]{1,0:T(8,128)(2,1)S(1)} %get-tuple-element.63), channel_id=1, source_target_pairs={{0,1},{1,2},{2,3},{3,4},{4,5},{12,13},{13,14},{14,15},{15,16},{16,... | collective-permute-start | bytes 55304 | tf_op jit(solution)/shard_map/ppermute | solution.py:307
  48.7 24.6 %copy-start.1 = (bf16[1152,1152]{1,0:T(8,128)(2,1)S(1)}, bf16[1152,1152]{1,0:T(8,128)(2,1)}, u32[]{:S(2)}) copy-start(bf16[1152,1152]{1,0:T(8,128)(2,1)} %one_ref.17) | copy-start | bytes 7962628
  48.7 24.6 %copy-start.2 = (bf16[1152,1152]{1,0:T(8,128)(2,1)S(1)}, bf16[1152,1152]{1,0:T(8,128)(2,1)}, u32[]{:S(2)}) copy-start(bf16[1152,1152]{1,0:T(8,128)(2,1)} %two_ref.1) | copy-start | bytes 7962628

commit v9 on v8

--- a/solution.py
+++ b/solution.py
@@ -10,6 +10,7 @@
 SUBSTEPS = 4
 KEEP = 0.25
 CHAIN = 12
+TURN = 7
 ROUND = 3
 
 
@@ -59,14 +60,14 @@
     place = edge % CHAIN
     if opening:
         return 1 * (place == CHAIN - 1) + 1 * (place == CHAIN - 3) + 2 * (place % 2) * (place < CHAIN - 3)
-    return 2 * (place < 5) + 1 * (place == 5) + 1 * (place == CHAIN - 1)
+    return 2 * (place < TURN) + 1 * (place == TURN) + 1 * (place == CHAIN - 1)
 
 
 def down_of(edge, opening):
     place = edge % CHAIN
     if opening:
         return 1 * (place == CHAIN - 1) + 2 * (place == CHAIN - 2) + 2 * (place % 2) * (place < CHAIN - 2)
-    return 1 * (place == 5) + 1 * (place == CHAIN - 1) + 2 * (place > 5) * (place < CHAIN - 1)
+    return 1 * (place == TURN) + 1 * (place == CHAIN - 1) + 2 * (place > TURN) * (place < CHAIN - 1)
 
 
 def pairs_of(exchange, dom, opening):

time: 75.4 us -> 75.2 us (level)
  the two profiles are of different devices: /device:TPU:264 before, /device:TPU:8 now
where the time goes in v9:
time: 75.2 us; the launch traced here: 74.8 us
  starting transfers between devices  39.4 us (52%)
  blocking collectives  25.2 us (34%)
  Pallas kernels  8.53 us (11%)
  waiting for transfers between devices  1.51 us (2%)
    ppermute x12, starting transfers between devices, per_device(): lax.ppermute(x, 'dom', pairs_of(i, dom, opening))  39.4 us
    all_to_all x1, blocking collectives, per_device(): lax.all_to_all(final, 'comp', split_axis=0, concat_axis=0, tiled=True)  25.2 us
    pallas_call x3, Pallas kernels, per_device(): call(functools.partial(inner_kernel, substep == 0), [vm(blocks, bf16), vm...  2.12 us
    pallas_call x1, Pallas kernels, per_device(): call(load_kernel, [sm((nnz, n)), sm((1, n)), vm(blocks, bf16), vm(blocks,...  1.95 us
    pallas_call x1, Pallas kernels, source_terms(): pl.pallas_call(source_kernel, out_shape=jax.ShapeDtypeStruct((1, cells, c...  1.68 us
    ppermute x12, waiting for transfers between devices, per_device(): lax.ppermute(x, 'dom', pairs_of(i, dom, opening))  1.51 us
  transfers between devices with their start and end apart: 12, of which 3 were waited for; matrix products, arithmetic and copies ran while one was open for 0% of the time, Pallas kernels for 6%

profile of v9, /device:TPU:8, one launch (start us, length us, event | category | flops | bytes accessed | tf_op | source)
XLA Modules:
  0.0 74.8 jit_solution(12164485058963939171)
XLA Ops:
  0.0 0.9 %begin.1 = (bf16[72,128]{1,0:T(8,128)(2,1)S(1)}, bf16[72,128]{1,0:T(8,128)(2,1)S(1)}, bf16[72,128]{1,0:T(8,128)(2,1)S(1)}) custom-call(f32[72,2048]{1,0:T(8,128)} %action_ref.3), custom_call_target="tpu_custom_call" | custom-call | tf_op jit(solution)/shard_map/begin/pallas_call | solution.py:312
  0.9 4.3 %collective-permute-start = (bf16[72,128]{1,0:T(8,128)(2,1)S(1)}, bf16[72,128]{1,0:T(8,128)(2,1)S(1)}, u32[]{:S(2)}, u32[]{:S(2)}) collective-permute-start(bf16[72,128]{1,0:T(8,128)(2,1)S(1)} %get-tuple-element.39), channel_id=1, source_target_pairs={{0,1},{2,3},{4,5},{6,7},{8,9},{10,11},{12,13},{14,15},{16,17},{18,... | collective-permute-start | bytes 55304 | tf_op jit(solution)/shard_map/ppermute | solution.py:308
  5.2 11.5 %collective-permute-start.1 = (bf16[72,128]{1,0:T(8,128)(2,1)S(1)}, bf16[72,128]{1,0:T(8,128)(2,1)S(1)}, u32[]{:S(2)}, u32[]{:S(2)}) collective-permute-start(bf16[72,128]{1,0:T(8,128)(2,1)S(1)} %get-tuple-element.40), channel_id=1, source_target_pairs={{9,10},{11,12},{21,22},{23,24},{33,34},{35,36},{45,46},{12,11},{24... | collective-permute-start | bytes 55304 | tf_op jit(solution)/shard_map/ppermute | solution.py:308
  16.7 0.7 collective-permute-start.2
  17.4 1.9 %load.1 = (s32[3,16]{1,0:T(4,128)S(4)}, s32[1,16]{1,0:T(1,128)S(4)}, bf16[16,72,128]{2,1,0:T(8,128)(2,1)S(1)}, f32[16,72,128]{2,1,0:T(8,128)S(1)}, f32[2,72,128]...) custom-call(f32[72,2048]{1,0:T(8,128)} %action_ref.3, ...), custom_call_target="tpu_custom_call" | custom-call | tf_op jit(solution)/shard_map/load/pallas_call | solution.py:321
  19.4 0.2 edges.3
  19.6 1.3 %collective-permute-start.3 = (bf16[72,128]{1,0:T(8,128)(2,1)S(1)}, bf16[72,128]{1,0:T(8,128)(2,1)S(1)}, u32[]{:S(2)}, u32[]{:S(2)}) collective-permute-start(bf16[72,128]{1,0:T(8,128)(2,1)S(1)} %get-tuple-element.47), channel_id=1, source_target_pairs={{8,9},{9,10},{10,11},{20,21},{21,22},{22,23},{32,33},{33,34},{34,3... | collective-permute-start | bytes 55304 | tf_op jit(solution)/shard_map/ppermute | solution.py:308
  20.9 5.2 %collective-permute-start.4 = (bf16[72,128]{1,0:T(8,128)(2,1)S(1)}, bf16[72,128]{1,0:T(8,128)(2,1)S(1)}, u32[]{:S(2)}, u32[]{:S(2)}) collective-permute-start(bf16[72,128]{1,0:T(8,128)(2,1)S(1)} %get-tuple-element.48), channel_id=1, source_target_pairs={{7,8},{11,12},{19,20},{23,24},{31,32},{35,36},{43,44},{8,7},{12,11... | collective-permute-start | bytes 55304 | tf_op jit(solution)/shard_map/ppermute | solution.py:308
  26.1 1.3 %collective-permute-start.5 = (bf16[72,128]{1,0:T(8,128)(2,1)S(1)}, bf16[72,128]{1,0:T(8,128)(2,1)S(1)}, u32[]{:S(2)}, u32[]{:S(2)}) collective-permute-start(bf16[72,128]{1,0:T(8,128)(2,1)S(1)} %get-tuple-element.49), channel_id=1, source_target_pairs={{0,1},{1,2},{2,3},{3,4},{4,5},{5,6},{6,7},{12,13},{13,14},{14,15},... | collective-permute-start | bytes 55304 | tf_op jit(solution)/shard_map/ppermute | solution.py:308
  27.4 0.7 inner.3
  28.1 0.6 collective-permute-done.4.in1
  29.1 1.3 %collective-permute-start.6 = (bf16[72,128]{1,0:T(8,128)(2,1)S(1)}, bf16[72,128]{1,0:T(8,128)(2,1)S(1)}, u32[]{:S(2)}, u32[]{:S(2)}) collective-permute-start(bf16[72,128]{1,0:T(8,128)(2,1)S(1)} %get-tuple-element.54), channel_id=1, source_target_pairs={{8,9},{9,10},{10,11},{20,21},{21,22},{22,23},{32,33},{33,34},{34,3... | collective-permute-start | bytes 55304 | tf_op jit(solution)/shard_map/ppermute | solution.py:308
  30.4 5.0 %collective-permute-start.7 = (bf16[72,128]{1,0:T(8,128)(2,1)S(1)}, bf16[72,128]{1,0:T(8,128)(2,1)S(1)}, u32[]{:S(2)}, u32[]{:S(2)}) collective-permute-start(bf16[72,128]{1,0:T(8,128)(2,1)S(1)} %get-tuple-element.55), channel_id=1, source_target_pairs={{7,8},{11,12},{19,20},{23,24},{31,32},{35,36},{43,44},{8,7},{12,11... | collective-permute-start | bytes 55304 | tf_op jit(solution)/shard_map/ppermute | solution.py:308
  35.4 1.3 %collective-permute-start.8 = (bf16[72,128]{1,0:T(8,128)(2,1)S(1)}, bf16[72,128]{1,0:T(8,128)(2,1)S(1)}, u32[]{:S(2)}, u32[]{:S(2)}) collective-permute-start(bf16[72,128]{1,0:T(8,128)(2,1)S(1)} %get-tuple-element.56), channel_id=1, source_target_pairs={{0,1},{1,2},{2,3},{3,4},{4,5},{5,6},{6,7},{12,13},{13,14},{14,15},... | collective-permute-start | bytes 55304 | tf_op jit(solution)/shard_map/ppermute | solution.py:308
  36.7 0.7 inner.4
  37.4 0.7 collective-permute-done.7.in1
  38.4 1.3 %collective-permute-start.9 = (bf16[72,128]{1,0:T(8,128)(2,1)S(1)}, bf16[72,128]{1,0:T(8,128)(2,1)S(1)}, u32[]{:S(2)}, u32[]{:S(2)}) collective-permute-start(bf16[72,128]{1,0:T(8,128)(2,1)S(1)} %get-tuple-element.61), channel_id=1, source_target_pairs={{8,9},{9,10},{10,11},{20,21},{21,22},{22,23},{32,33},{33,34},{34,3... | collective-permute-start | bytes 55304 | tf_op jit(solution)/shard_map/ppermute | solution.py:308
  39.7 5.0 %collective-permute-start.10 = (bf16[72,128]{1,0:T(8,128)(2,1)S(1)}, bf16[72,128]{1,0:T(8,128)(2,1)S(1)}, u32[]{:S(2)}, u32[]{:S(2)}) collective-permute-start(bf16[72,128]{1,0:T(8,128)(2,1)S(1)} %get-tuple-element.62), channel_id=1, source_target_pairs={{7,8},{11,12},{19,20},{23,24},{31,32},{35,36},{43,44},{8,7},{12,11... | collective-permute-start | bytes 55304 | tf_op jit(solution)/shard_map/ppermute | solution.py:308
  44.7 1.3 %collective-permute-start.11 = (bf16[72,128]{1,0:T(8,128)(2,1)S(1)}, bf16[72,128]{1,0:T(8,128)(2,1)S(1)}, u32[]{:S(2)}, u32[]{:S(2)}) collective-permute-start(bf16[72,128]{1,0:T(8,128)(2,1)S(1)} %get-tuple-element.63), channel_id=1, source_target_pairs={{0,1},{1,2},{2,3},{3,4},{4,5},{5,6},{6,7},{12,13},{13,14},{14,15},... | collective-permute-start | bytes 55304 | tf_op jit(solution)/shard_map/ppermute | solution.py:308
  46.0 0.7 inner.5
  46.7 0.7 last_inner.1.inner_ref
  47.4 0.5 last_edge.1
  48.0 25.2 %all_to_all.5 = bf16[16,72,128]{2,1,0:T(8,128)(2,1)S(1)} all-to-all(bf16[16,72,128]{2,1,0:T(8,128)(2,1)S(1)} %last_edge.1), channel_id=1, replica_groups=mesh['comp'=16,'dom'=48] {'comp'}, dimensions={0} | all-to-all | bytes 589824 | tf_op jit(solution)/shard_map/all_to_all | solution.py:354
  73.1 1.7 %source_terms.1 = f32[1,128,1152]{2,1,0:T(8,128)} custom-call(bf16[1152,128]{1,0:T(8,128)(2,1)S(1)} %bitcast.4, bf16[1152,1152]{1,0:T(8,128)(2,1)S(1)} %copy-done.1, bf16[1152,1152]{1,0:T(8,128)(2,1)S(1)} %copy-done.2), custom_call_target="tpu_custom_call" | custom-call | tf_op jit(solution)/shard_map/source_terms/pallas_call | solution.py:283
  (18 shorter events, 0.7 us)
Async XLA Ops:
  0.0 19.4 %copy-start = (bf16[16,3,128,128]{3,2,1,0:T(8,128)(2,1)S(1)}, bf16[16,3,128,128]{3,2,1,0:T(8,128)(2,1)}, u32[]{:S(2)}) copy-start(bf16[16,3,128,128]{3,2,1,0:T(8,128)(2,1)} %one_ref.16) | copy-start | bytes 4718596
  0.9 18.4 %collective-permute-start = (bf16[72,128]{1,0:T(8,128)(2,1)S(1)}, bf16[72,128]{1,0:T(8,128)(2,1)S(1)}, u32[]{:S(2)}, u32[]{:S(2)}) collective-permute-start(bf16[72,128]{1,0:T(8,128)(2,1)S(1)} %get-tuple-element.39), channel_id=1, source_target_pairs={{0,1},{2,3},{4,5},{6,7},{8,9},{10,11},{12,13},{14,15},{16,17},{18,... | collective-permute-start | bytes 55304 | tf_op jit(solution)/shard_map/ppermute | solution.py:308
  5.2 14.1 %collective-permute-start.1 = (bf16[72,128]{1,0:T(8,128)(2,1)S(1)}, bf16[72,128]{1,0:T(8,128)(2,1)S(1)}, u32[]{:S(2)}, u32[]{:S(2)}) collective-permute-start(bf16[72,128]{1,0:T(8,128)(2,1)S(1)} %get-tuple-element.40), channel_id=1, source_target_pairs={{9,10},{11,12},{21,22},{23,24},{33,34},{35,36},{45,46},{12,11},{24... | collective-permute-start | bytes 55304 | tf_op jit(solution)/shard_map/ppermute | solution.py:308
  16.7 2.6 %collective-permute-start.2 = (bf16[72,128]{1,0:T(8,128)(2,1)S(1)}, bf16[72,128]{1,0:T(8,128)(2,1)S(1)}, u32[]{:S(2)}, u32[]{:S(2)}) collective-permute-start(bf16[72,128]{1,0:T(8,128)(2,1)S(1)} %get-tuple-element.41), channel_id=1, source_target_pairs={{1,2},{3,4},{5,6},{7,8},{13,14},{15,16},{17,18},{19,20},{25,26},{2... | collective-permute-start | bytes 55304 | tf_op jit(solution)/shard_map/ppermute | solution.py:308
  19.6 8.5 %collective-permute-start.3 = (bf16[72,128]{1,0:T(8,128)(2,1)S(1)}, bf16[72,128]{1,0:T(8,128)(2,1)S(1)}, u32[]{:S(2)}, u32[]{:S(2)}) collective-permute-start(bf16[72,128]{1,0:T(8,128)(2,1)S(1)} %get-tuple-element.47), channel_id=1, source_target_pairs={{8,9},{9,10},{10,11},{20,21},{21,22},{22,23},{32,33},{33,34},{34,3... | collective-permute-start | bytes 55304 | tf_op jit(solution)/shard_map/ppermute | solution.py:308
  20.9 7.8 %collective-permute-start.4 = (bf16[72,128]{1,0:T(8,128)(2,1)S(1)}, bf16[72,128]{1,0:T(8,128)(2,1)S(1)}, u32[]{:S(2)}, u32[]{:S(2)}) collective-permute-start(bf16[72,128]{1,0:T(8,128)(2,1)S(1)} %get-tuple-element.48), channel_id=1, source_target_pairs={{7,8},{11,12},{19,20},{23,24},{31,32},{35,36},{43,44},{8,7},{12,11... | collective-permute-start | bytes 55304 | tf_op jit(solution)/shard_map/ppermute | solution.py:308
  26.1 2.7 %collective-permute-start.5 = (bf16[72,128]{1,0:T(8,128)(2,1)S(1)}, bf16[72,128]{1,0:T(8,128)(2,1)S(1)}, u32[]{:S(2)}, u32[]{:S(2)}) collective-permute-start(bf16[72,128]{1,0:T(8,128)(2,1)S(1)} %get-tuple-element.49), channel_id=1, source_target_pairs={{0,1},{1,2},{2,3},{3,4},{4,5},{5,6},{6,7},{12,13},{13,14},{14,15},... | collective-permute-start | bytes 55304 | tf_op jit(solution)/shard_map/ppermute | solution.py:308
  29.1 8.3 %collective-permute-start.6 = (bf16[72,128]{1,0:T(8,128)(2,1)S(1)}, bf16[72,128]{1,0:T(8,128)(2,1)S(1)}, u32[]{:S(2)}, u32[]{:S(2)}) collective-permute-start(bf16[72,128]{1,0:T(8,128)(2,1)S(1)} %get-tuple-element.54), channel_id=1, source_target_pairs={{8,9},{9,10},{10,11},{20,21},{21,22},{22,23},{32,33},{33,34},{34,3... | collective-permute-start | bytes 55304 | tf_op jit(solution)/shard_map/ppermute | solution.py:308
  30.4 7.8 %collective-permute-start.7 = (bf16[72,128]{1,0:T(8,128)(2,1)S(1)}, bf16[72,128]{1,0:T(8,128)(2,1)S(1)}, u32[]{:S(2)}, u32[]{:S(2)}) collective-permute-start(bf16[72,128]{1,0:T(8,128)(2,1)S(1)} %get-tuple-element.55), channel_id=1, source_target_pairs={{7,8},{11,12},{19,20},{23,24},{31,32},{35,36},{43,44},{8,7},{12,11... | collective-permute-start | bytes 55304 | tf_op jit(solution)/shard_map/ppermute | solution.py:308
  35.4 2.7 %collective-permute-start.8 = (bf16[72,128]{1,0:T(8,128)(2,1)S(1)}, bf16[72,128]{1,0:T(8,128)(2,1)S(1)}, u32[]{:S(2)}, u32[]{:S(2)}) collective-permute-start(bf16[72,128]{1,0:T(8,128)(2,1)S(1)} %get-tuple-element.56), channel_id=1, source_target_pairs={{0,1},{1,2},{2,3},{3,4},{4,5},{5,6},{6,7},{12,13},{13,14},{14,15},... | collective-permute-start | bytes 55304 | tf_op jit(solution)/shard_map/ppermute | solution.py:308
  38.4 9.0 %collective-permute-start.9 = (bf16[72,128]{1,0:T(8,128)(2,1)S(1)}, bf16[72,128]{1,0:T(8,128)(2,1)S(1)}, u32[]{:S(2)}, u32[]{:S(2)}) collective-permute-start(bf16[72,128]{1,0:T(8,128)(2,1)S(1)} %get-tuple-element.61), channel_id=1, source_target_pairs={{8,9},{9,10},{10,11},{20,21},{21,22},{22,23},{32,33},{33,34},{34,3... | collective-permute-start | bytes 55304 | tf_op jit(solution)/shard_map/ppermute | solution.py:308
  39.7 7.8 %collective-permute-start.10 = (bf16[72,128]{1,0:T(8,128)(2,1)S(1)}, bf16[72,128]{1,0:T(8,128)(2,1)S(1)}, u32[]{:S(2)}, u32[]{:S(2)}) collective-permute-start(bf16[72,128]{1,0:T(8,128)(2,1)S(1)} %get-tuple-element.62), channel_id=1, source_target_pairs={{7,8},{11,12},{19,20},{23,24},{31,32},{35,36},{43,44},{8,7},{12,11... | collective-permute-start | bytes 55304 | tf_op jit(solution)/shard_map/ppermute | solution.py:308
  44.7 2.7 %collective-permute-start.11 = (bf16[72,128]{1,0:T(8,128)(2,1)S(1)}, bf16[72,128]{1,0:T(8,128)(2,1)S(1)}, u32[]{:S(2)}, u32[]{:S(2)}) collective-permute-start(bf16[72,128]{1,0:T(8,128)(2,1)S(1)} %get-tuple-element.63), channel_id=1, source_target_pairs={{0,1},{1,2},{2,3},{3,4},{4,5},{5,6},{6,7},{12,13},{13,14},{14,15},... | collective-permute-start | bytes 55304 | tf_op jit(solution)/shard_map/ppermute | solution.py:308
  47.4 25.7 %copy-start.1 = (bf16[1152,1152]{1,0:T(8,128)(2,1)S(1)}, bf16[1152,1152]{1,0:T(8,128)(2,1)}, u32[]{:S(2)}) copy-start(bf16[1152,1152]{1,0:T(8,128)(2,1)} %one_ref.17) | copy-start | bytes 7962628
  47.4 25.7 %copy-start.2 = (bf16[1152,1152]{1,0:T(8,128)(2,1)S(1)}, bf16[1152,1152]{1,0:T(8,128)(2,1)}, u32[]{:S(2)}) copy-start(bf16[1152,1152]{1,0:T(8,128)(2,1)} %two_ref.1) | copy-start | bytes 7962628
